TPU v7x, 256 devices: a whole 4x4x8 slice. The times are simulated.
256 devices in a mesh: freq: 64 (over y, z, core), sky: 4 (over x).
Axes of the slice: x: 4, y: 4, z: 8, core: 2. Of those that a mesh axis runs over, the one named last changes fastest.
Arguments:
- sky_maps: bfloat16 [1024, 96, 4096], P('freq', 'sky'), may hold values from -240 to 240
- beam_index: int32 [1024], P('freq'), may hold values from 0 to 7
- beam_taps: float32 [8, 31], replicated, may hold values from 0.05 to 1
- start_seed: int32 [1024, 16], replicated, may hold values from -64 to 64
Outputs:
- cleaned: bfloat16 [1024, 256, 1536], P(None, ('freq', 'sky'))
All inputs are finite; a program needn't handle non-finite values.
Results may differ from a plain program's by a relative error of at most 0.0079.
The roundings to bfloat16 on the way count: a program that leaves them out, or rounds other values in their place, can miss the bound.
Values may be sent and summed in bfloat16 or wider, within the bound.
No kernel may reach another device: no remote copies, remote signals or barrier semaphores. Data moves between devices by JAX's collectives and lax.ppermute only.
A program may use at most 64 MiB of HBM per device.

v0:
```python
import jax
import jax.numpy as jnp
from jax import lax
from jax.sharding import PartitionSpec as P

ITERS = 8


def with_halo(x, sides, width):
    for axis, dim in sides:
        size, length = (lax.axis_size(axis), x.shape[dim])
        up = [(i, (i + 1) % size) for i in range(size - 1)]
        down = [(j, i) for i, j in up]
        last = lax.slice_in_dim(x, length - width, length, axis=dim)
        leading = lax.slice_in_dim(x, 0, width, axis=dim)
        before = lax.ppermute(last, axis, up)
        after = lax.ppermute(leading, axis, down)
        x = jnp.concatenate([before, x, after], axis=dim)
    return x


def column_pass(padded, kernels, strip_rows, half_taps, tap_count):
    row_pass = jnp.zeros((padded.shape[0], strip_rows, padded.shape[2]), jnp.float32)
    for offset in range(tap_count):
        row_pass = row_pass + kernels[:, offset, None, None] * padded[
            :, offset : offset + strip_rows, :
        ].astype(jnp.float32)
    columns = padded.shape[2]
    widened = jnp.pad(row_pass, ((0, 0), (0, 0), (half_taps, half_taps)))
    col_pass = jnp.zeros(row_pass.shape, jnp.float32)
    for offset in range(tap_count):
        col_pass = (
            col_pass + kernels[:, offset, None, None] * widened[:, :, offset : offset + columns]
        )
    return col_pass.astype(jnp.bfloat16)


def orthonormal(images):
    gram_matrix = jnp.dot(images.T, images, precision=lax.Precision.HIGHEST)
    factor = jnp.linalg.cholesky(gram_matrix)
    return lax.linalg.triangular_solve(
        factor, images, left_side=False, lower=True, transpose_a=True
    )


def local_covariance(tile_data):
    return lax.dot_general(
        tile_data, tile_data, (((1,), (1,)), ((), ())), preferred_element_type=jnp.float32
    )


def body(sky_maps, beam_index, beam_taps, start_seed):
    channels, strip_rows, columns = sky_maps.shape
    beam_count, tap_count = beam_taps.shape
    half_taps = (tap_count - 1) // 2
    onehot = (beam_index[:, None] == jnp.arange(beam_count, dtype=jnp.int32)[None, :]).astype(
        jnp.float32
    )
    tap_rows = jnp.dot(onehot, beam_taps, precision=lax.Precision.HIGHEST)
    kernels = tap_rows / jnp.sum(tap_rows, axis=1, keepdims=True)
    padded = with_halo(sky_maps, (("sky", 1),), half_taps)
    smoothed = column_pass(padded, kernels, strip_rows, half_taps, tap_count)
    freq_count = lax.axis_size("freq")
    sky_count = lax.axis_size("sky")
    tile_cols = columns // freq_count
    grouped = lax.all_to_all(
        smoothed.reshape(channels, strip_rows, freq_count, tile_cols),
        "freq",
        split_axis=2,
        concat_axis=0,
        tiled=True,
    )
    all_chans = channels * freq_count
    tile_data = grouped.reshape(all_chans, strip_rows * tile_cols)
    wide_tile = tile_data.astype(jnp.float32)
    total_pixels = strip_rows * columns * sky_count
    subspace = start_seed.astype(jnp.float32)
    covariance = lax.psum(local_covariance(tile_data), ("freq", "sky")) / total_pixels
    for sweep in range(ITERS):
        images = jnp.dot(covariance, subspace, precision=lax.Precision.HIGHEST)
        subspace = orthonormal(images)
    coeffs = jnp.dot(subspace.T, wide_tile, precision=lax.Precision.HIGHEST)
    cleaned = (wide_tile - jnp.dot(subspace, coeffs, precision=lax.Precision.HIGHEST)).astype(
        jnp.bfloat16
    )
    return cleaned.reshape(all_chans, 1, strip_rows * tile_cols)


def solution(mesh):
    return jax.shard_map(
        body,
        mesh=mesh,
        in_specs=(P("freq", "sky", None), P("freq"), P(), P()),
        out_specs=P(None, ("freq", "sky"), None),
        check_vma=False,
    )
```

profile of v0, /device:TPU:33, one launch (start us, length us, event | category | flops | bytes accessed | tf_op | source)
XLA Modules:
  0.0 662.7 jit_solution(16235698417459183960)
XLA Ops:
  6.5 2.9 fusion.109
  10.7 3.2 collective-permute-start
  18.0 37.3 %collective-permute-done = bf16[16,15,4096]{2,0,1:T(8,128)(2,1)S(1)} collective-permute-done((bf16[16,15,4096]{2,0,1:T(8,128)(2,1)S(1)}, bf16[16,15,4096]{2,0,1:T(8,128)(2,1)S(1)}, u32[]{:S(2)}, u32[]{:S(2)}) %collective-permute-start) | collective-permute-done | bytes 1966112 | tf_op jit(solution)/shard_map/ppermute | solution.py:16
  56.4 4.0 collective-permute-done.1
  61.5 40.9 %multiply_add_fusion = f32[16,24,4096]{2,1,0:T(8,128)S(1)} fusion(bf16[16,24,4096]{2,1,0:T(8,128)(2,1)S(1)} %copy-done.2, bf16[16,15,4096]{2,1,0:T(8,128)(2,1)S(1)} %copy.24, bf16[16,39,4096]{2,1,0:T(8,128)(2,1)S(1)} %copy_dynamic-update-slice_fusion, f32[16]{0:T(128)S(1)} %get-tuple-element.8, f32[16]{0:T(128)S(1)} %get-tuple-element.9, ...), kind=kLoop, calls=%fused_computation.62 | loop fusion | flops 215482368 | bytes 58591168 | tf_op jit(solution)/shard_map/add | solution.py:25
  102.3 50.4 %add_convert_fusion = bf16[16,24,4096]{2,1,0:T(8,128)(2,1)S(1)} fusion(f32[16,24,4096]{2,1,0:T(8,128)S(1)} %multiply_add_fusion, f32[16]{0:T(128)S(1)} %get-tuple-element.8, f32[16]{0:T(128)S(1)} %get-tuple-element.9, f32[16]{0:T(128)S(1)} %get-tuple-element.10, f32[16]{0:T(128)S(1)} %get-tuple-element.11, f32[16]{0:T(128)S(1)} %get-tuple-element.12, ...), kind=kLoop, calls=%fused_computation.29 | loop fusion | flops 97517568 | bytes 9439168 | tf_op jit(solution)/shard_map/convert_element_type | solution.py:35
  152.8 7.9 %reshape.54 = bf16[16,24,64,64]{3,2,1,0:T(8,128)(2,1)} reshape(bf16[16,24,4096]{2,1,0:T(8,128)(2,1)S(1)} %add_convert_fusion) | data formatting | bytes 6291456 | tf_op jit(solution)/shard_map/reshape | solution.py:67
  160.7 9.5 %copy.40 = bf16[16,24,64,64]{3,1,0,2:T(8,128)(2,1)} copy(bf16[16,24,64,64]{3,2,1,0:T(8,128)(2,1)} %reshape.54) | data formatting | bytes 6291456 | tf_op jit(solution)/shard_map/reshape | solution.py:67
  170.2 9.7 %reshape.118 = bf16[64,2,12288]{2,1,0:T(2,128)(2,1)S(1)} reshape(bf16[64,16,24,64]{3,2,1,0:T(8,128)(2,1)} %bitcast.141) | data formatting | bytes 6291456
  179.9 85.8 %all_to_all.15 = bf16[64,2,12288]{2,1,0:T(2,128)(2,1)} all-to-all(bf16[64,2,12288]{2,1,0:T(2,128)(2,1)S(1)} %reshape.118), channel_id=1, replica_groups=mesh['freq'=64,'sky'=4] {'freq'}, dimensions={0} | all-to-all | bytes 6291456 | tf_op jit(solution)/shard_map/all_to_all | solution.py:66
  265.7 11.1 %reshape.119 = bf16[64,16,24,64]{3,2,1,0:T(8,128)(2,1)} reshape(bf16[64,2,12288]{2,1,0:T(2,128)(2,1)} %all_to_all.15) | data formatting | bytes 6291456
  276.8 7.4 %bitcast_bitcast_fusion = bf16[64,16,24,1,64]{4,2,1,0,3:T(8,128)(2,1)} fusion(bf16[64,16,24,64]{3,2,1,0:T(8,128)(2,1)} %reshape.119), kind=kLoop, calls=%fused_computation.224 | loop fusion | bytes 6291456 | tf_op jit(solution)/shard_map/all_to_all | solution.py:66
  284.2 7.9 %reshape.55 = bf16[1024,1536]{1,0:T(8,128)(2,1)S(1)} reshape(bf16[64,16,24,1,64]{4,2,1,0,3:T(8,128)(2,1)} %bitcast_bitcast_fusion) | data formatting | bytes 6291456 | tf_op jit(solution)/shard_map/reshape | solution.py:74
  292.2 5.4 fusion.111
  297.6 265.8 %all-reduce.3.cloned.1.call-done = f32[1024,1024]{1,0:T(8,128)} async-done(((f32[1024,1024]{1,0:T(8,128)}), f32[1024,1024]{1,0:T(8,128)}) %all-reduce.3.cloned.1.call-update) | async-done | bytes 4194320 | tf_op jit(solution)/shard_map/psum | solution.py:78
  563.4 5.9 fusion.50
  569.6 1.5 cholesky.134
  573.9 5.9 fusion.48
  580.1 1.5 cholesky.145
  584.4 5.9 fusion.46
  590.5 1.5 cholesky.156
  594.9 5.9 fusion.44
  601.0 1.6 cholesky.167
  605.5 5.9 fusion.42
  611.7 1.5 cholesky.178
  616.0 5.9 fusion.40
  622.1 1.5 cholesky.189
  626.5 5.9 fusion.38
  632.6 1.5 cholesky.200
  637.0 5.9 fusion.36
  643.3 1.5 cholesky.211
  649.0 6.7 %fusion.21 = bf16[1024,1,1536]{2,0,1:T(8,128)(2,1)} fusion(f32[1024,16]{0,1:T(8,128)S(1)} %convolution_bitcast_fusion, f32[16,1536]{1,0:T(8,128)S(1)} %fusion.120, bf16[1024,1536]{1,0:T(8,128)(2,1)S(1)} %reshape.55), kind=kOutput, calls=%fused_computation.63 | convolution fusion | flops 306708480 | bytes 6455296 | tf_op jit(solution)/shard_map/dot_general | solution.py:83
  (87 shorter events, 33.7 us)
Async XLA Ops:
  6.5 9.8 %copy-start = (f32[8,31]{1,0:T(8,128)S(1)}, f32[8,31]{1,0:T(8,128)}, u32[]{:S(2)}) copy-start(f32[8,31]{1,0:T(8,128)} %param.9) | copy-start | bytes 2980
  6.5 9.8 %copy-start.4 = (s32[16]{0:T(128)S(1)}, s32[16]{0:T(128)}, u32[]{:S(2)}) copy-start(s32[16]{0:T(128)} %param.8) | copy-start | bytes 196
  6.5 556.9 %all-reduce.3.cloned.1.call-start = ((), (), s32[]{:S(2)}) async-start(), calls=%async_computation.1 | async-start | bytes 8388608 | tf_op jit(solution)/shard_map/psum | solution.py:78
  9.5 8.2 %copy-start.2 = (bf16[16,24,4096]{2,1,0:T(8,128)(2,1)S(1)}, bf16[16,24,4096]{2,1,0:T(8,128)(2,1)}, u32[]{:S(2)}) copy-start(bf16[16,24,4096]{2,1,0:T(8,128)(2,1)} %param.7) | copy-start | bytes 9437188
  10.7 44.6 %collective-permute-start = (bf16[16,15,4096]{2,0,1:T(8,128)(2,1)S(1)}, bf16[16,15,4096]{2,0,1:T(8,128)(2,1)S(1)}, u32[]{:S(2)}, u32[]{:S(2)}) collective-permute-start(bf16[16,15,4096]{2,0,1:T(8,128)(2,1)S(1)} %copy.36), channel_id=1, source_target_pairs={{0,1},{1,2},{2,3},{4,5},{5,6},{6,7},{8,9},{9,10},{10,11},{12,13},{... | collective-permute-start | bytes 5898248 | tf_op jit(solution)/shard_map/ppermute | solution.py:16
  15.1 45.3 %collective-permute-start.1 = (bf16[16,15,4096]{2,0,1:T(8,128)(2,1)S(1)}, bf16[16,15,4096]{2,0,1:T(8,128)(2,1)S(1)}, u32[]{:S(2)}, u32[]{:S(2)}) collective-permute-start(bf16[16,15,4096]{2,0,1:T(8,128)(2,1)S(1)} %copy.37), channel_id=1, source_target_pairs={{1,0},{2,1},{3,2},{5,4},{6,5},{7,6},{9,8},{10,9},{11,10},{13,12},{... | collective-permute-start | bytes 5898248 | tf_op jit(solution)/shard_map/ppermute | solution.py:17
  292.1 271.3 %copy-start.3 = (s32[1024,16]{0,1:T(8,128)S(1)}, s32[1024,16]{0,1:T(8,128)}, u32[]{:S(2)}) copy-start(s32[1024,16]{0,1:T(8,128)} %param.10) | copy-start | bytes 196612
  636.7 18.9 %copy-start.1 = (f32[8,31]{1,0:T(8,128)S(1)}, f32[8,31]{1,0:T(8,128)}, u32[]{:S(2)}) copy-start(f32[8,31]{1,0:T(8,128)} %param.9) | copy-start | bytes 2980
Sparse Core Ops, SparseCore 0:
  297.7 265.6 all-reduce.2
where the time goes:
time: 671 us; the launch traced here: 663 us
  waiting for transfers between devices  307 us (46%)
  other arithmetic  124 us (18%)
  blocking collectives  85.8 us (13%)
  matrix products  64.5 us (10%)
  local copies, waits for them, and re-layouts  62.9 us (9%)
  between operations  13.9 us (2%)
    psum x1, waiting for transfers between devices, body(): lax.psum(local_covariance(tile_data), ('freq', 'sky')) / total_pixels  266 us
    all_to_all x1, blocking collectives, body(): lax.all_to_all(smoothed.reshape(channels, strip_rows, freq_count, tile_co...  85.8 us
    convert_element_type x1, other arithmetic, column_pass(): return col_pass.astype(jnp.bfloat16)  50.4 us
    dot_general x8, matrix products, body(): images = jnp.dot(covariance, subspace, precision=lax.Precision.HIGHEST)  47 us
    add x1, other arithmetic, column_pass(): row_pass + kernels[:, offset, None, None] * padded[:, offset:offset + str...  40.9 us
    ppermute x1, waiting for transfers between devices, with_halo(): before = lax.ppermute(last, axis, up)  37.3 us
    unnamed x15, local copies, waits for them, and re-layouts  23.5 us
    another operation x24, other arithmetic, orthonormal(): factor = jnp.linalg.cholesky(gram_matrix)  17.5 us
  transfers between devices with their start and end apart: 3, of which 3 were waited for; matrix products, arithmetic and copies ran while one was open for 1% of the time, Pallas kernels for 0%

commit v1 on v0

v1 whole, which is shorter than its diff:
```python
import jax
import jax.numpy as jnp
from jax import lax
from jax.experimental import pallas as pl
from jax.experimental.pallas import tpu as pltpu
from jax.sharding import Mesh, PartitionSpec as P

ITERS = 8
F32 = jnp.float32
BF16 = jnp.bfloat16
NT = (((1,), (1,)), ((), ()))
TN = (((0,), (0,)), ((), ()))
VMEM_LIMIT = 60 * 1024 * 1024


def vmem():
    return pl.BlockSpec(memory_space=pltpu.VMEM)


def smem():
    return pl.BlockSpec(memory_space=pltpu.SMEM)


def split2(x):
    hi = x.astype(BF16)
    return hi, (x - hi.astype(F32)).astype(BF16)


def split3(x):
    hi = x.astype(BF16)
    rest = x - hi.astype(F32)
    mid = rest.astype(BF16)
    return hi, mid, (rest - mid.astype(F32)).astype(BF16)


def prep_kernel(index_ref, taps_ref, col_ref, row_ref, order_ref, padded_ref):
    beams, taps = taps_ref.shape
    channels = index_ref.shape[0]
    padded_ref[...] = jnp.zeros_like(padded_ref)
    padded_ref[:, 0:taps] = taps_ref[...]
    table = padded_ref[...]
    table = table / jnp.sum(table, axis=1, keepdims=True)
    padded_ref[...] = table
    for beam in range(beams):
        line = jnp.broadcast_to(table[beam : beam + 1, :], (128, 256))
        band = pltpu.roll(line, 49, 1, stride=1, stride_axis=0)
        hi, mid = split2(band)
        col_ref[beam, 0:128, :] = hi
        col_ref[beam, 128:256, :] = mid
    lane = lax.broadcasted_iota(jnp.int32, (32, 256), 1)
    line_no = lax.broadcasted_iota(jnp.int32, (32, 256), 0)
    for channel in range(channels):
        line = jnp.broadcast_to(padded_ref[pl.ds(index_ref[channel], 1), :], (32, 256))
        band = pltpu.roll(line, 1, 1, stride=1, stride_axis=0)
        moved = pltpu.roll(band, 8, 1)
        band = jnp.where(lane < 32, band, jnp.where(lane < 40, 0.0, moved))
        band = jnp.where((lane < 64) & (line_no < 24), band, 0.0)
        group, place = channel // 4, channel % 4
        if place:
            band = pltpu.roll(band, 64 * place, 1)
        for part, value in enumerate(split3(band)):
            row_ref[group, part * 128 + place * 32 : part * 128 + place * 32 + 32, :] = value
    rows = order_ref.shape[0]
    out_row = lax.broadcasted_iota(jnp.int32, order_ref.shape, 0)
    in_row = lax.broadcasted_iota(jnp.int32, order_ref.shape, 1)
    count = rows // 24
    wanted = (out_row % count) * 32 + out_row // count
    order_ref[...] = jnp.where(in_row == wanted, 1.0, 0.0).astype(BF16)


def prepare(beam_index, beam_taps, chunk):
    channels = beam_index.shape[0]
    beams = beam_taps.shape[0]
    return pl.pallas_call(
        prep_kernel,
        out_shape=(
            jax.ShapeDtypeStruct((beams, 256, 256), BF16),
            jax.ShapeDtypeStruct((channels // 4, 384, 256), BF16),
            jax.ShapeDtypeStruct((chunk * 24, chunk * 32), BF16),
        ),
        in_specs=[smem(), vmem()],
        out_specs=(vmem(), vmem(), vmem()),
        scratch_shapes=[pltpu.VMEM((beams, 256), F32)],
        cost_estimate=pl.CostEstimate(flops=10**6, bytes_accessed=2 * 10**6, transcendentals=0),
        name="prep",
    )(beam_index, beam_taps)


def smooth_kernel(
    index_ref, before, top, bottom, after, col_ref, row_ref, order_ref, out_ref, hi_ref, mid_ref, sm_ref
):
    channels = before.shape[0]
    columns = before.shape[2]
    blocks = columns // 256
    tiles = columns // 128
    lane = lax.broadcasted_iota(jnp.int32, (128, 128), 1)
    for group in range(channels // 4):
        weights = row_ref[group]

        def row_step(n, tail):
            cols = pl.ds(pl.multiple_of(n * 256, 256), 256)
            data = jnp.concatenate(
                [
                    ref[group * 4 + place, :, cols]
                    for place in range(4)
                    for ref in (before, top, bottom, after)
                ],
                axis=0,
            )
            full = jnp.dot(weights, data, preferred_element_type=F32)
            value = full[0:128] + full[128:256] + full[256:384]
            moved = pltpu.roll(value, 64, 1)
            first = jnp.where(lane < 64, tail, moved[:, 0:128])
            for half, piece in ((0, first), (1, moved[:, 128:256])):
                hi, mid = split2(piece)
                for place in range(4):
                    rows = slice(place * 32, place * 32 + 32)
                    hi_ref[group * 4 + place, 2 * n + half] = hi[rows]
                    mid_ref[group * 4 + place, 2 * n + half] = mid[rows]
            return moved[:, 0:128]

        tail = lax.fori_loop(0, blocks, row_step, jnp.zeros((128, 128), F32))
        hi, mid = split2(jnp.where(lane < 64, tail, 0.0))
        for place in range(4):
            rows = slice(place * 32, place * 32 + 32)
            hi_ref[group * 4 + place, tiles] = hi[rows]
            mid_ref[group * 4 + place, tiles] = mid[rows]

    run = 16

    def col_step(channel, carry):
        band = col_ref[index_ref[channel]]
        rows = pl.ds(pl.multiple_of(channel * 32, 32), 32)
        for start in range(0, tiles, run):
            total = None
            for ref in (hi_ref, mid_ref):
                data = jnp.concatenate(
                    [
                        ref[channel, start : start + run].reshape(run * 32, 128),
                        ref[channel, start + 1 : start + run + 1].reshape(run * 32, 128),
                    ],
                    axis=1,
                )
                term = lax.dot_general(data, band, NT, preferred_element_type=F32)
                total = term if total is None else total + term
            value = (total[:, 0:128] + total[:, 128:256]).astype(BF16)
            sm_ref[start : start + run, rows, :] = value.reshape(run, 32, 128)
        return carry

    lax.fori_loop(0, channels, col_step, 0)

    lane3 = lax.broadcasted_iota(jnp.int32, (12, channels, 128), 2)

    def place_step(n, carry):
        data = jnp.concatenate([sm_ref[2 * n], sm_ref[2 * n + 1]], axis=1)
        moved = jnp.dot(order_ref[...], data, preferred_element_type=F32)
        for t in range(2):
            four = moved[:, t * 128 : t * 128 + 128].reshape(12, 2, channels, 128)
            even, odd = four[:, 0], four[:, 1]
            low = jnp.where(lane3 < 64, even, pltpu.roll(odd, 64, 2)).astype(BF16)
            high = jnp.where(lane3 < 64, pltpu.roll(even, 64, 2), odd).astype(BF16)
            for q in range(12):
                out_ref[4 * n + 2 * t, :, q * 128 : q * 128 + 128] = low[q]
                out_ref[4 * n + 2 * t + 1, :, q * 128 : q * 128 + 128] = high[q]
        return carry

    lax.fori_loop(0, blocks, place_step, 0)


def smooth(beam_index, before, top, bottom, after, col, row, order):
    channels, _, columns = before.shape
    tiles = columns // 128
    return pl.pallas_call(
        smooth_kernel,
        out_shape=jax.ShapeDtypeStruct((columns // 64, channels, 1536), BF16),
        in_specs=[smem()] + [vmem()] * 7,
        out_specs=vmem(),
        scratch_shapes=[
            pltpu.VMEM((channels, tiles + 1, 32, 128), BF16),
            pltpu.VMEM((channels, tiles + 1, 32, 128), BF16),
            pltpu.VMEM((tiles, channels * 32, 128), BF16),
        ],
        compiler_params=pltpu.CompilerParams(vmem_limit_bytes=VMEM_LIMIT),
        cost_estimate=pl.CostEstimate(
            flops=8 * 10**9, bytes_accessed=15 * 10**6, transcendentals=0
        ),
        name="smooth",
    )(beam_index, before, top, bottom, after, col, row, order)


def cov_kernel(core_ref, data_ref, keep_ref, send_ref):
    core = core_ref[0]

    def fill(out_ref, first):
        def step(i, carry):
            block = first + i
            left = data_ref[pl.ds(pl.multiple_of(block * 128, 128), 128), :]
            for d in range(5):
                other = lax.rem(block + d, 8)
                right = data_ref[pl.ds(pl.multiple_of(other * 128, 128), 128), :]
                out_ref[i, d * 128 : d * 128 + 128, :] = lax.dot_general(
                    left, right, NT, preferred_element_type=F32
                )
            return carry

        lax.fori_loop(0, 4, step, 0)

    fill(keep_ref, core * 4)
    fill(send_ref, (1 - core) * 4)


def local_covariance(core, data):
    shape = jax.ShapeDtypeStruct((4, 640, 128), F32)
    return pl.pallas_call(
        cov_kernel,
        out_shape=(shape, shape),
        in_specs=[smem(), vmem()],
        out_specs=(vmem(), vmem()),
        compiler_params=pltpu.CompilerParams(vmem_limit_bytes=VMEM_LIMIT),
        cost_estimate=pl.CostEstimate(
            flops=2 * 10**9, bytes_accessed=6 * 10**6, transcendentals=0
        ),
        name="cov",
    )(core, data)


def everywhere(x, axes, size):
    copies = jnp.broadcast_to(x[None], (size,) + x.shape)
    return lax.all_to_all(copies, axes, 0, 0, tiled=True)


def reduce_all(keep, send):
    swap = [(0, 1), (1, 0)]
    half = keep + lax.ppermute(send, "core", swap)
    got = lax.all_to_all(half.reshape(4, 640, 128), "sky", 0, 0, tiled=True)
    quarter = jnp.sum(got, axis=0)
    got = lax.all_to_all(quarter.reshape(32, 20, 128), ("y", "z"), 0, 0, tiled=True)
    mine = jnp.sum(got, axis=0)
    quarter = everywhere(mine, ("y", "z"), 32).reshape(640, 128)
    half = everywhere(quarter, "sky", 4).reshape(4, 640, 128)
    other = lax.ppermute(half, "core", swap)
    return half, other


def inverse_factor(gram):
    size = gram.shape[0]
    row = lax.broadcasted_iota(jnp.int32, (size, 128), 0)
    lane = lax.broadcasted_iota(jnp.int32, (size, 128), 1)
    unit = jnp.where(lane == row + size, 1.0, 0.0).astype(F32)
    work = jnp.concatenate([gram, jnp.zeros((size, 128 - size), F32)], axis=1) + unit
    for j in range(size):
        column = work[:, j : j + 1]
        factor = jnp.where(row[:, 0:1] > j, column, 0.0) * (1.0 / work[j : j + 1, j : j + 1])
        work = work - factor * work[j : j + 1, :]
    pivot = jnp.sum(jnp.where(lane == row, work, 0.0), axis=1, keepdims=True)
    scale = lax.rsqrt(pivot)
    scale = scale * (1.5 - 0.5 * pivot * scale * scale)
    return (work * scale)[:, size : 2 * size]


def clean_kernel(core_ref, near_ref, far_ref, seed_ref, data_ref, out_ref, cov_ref, basis_ref, coef_ref):
    core = core_ref[0]
    modes = seed_ref.shape[0]
    count = seed_ref.shape[1]
    pixels = data_ref.shape[1]
    scale = 1.0 / (256 * pixels)
    for i in range(8):
        for d in range(5):
            rows = slice(d * 128, d * 128 + 128)
            near, far = near_ref[i % 4, rows, :], far_ref[i % 4, rows, :]
            block = jnp.where(core == i // 4, near, far) * scale
            j = (i + d) % 8
            hi, mid = split2(block)
            cov_ref[i * 128 : i * 128 + 128, j * 128 : j * 128 + 128] = hi
            cov_ref[i * 128 : i * 128 + 128, count + j * 128 : count + j * 128 + 128] = mid
            if d in (1, 2, 3):
                hi, mid = split2(block.T)
                cov_ref[j * 128 : j * 128 + 128, i * 128 : i * 128 + 128] = hi
                cov_ref[j * 128 : j * 128 + 128, count + i * 128 : count + i * 128 + 128] = mid

    def fold(x):
        return x[0:modes] + x[modes : 2 * modes] + x[2 * modes : 3 * modes]

    def stack(x):
        return jnp.concatenate(split3(x), axis=0)

    def times_cov(parts):
        wide = fold(jnp.dot(parts, cov_ref[...], preferred_element_type=F32))
        return wide[:, 0:count] + wide[:, count : 2 * count]

    def gram_of(parts):
        tall = fold(lax.dot_general(parts, parts, NT, preferred_element_type=F32))
        return tall[:, 0:modes] + tall[:, modes : 2 * modes] + tall[:, 2 * modes : 3 * modes]

    def exact_dot(a, b):
        return lax.dot(a, b, precision=lax.Precision.HIGHEST, preferred_element_type=F32)

    images = times_cov(stack(seed_ref[...].astype(F32)))

    def sweep(step, images):
        parts = stack(images)
        inverse = inverse_factor(gram_of(parts))
        return exact_dot(inverse, times_cov(parts))

    images = lax.fori_loop(0, ITERS - 1, sweep, images)
    basis = exact_dot(inverse_factor(gram_of(stack(images))), images)
    hi, mid, low = split3(basis)
    basis_ref[...] = jnp.concatenate([hi, hi, mid, mid, hi, low], axis=0)
    data = data_ref[...]
    coef = fold(
        jnp.dot(jnp.concatenate([hi, mid, low], axis=0), data, preferred_element_type=F32)
    )
    hi, mid, low = split3(coef)
    coef_ref[...] = jnp.concatenate([hi, mid, hi, mid, low, hi], axis=0)
    for m in range(count // 128):
        rows = slice(m * 128, m * 128 + 128)
        part = lax.dot_general(
            basis_ref[:, rows], coef_ref[...], TN, preferred_element_type=F32
        )
        out_ref[rows, :] = (data_ref[rows, :].astype(F32) - part).astype(BF16)


def clean(core, near, far, seed, data):
    modes, count = seed.shape
    pixels = data.shape[1]
    return pl.pallas_call(
        clean_kernel,
        out_shape=jax.ShapeDtypeStruct((count, pixels), BF16),
        in_specs=[smem()] + [vmem()] * 4,
        out_specs=vmem(),
        scratch_shapes=[
            pltpu.VMEM((count, 2 * count), BF16),
            pltpu.VMEM((6 * modes, count), BF16),
            pltpu.VMEM((6 * modes, pixels), BF16),
        ],
        compiler_params=pltpu.CompilerParams(vmem_limit_bytes=VMEM_LIMIT),
        cost_estimate=pl.CostEstimate(
            flops=3 * 10**9, bytes_accessed=12 * 10**6, transcendentals=0
        ),
        name="clean",
    )(core, near, far, seed, data)


def body(sky_maps, beam_index, beam_taps, start_seed):
    channels, strip_rows, columns = sky_maps.shape
    core = lax.axis_index("core").astype(jnp.int32).reshape(1)
    top = sky_maps[:, 0:16, :]
    bottom = sky_maps[:, strip_rows - 16 : strip_rows, :]
    before = lax.ppermute(bottom, "sky", [(i, i + 1) for i in range(3)])
    after = lax.ppermute(top, "sky", [(i + 1, i) for i in range(3)])
    col, row, order = prepare(beam_index, beam_taps, channels)
    pieces = smooth(beam_index, before, top, bottom, after, col, row, order)
    data = lax.all_to_all(pieces, ("y", "z", "core"), 0, 0, tiled=True)
    data = data.reshape(64 * channels, 1536)
    keep, send = local_covariance(core, data)
    near, far = reduce_all(keep, send)
    cleaned = clean(core, near, far, start_seed.T, data)
    return cleaned[:, None, :]


def solution(mesh):
    fine = Mesh(mesh.devices.reshape(4, 8, 2, 4), ("y", "z", "core", "sky"))
    freq = ("y", "z", "core")
    return jax.shard_map(
        body,
        mesh=fine,
        in_specs=(P(freq, "sky", None), P(freq), P(), P()),
        out_specs=P(None, freq + ("sky",), None),
        check_vma=False,
    )
```

time: 671 us -> 302 us (0.45); the launches traced: 663 us -> 302 us
  waiting for transfers between devices: 307 us -> 122 us
  other arithmetic: 124 us -> 1.63 us
  Pallas kernels: 0 us -> 73.6 us
  matrix products: 64.5 us -> 0 us
  local copies, waits for them, and re-layouts: 62.9 us -> 6.87 us
  starting transfers between devices: 4.53 us -> 22.9 us
  between operations: 13.9 us -> 0.07 us
  blocking collectives: 85.8 us -> 75.3 us
    psum x1 -> x0, waiting for transfers between devices: 266 us -> none  [body(): lax.psum(local_covariance(tile_data), ('freq', 'sky')) / total_pixels]
    pallas_call x0 -> x4, Pallas kernels: none -> 73.6 us  [the longest x1 38.5 us: smooth(): pl.pallas_call(smooth_kernel, out_shape=jax.ShapeDtypeStruct((columns //...]
    all_to_all x0 -> x1, waiting for transfers between devices: none -> 72.4 us  [body(): data = lax.all_to_all(pieces, ('y', 'z', 'core'), 0, 0, tiled=True)]
    dot_general x20 -> x0, matrix products: 62.4 us -> none  [the longest x8 47 us: body(): images = jnp.dot(covariance, subspace, precision=lax.Precision.HIGHEST)]
    convert_element_type x1 -> x0, other arithmetic: 50.4 us -> none  [column_pass(): return col_pass.astype(jnp.bfloat16)]
    add x1, other arithmetic: 40.9 us -> 1.5 us  [reduce_all(): half = keep + lax.ppermute(send, 'core', swap)]
    another operation x40 -> x0, other arithmetic: 32.5 us -> none  [the longest x24 17.5 us: orthonormal(): factor = jnp.linalg.cholesky(gram_matrix)]
    reshape x3 -> x1, local copies, waits for them, and re-layouts: 25.3 us -> 0.03 us  [reduce_all(): quarter.reshape(32, 20, 128)]
  transfers between devices with their start and end apart: 3 -> 5, of which waited for: 3 -> 5; matrix products, arithmetic and copies ran while one was open for 1% -> 0% of each run, Pallas kernels for 0% -> 1%
where the time goes in v1:
time: 302 us
  waiting for transfers between devices  122 us (40%)
  blocking collectives  75.3 us (25%)
  Pallas kernels  73.6 us (24%)
  starting transfers between devices  22.9 us (8%)
  local copies, waits for them, and re-layouts  6.87 us (2%)
    all_to_all x1, waiting for transfers between devices, body(): data = lax.all_to_all(pieces, ('y', 'z', 'core'), 0, 0, tiled=True)  72.4 us
    pallas_call x1, Pallas kernels, smooth(): pl.pallas_call(smooth_kernel, out_shape=jax.ShapeDtypeStruct((columns //...  38.5 us
    ppermute x1, waiting for transfers between devices, body(): before = lax.ppermute(bottom, 'sky', [(i, i + 1) for i in range(3)])  38.4 us
    all_to_all x2, blocking collectives, everywhere(): return lax.all_to_all(copies, axes, 0, 0, tiled=True)  35.8 us
    pallas_call x1, Pallas kernels, clean(): pl.pallas_call(clean_kernel, out_shape=jax.ShapeDtypeStruct((count, pixel...  22.9 us
    all_to_all x1, blocking collectives, reduce_all(): got = lax.all_to_all(half.reshape(4, 640, 128), 'sky', 0, 0, tiled=True)  20.1 us
    all_to_all x1, blocking collectives, reduce_all(): lax.all_to_all(quarter.reshape(32, 20, 128), ('y', 'z'), 0, 0, tiled=True)  19.4 us
    all_to_all x1, starting transfers between devices, body(): data = lax.all_to_all(pieces, ('y', 'z', 'core'), 0, 0, tiled=True)  13.2 us
  transfers between devices with their start and end apart: 5, of which 5 were waited for; matrix products, arithmetic and copies ran while one was open for 0% of the time, Pallas kernels for 1%

profile of v1, /device:TPU:33, one launch (start us, length us, event | category | flops | bytes accessed | tf_op | source)
XLA Modules:
  0.0 301.9 jit_solution(15145127754603263387)
XLA Ops:
  0.0 4.0 %fusion = (bf16[16,16,4096]{2,1,0:T(8,128)(2,1)S(1)}, bf16[16,16,4096]{2,1,0:T(8,128)(2,1)}) fusion(bf16[16,24,4096]{2,1,0:T(8,128)(2,1)} %param.4), kind=kLoop, calls=%fused_computation | loop fusion | bytes 8388608 | tf_op jit(solution)/shard_map/slice | solution.py:347
  4.0 0.0 copy-start.1
  4.0 4.4 %collective-permute-start = (bf16[16,16,4096]{2,1,0:T(8,128)(2,1)}, bf16[16,16,4096]{2,1,0:T(8,128)(2,1)}, u32[]{:S(2)}, u32[]{:S(2)}) collective-permute-start(bf16[16,16,4096]{2,1,0:T(8,128)(2,1)} %get-tuple-element.16.bottom), channel_id=1, source_target_pairs={{0,1},{1,2},{2,3},{4,5},{5,6},{6,7},{8,9},{9,10},{10,11},{12,13},{... | collective-permute-start | bytes 6291464 | tf_op jit(solution)/shard_map/ppermute | solution.py:349
  8.4 1.3 collective-permute-start.1
  9.7 3.7 %prep.1 = (bf16[8,256,256]{2,1,0:T(8,128)(2,1)}, bf16[4,384,256]{2,1,0:T(8,128)(2,1)}, bf16[384,512]{1,0:T(8,128)(2,1)}) custom-call(s32[16]{0:T(128)} %index_ref.3, f32[8,31]{1,0:T(8,128)} %taps_ref.1), custom_call_target="tpu_custom_call" | custom-call | flops 1000000 | bytes 2000000 | tf_op jit(solution)/shard_map/prep/pallas_call | solution.py:74
  13.3 38.4 %collective-permute-done.before = bf16[16,16,4096]{2,1,0:T(8,128)(2,1)} collective-permute-done((bf16[16,16,4096]{2,1,0:T(8,128)(2,1)}, bf16[16,16,4096]{2,1,0:T(8,128)(2,1)}, u32[]{:S(2)}, u32[]{:S(2)}) %collective-permute-start) | collective-permute-done | bytes 2097184 | tf_op jit(solution)/shard_map/ppermute | solution.py:349
  51.7 4.9 %collective-permute-done.1.after = bf16[16,16,4096]{2,1,0:T(8,128)(2,1)} collective-permute-done((bf16[16,16,4096]{2,1,0:T(8,128)(2,1)S(1)}, bf16[16,16,4096]{2,1,0:T(8,128)(2,1)}, u32[]{:S(2)}, u32[]{:S(2)}) %collective-permute-start.1) | collective-permute-done | bytes 2097184 | tf_op jit(solution)/shard_map/ppermute | solution.py:350
  56.6 0.0 copy-done.1
  56.6 38.5 %smooth.1 = bf16[64,16,1536]{2,1,0:T(8,128)(2,1)} custom-call(s32[16]{0:T(128)} %index_ref.3, bf16[16,16,4096]{2,1,0:T(8,128)(2,1)} %collective-permute-done.before, bf16[16,16,4096]{2,1,0:T(8,128)(2,1)} %copy-done.1, bf16[16,16,4096]{2,1,0:T(8,128)(2,1)} %get-tuple-element.16.bottom, bf16[16,16,4096]{2,1,0:T(8,128)(2,1)} %collective-permute-done.1.after, ...), custom_call_target="tpu_custom_call" | custom-call | flops 8000000000 | bytes 15000000 | tf_op jit(solution)/shard_map/smooth/pallas_call | solution.py:173
  95.1 13.2 %all-to-all-start = ((bf16[64,16,1536]{2,1,0:T(8,128)(2,1)}), bf16[64,16,1536]{2,1,0:T(8,128)(2,1)S(1)}, u32[]{:S(2)}, u32[]{:S(2)}) async-start(bf16[64,16,1536]{2,1,0:T(8,128)(2,1)} %smooth.1), calls=%async_computation | async-start | bytes 6291456 | tf_op jit(solution)/shard_map/all_to_all | solution.py:353
  108.3 72.4 %all-to-all-done = bf16[64,16,1536]{2,1,0:T(8,128)(2,1)S(1)} async-done(((bf16[64,16,1536]{2,1,0:T(8,128)(2,1)}), bf16[64,16,1536]{2,1,0:T(8,128)(2,1)S(1)}, u32[]{:S(2)}, u32[]{:S(2)}) %all-to-all-start) | async-done | bytes 3145760 | tf_op jit(solution)/shard_map/all_to_all | solution.py:353
  180.7 0.0 copy-start
  180.7 1.6 copy-done
  182.4 8.7 %cov.1 = (f32[4,640,128]{2,1,0:T(8,128)}, f32[4,640,128]{2,1,0:T(8,128)}) custom-call(s32[1]{0:T(128)} %bitcast.core_ref, bf16[1024,1536]{1,0:T(8,128)(2,1)} %bitcast.4), custom_call_target="tpu_custom_call" | custom-call | flops 2000000000 | bytes 6000000 | tf_op jit(solution)/shard_map/cov/pallas_call | solution.py:214
  191.0 0.0 collective-permute-start.2
  191.0 3.2 %collective-permute-done.2 = f32[4,640,128]{2,1,0:T(8,128)S(1)} collective-permute-done((f32[4,640,128]{2,1,0:T(8,128)}, f32[4,640,128]{2,1,0:T(8,128)S(1)}, u32[]{:S(2)}, u32[]{:S(2)}) %collective-permute-start.2) | collective-permute-done | bytes 1310752 | tf_op jit(solution)/shard_map/ppermute | solution.py:234
  194.3 1.5 add.3
  195.8 20.1 %all_to_all.25 = f32[4,640,128]{2,1,0:T(8,128)S(1)} all-to-all(f32[4,640,128]{2,1,0:T(8,128)S(1)} %add.3), channel_id=1, replica_groups=mesh['y'=4,'z'=8,'core'=2,'sky'=4] {'sky'}, dimensions={0} | all-to-all | bytes 2621440 | tf_op jit(solution)/shard_map/all_to_all | solution.py:235
  215.9 0.1 reduce_sum.18
  216.0 19.4 %all_to_all.26 = f32[32,20,128]{2,1,0:T(8,128)S(1)} all-to-all(f32[32,20,128]{2,1,0:T(8,128)S(1)} %reshape.13), channel_id=1, replica_groups=mesh['y'=4,'z'=8,'core'=2,'sky'=4] {'y','z'}, dimensions={0} | all-to-all | bytes 655360 | tf_op jit(solution)/shard_map/all_to_all | solution.py:237
  235.5 18.4 %all_to_all.27 = f32[32,20,128]{2,1,0:T(8,128)S(1)} all-to-all(f32[32,20,128]{2,1,0:T(8,128)S(1)} %broadcast_in_dim.16), channel_id=1, replica_groups=mesh['y'=4,'z'=8,'core'=2,'sky'=4] {'y','z'}, dimensions={0} | all-to-all | bytes 655360 | tf_op jit(solution)/shard_map/all_to_all | solution.py:229
  253.9 0.1 broadcast_in_dim.18
  254.0 17.3 %all_to_all.28.near_ref = f32[4,640,128]{2,1,0:T(8,128)S(1)} all-to-all(f32[4,640,128]{2,1,0:T(8,128)S(1)} %broadcast_in_dim.18), channel_id=1, replica_groups=mesh['y'=4,'z'=8,'core'=2,'sky'=4] {'sky'}, dimensions={0} | all-to-all | bytes 2621440 | tf_op jit(solution)/shard_map/all_to_all | solution.py:229
  271.4 0.0 copy-start.2
  271.4 3.9 %collective-permute-start.3 = (f32[4,640,128]{2,1,0:T(8,128)S(1)}, f32[4,640,128]{2,1,0:T(8,128)S(1)}, u32[]{:S(2)}, u32[]{:S(2)}) collective-permute-start(f32[4,640,128]{2,1,0:T(8,128)S(1)} %all_to_all.28.near_ref), channel_id=1, source_target_pairs={{0,4},{4,0},{1,5},{5,1},{2,6},{6,2},{3,7},{7,3},{8,12},{12,8},{9,1... | collective-permute-start | bytes 3932168 | tf_op jit(solution)/shard_map/ppermute | solution.py:241
  275.3 2.7 collective-permute-done.3.far_ref
  278.0 0.0 copy-start.3
  278.0 0.0 copy-done.2
  278.0 1.1 copy-done.3
  279.1 22.9 %clean.1 = bf16[1024,1536]{1,0:T(8,128)(2,1)} custom-call(s32[1]{0:T(128)} %bitcast.core_ref, f32[4,640,128]{2,1,0:T(8,128)} %copy-done.2, f32[4,640,128]{2,1,0:T(8,128)} %copy-done.3, s32[16,1024]{1,0:T(8,128)} %bitcast.6, bf16[1024,1536]{1,0:T(8,128)(2,1)} %bitcast.5), custom_call_target="tpu_custom_call" | custom-call | flops 3000000000 | bytes 12000000 | tf_op jit(solution)/shard_map/clean/pallas_call | solution.py:326
  (4 shorter events, 0.1 us)
Async XLA Ops:
  4.0 52.6 %copy-start.1 = (bf16[16,16,4096]{2,1,0:T(8,128)(2,1)}, bf16[16,16,4096]{2,1,0:T(8,128)(2,1)S(1)}, u32[]{:S(2)}) copy-start(bf16[16,16,4096]{2,1,0:T(8,128)(2,1)S(1)} %get-tuple-element.15.top) | copy-start | bytes 6291460
  4.0 47.7 %collective-permute-start = (bf16[16,16,4096]{2,1,0:T(8,128)(2,1)}, bf16[16,16,4096]{2,1,0:T(8,128)(2,1)}, u32[]{:S(2)}, u32[]{:S(2)}) collective-permute-start(bf16[16,16,4096]{2,1,0:T(8,128)(2,1)} %get-tuple-element.16.bottom), channel_id=1, source_target_pairs={{0,1},{1,2},{2,3},{4,5},{5,6},{6,7},{8,9},{9,10},{10,11},{12,13},{... | collective-permute-start | bytes 6291464 | tf_op jit(solution)/shard_map/ppermute | solution.py:349
  8.4 48.2 %collective-permute-start.1 = (bf16[16,16,4096]{2,1,0:T(8,128)(2,1)S(1)}, bf16[16,16,4096]{2,1,0:T(8,128)(2,1)}, u32[]{:S(2)}, u32[]{:S(2)}) collective-permute-start(bf16[16,16,4096]{2,1,0:T(8,128)(2,1)S(1)} %get-tuple-element.15.top), channel_id=1, source_target_pairs={{1,0},{2,1},{3,2},{5,4},{6,5},{7,6},{9,8},{10,9},{11,10},{13,12},{... | collective-permute-start | bytes 6291464 | tf_op jit(solution)/shard_map/ppermute | solution.py:350
  95.1 85.7 %all-to-all-start = ((bf16[64,16,1536]{2,1,0:T(8,128)(2,1)}), bf16[64,16,1536]{2,1,0:T(8,128)(2,1)S(1)}, u32[]{:S(2)}, u32[]{:S(2)}) async-start(bf16[64,16,1536]{2,1,0:T(8,128)(2,1)} %smooth.1), calls=%async_computation | async-start | bytes 6291456 | tf_op jit(solution)/shard_map/all_to_all | solution.py:353
  180.7 1.6 copy-start
  191.0 3.2 %collective-permute-start.2 = (f32[4,640,128]{2,1,0:T(8,128)}, f32[4,640,128]{2,1,0:T(8,128)S(1)}, u32[]{:S(2)}, u32[]{:S(2)}) collective-permute-start(f32[4,640,128]{2,1,0:T(8,128)} %get-tuple-element.14), channel_id=1, source_target_pairs={{0,4},{4,0},{1,5},{5,1},{2,6},{6,2},{3,7},{7,3},{8,12},{12,8},{9,1... | collective-permute-start | bytes 3932168 | tf_op jit(solution)/shard_map/ppermute | solution.py:234
  271.4 6.6 %copy-start.2 = (f32[4,640,128]{2,1,0:T(8,128)}, f32[4,640,128]{2,1,0:T(8,128)S(1)}, u32[]{:S(2)}) copy-start(f32[4,640,128]{2,1,0:T(8,128)S(1)} %all_to_all.28.near_ref) | copy-start | bytes 3932164
  271.4 6.6 %collective-permute-start.3 = (f32[4,640,128]{2,1,0:T(8,128)S(1)}, f32[4,640,128]{2,1,0:T(8,128)S(1)}, u32[]{:S(2)}, u32[]{:S(2)}) collective-permute-start(f32[4,640,128]{2,1,0:T(8,128)S(1)} %all_to_all.28.near_ref), channel_id=1, source_target_pairs={{0,4},{4,0},{1,5},{5,1},{2,6},{6,2},{3,7},{7,3},{8,12},{12,8},{9,1... | collective-permute-start | bytes 3932168 | tf_op jit(solution)/shard_map/ppermute | solution.py:241
  278.0 1.1 copy-start.3

commit v2 on v1

--- a/solution.py
+++ b/solution.py
@@ -10,6 +10,8 @@
 BF16 = jnp.bfloat16
 NT = (((1,), (1,)), ((), ()))
 TN = (((0,), (0,)), ((), ()))
+ROW_UNROLL, COL_UNROLL, PLACE_UNROLL, COL_RUN = 16, 4, 16, 16
+CHUNK = 8
 VMEM_LIMIT = 60 * 1024 * 1024
 
 
@@ -89,106 +91,123 @@
 def smooth_kernel(
     index_ref, before, top, bottom, after, col_ref, row_ref, order_ref, out_ref, hi_ref, mid_ref, sm_ref
 ):
-    channels = before.shape[0]
+    group = pl.program_id(0)
     columns = before.shape[2]
     blocks = columns // 256
     tiles = columns // 128
     lane = lax.broadcasted_iota(jnp.int32, (128, 128), 1)
-    for group in range(channels // 4):
-        weights = row_ref[group]
-
-        def row_step(n, tail):
-            cols = pl.ds(pl.multiple_of(n * 256, 256), 256)
-            data = jnp.concatenate(
-                [
-                    ref[group * 4 + place, :, cols]
-                    for place in range(4)
-                    for ref in (before, top, bottom, after)
-                ],
-                axis=0,
-            )
-            full = jnp.dot(weights, data, preferred_element_type=F32)
-            value = full[0:128] + full[128:256] + full[256:384]
-            moved = pltpu.roll(value, 64, 1)
-            first = jnp.where(lane < 64, tail, moved[:, 0:128])
-            for half, piece in ((0, first), (1, moved[:, 128:256])):
-                hi, mid = split2(piece)
-                for place in range(4):
-                    rows = slice(place * 32, place * 32 + 32)
-                    hi_ref[group * 4 + place, 2 * n + half] = hi[rows]
-                    mid_ref[group * 4 + place, 2 * n + half] = mid[rows]
-            return moved[:, 0:128]
-
-        tail = lax.fori_loop(0, blocks, row_step, jnp.zeros((128, 128), F32))
-        hi, mid = split2(jnp.where(lane < 64, tail, 0.0))
+
+    def keep(tile, piece):
+        hi, mid = split2(piece)
         for place in range(4):
             rows = slice(place * 32, place * 32 + 32)
-            hi_ref[group * 4 + place, tiles] = hi[rows]
-            mid_ref[group * 4 + place, tiles] = mid[rows]
-
-    run = 16
-
-    def col_step(channel, carry):
+            hi_ref[place, tile] = hi[rows]
+            mid_ref[place, tile] = mid[rows]
+
+    def row_step(n, tail):
+        cols = pl.ds(pl.multiple_of(n * 256, 256), 256)
+        data = jnp.concatenate(
+            [ref[place, :, cols] for place in range(4) for ref in (before, top, bottom, after)],
+            axis=0,
+        )
+        full = jnp.dot(row_ref[0], data, preferred_element_type=F32)
+        value = full[0:128] + full[128:256] + full[256:384]
+        moved = pltpu.roll(value, 64, 1)
+        keep(2 * n, jnp.where(lane < 64, tail, moved[:, 0:128]))
+        keep(2 * n + 1, moved[:, 128:256])
+        return moved[:, 0:128]
+
+    tail = lax.fori_loop(0, blocks, row_step, jnp.zeros((128, 128), F32), unroll=ROW_UNROLL)
+    keep(tiles, jnp.where(lane < 64, tail, 0.0))
+
+    def col_step(place, carry):
+        channel = group * 4 + place
         band = col_ref[index_ref[channel]]
         rows = pl.ds(pl.multiple_of(channel * 32, 32), 32)
-        for start in range(0, tiles, run):
+        for start in range(0, tiles, COL_RUN):
             total = None
             for ref in (hi_ref, mid_ref):
                 data = jnp.concatenate(
                     [
-                        ref[channel, start : start + run].reshape(run * 32, 128),
-                        ref[channel, start + 1 : start + run + 1].reshape(run * 32, 128),
+                        ref[place, start : start + COL_RUN].reshape(COL_RUN * 32, 128),
+                        ref[place, start + 1 : start + COL_RUN + 1].reshape(COL_RUN * 32, 128),
                     ],
                     axis=1,
                 )
                 term = lax.dot_general(data, band, NT, preferred_element_type=F32)
                 total = term if total is None else total + term
             value = (total[:, 0:128] + total[:, 128:256]).astype(BF16)
-            sm_ref[start : start + run, rows, :] = value.reshape(run, 32, 128)
+            sm_ref[start : start + COL_RUN, rows, :] = value.reshape(COL_RUN, 32, 128)
         return carry
 
-    lax.fori_loop(0, channels, col_step, 0)
-
-    lane3 = lax.broadcasted_iota(jnp.int32, (12, channels, 128), 2)
-
-    def place_step(n, carry):
-        data = jnp.concatenate([sm_ref[2 * n], sm_ref[2 * n + 1]], axis=1)
-        moved = jnp.dot(order_ref[...], data, preferred_element_type=F32)
-        for t in range(2):
-            four = moved[:, t * 128 : t * 128 + 128].reshape(12, 2, channels, 128)
-            even, odd = four[:, 0], four[:, 1]
-            low = jnp.where(lane3 < 64, even, pltpu.roll(odd, 64, 2)).astype(BF16)
-            high = jnp.where(lane3 < 64, pltpu.roll(even, 64, 2), odd).astype(BF16)
-            for q in range(12):
-                out_ref[4 * n + 2 * t, :, q * 128 : q * 128 + 128] = low[q]
-                out_ref[4 * n + 2 * t + 1, :, q * 128 : q * 128 + 128] = high[q]
-        return carry
-
-    lax.fori_loop(0, blocks, place_step, 0)
+    lax.fori_loop(0, 4, col_step, 0, unroll=COL_UNROLL)
+
+    @pl.when(group == pl.num_programs(0) - 1)
+    def _():
+        channels = out_ref.shape[1]
+        lane3 = lax.broadcasted_iota(jnp.int32, (12, channels, 128), 2)
+
+        def place_step(n, carry):
+            data = jnp.concatenate([sm_ref[2 * n], sm_ref[2 * n + 1]], axis=1)
+            moved = jnp.dot(order_ref[...], data, preferred_element_type=F32)
+            for t in range(2):
+                four = moved[:, t * 128 : t * 128 + 128].reshape(12, 2, channels, 128)
+                even, odd = four[:, 0], four[:, 1]
+                low = jnp.where(lane3 < 64, even, pltpu.roll(odd, 64, 2)).astype(BF16)
+                high = jnp.where(lane3 < 64, pltpu.roll(even, 64, 2), odd).astype(BF16)
+                for q in range(12):
+                    out_ref[4 * n + 2 * t, :, q * 128 : q * 128 + 128] = low[q]
+                    out_ref[4 * n + 2 * t + 1, :, q * 128 : q * 128 + 128] = high[q]
+            return carry
+
+        lax.fori_loop(0, blocks, place_step, 0, unroll=PLACE_UNROLL)
 
 
 def smooth(beam_index, before, top, bottom, after, col, row, order):
     channels, _, columns = before.shape
     tiles = columns // 128
+    strip = pl.BlockSpec((4, 16, columns), lambda g: (g, 0, 0))
     return pl.pallas_call(
         smooth_kernel,
+        grid=(channels // 4,),
         out_shape=jax.ShapeDtypeStruct((columns // 64, channels, 1536), BF16),
-        in_specs=[smem()] + [vmem()] * 7,
-        out_specs=vmem(),
+        in_specs=[smem()]
+        + [strip] * 4
+        + [
+            pl.BlockSpec(col.shape, lambda g: (0, 0, 0)),
+            pl.BlockSpec((1,) + row.shape[1:], lambda g: (g, 0, 0)),
+            pl.BlockSpec(order.shape, lambda g: (0, 0)),
+        ],
+        out_specs=pl.BlockSpec((columns // 64, channels, 1536), lambda g: (0, 0, 0)),
         scratch_shapes=[
-            pltpu.VMEM((channels, tiles + 1, 32, 128), BF16),
-            pltpu.VMEM((channels, tiles + 1, 32, 128), BF16),
+            pltpu.VMEM((4, tiles + 1, 32, 128), BF16),
+            pltpu.VMEM((4, tiles + 1, 32, 128), BF16),
             pltpu.VMEM((tiles, channels * 32, 128), BF16),
         ],
         compiler_params=pltpu.CompilerParams(vmem_limit_bytes=VMEM_LIMIT),
         cost_estimate=pl.CostEstimate(
-            flops=8 * 10**9, bytes_accessed=15 * 10**6, transcendentals=0
+            flops=5 * 10**8 * channels, bytes_accessed=10**6 * channels, transcendentals=0
         ),
         name="smooth",
     )(beam_index, before, top, bottom, after, col, row, order)
 
 
-def cov_kernel(core_ref, data_ref, keep_ref, send_ref):
+def load_parts(parts, data_ref, sems):
+    copies, first = [], 0
+    for k, part in enumerate(parts):
+        rows = part.shape[0]
+        copies.append(
+            pltpu.make_async_copy(part, data_ref.at[first : first + rows], sems.at[k])
+        )
+        first += rows
+    for copy in copies:
+        copy.start()
+    return copies
+
+
+def cov_kernel(core_ref, part0, part1, keep_ref, send_ref, data_ref, sems):
+    for copy in load_parts((part0, part1), data_ref, sems):
+        copy.wait()
     core = core_ref[0]
 
     def fill(out_ref, first):
@@ -209,19 +228,28 @@
     fill(send_ref, (1 - core) * 4)
 
 
-def local_covariance(core, data):
+def anywhere():
+    return pl.BlockSpec(memory_space=pl.ANY)
+
+
+def local_covariance(core, parts):
     shape = jax.ShapeDtypeStruct((4, 640, 128), F32)
+    rows = sum(part.shape[0] for part in parts)
     return pl.pallas_call(
         cov_kernel,
         out_shape=(shape, shape),
-        in_specs=[smem(), vmem()],
+        in_specs=[smem(), anywhere(), anywhere()],
         out_specs=(vmem(), vmem()),
+        scratch_shapes=[
+            pltpu.VMEM((rows, parts[0].shape[1]), BF16),
+            pltpu.SemaphoreType.DMA((2,)),
+        ],
         compiler_params=pltpu.CompilerParams(vmem_limit_bytes=VMEM_LIMIT),
         cost_estimate=pl.CostEstimate(
             flops=2 * 10**9, bytes_accessed=6 * 10**6, transcendentals=0
         ),
         name="cov",
-    )(core, data)
+    )(core, *parts)
 
 
 def everywhere(x, axes, size):
@@ -258,8 +286,11 @@
     return (work * scale)[:, size : 2 * size]
 
 
-def clean_kernel(core_ref, near_ref, far_ref, seed_ref, data_ref, out_ref, cov_ref, basis_ref, coef_ref):
+def clean_kernel(
+    core_ref, near_ref, far_ref, seed_ref, part0, part1, out_ref, data_ref, cov_ref, basis_ref, coef_ref, sems
+):
     core = core_ref[0]
+    copies = load_parts((part0, part1), data_ref, sems)
     modes = seed_ref.shape[0]
     count = seed_ref.shape[1]
     pixels = data_ref.shape[1]
@@ -306,6 +337,8 @@
     basis = exact_dot(inverse_factor(gram_of(stack(images))), images)
     hi, mid, low = split3(basis)
     basis_ref[...] = jnp.concatenate([hi, hi, mid, mid, hi, low], axis=0)
+    for copy in copies:
+        copy.wait()
     data = data_ref[...]
     coef = fold(
         jnp.dot(jnp.concatenate([hi, mid, low], axis=0), data, preferred_element_type=F32)
@@ -317,45 +350,60 @@
         part = lax.dot_general(
             basis_ref[:, rows], coef_ref[...], TN, preferred_element_type=F32
         )
-        out_ref[rows, :] = (data_ref[rows, :].astype(F32) - part).astype(BF16)
-
-
-def clean(core, near, far, seed, data):
+        value = (data_ref[rows, :].astype(F32) - part).astype(BF16)
+        chunk, first = m // 4, (m % 4) * 16
+        out_ref[first : first + 16, chunk * 8 : chunk * 8 + 8, :] = value.reshape(16, 8, pixels)
+
+
+def clean(core, near, far, seed, parts):
     modes, count = seed.shape
-    pixels = data.shape[1]
+    pixels = parts[0].shape[1]
     return pl.pallas_call(
         clean_kernel,
-        out_shape=jax.ShapeDtypeStruct((count, pixels), BF16),
-        in_specs=[smem()] + [vmem()] * 4,
+        out_shape=jax.ShapeDtypeStruct((count // 16, 16, pixels), BF16),
+        in_specs=[smem()] + [vmem()] * 3 + [anywhere(), anywhere()],
         out_specs=vmem(),
         scratch_shapes=[
+            pltpu.VMEM((count, pixels), BF16),
             pltpu.VMEM((count, 2 * count), BF16),
             pltpu.VMEM((6 * modes, count), BF16),
             pltpu.VMEM((6 * modes, pixels), BF16),
+            pltpu.SemaphoreType.DMA((2,)),
         ],
         compiler_params=pltpu.CompilerParams(vmem_limit_bytes=VMEM_LIMIT),
         cost_estimate=pl.CostEstimate(
             flops=3 * 10**9, bytes_accessed=12 * 10**6, transcendentals=0
         ),
         name="clean",
-    )(core, near, far, seed, data)
+    )(core, near, far, seed, *parts)
 
 
 def body(sky_maps, beam_index, beam_taps, start_seed):
     channels, strip_rows, columns = sky_maps.shape
+    modes = start_seed.shape[1]
     core = lax.axis_index("core").astype(jnp.int32).reshape(1)
-    top = sky_maps[:, 0:16, :]
-    bottom = sky_maps[:, strip_rows - 16 : strip_rows, :]
-    before = lax.ppermute(bottom, "sky", [(i, i + 1) for i in range(3)])
-    after = lax.ppermute(top, "sky", [(i + 1, i) for i in range(3)])
-    col, row, order = prepare(beam_index, beam_taps, channels)
-    pieces = smooth(beam_index, before, top, bottom, after, col, row, order)
-    data = lax.all_to_all(pieces, ("y", "z", "core"), 0, 0, tiled=True)
-    data = data.reshape(64 * channels, 1536)
-    keep, send = local_covariance(core, data)
+    col, row, order = prepare(beam_index, beam_taps, CHUNK)
+    halos = []
+    for first in range(0, channels, CHUNK):
+        strip = sky_maps[first : first + CHUNK]
+        top = strip[:, 0:16, :]
+        bottom = strip[:, strip_rows - 16 : strip_rows, :]
+        before = lax.ppermute(bottom, "sky", [(i, i + 1) for i in range(3)])
+        after = lax.ppermute(top, "sky", [(i + 1, i) for i in range(3)])
+        halos.append((before, top, bottom, after))
+    parts = []
+    for k, halo in enumerate(halos):
+        mine = slice(k * CHUNK, (k + 1) * CHUNK)
+        rows = row[k * CHUNK // 4 : (k + 1) * CHUNK // 4]
+        pieces = smooth(beam_index[mine], *halo, col, rows, order)
+        data = lax.all_to_all(pieces, ("y", "z", "core"), 0, 0, tiled=True)
+        parts.append(data.reshape(64 * CHUNK, 1536))
+    seed = start_seed.T.reshape(modes, 64, channels // CHUNK, CHUNK)
+    seed = seed.transpose(0, 2, 1, 3).reshape(modes, 64 * channels)
+    keep, send = local_covariance(core, parts)
     near, far = reduce_all(keep, send)
-    cleaned = clean(core, near, far, start_seed.T, data)
-    return cleaned[:, None, :]
+    cleaned = clean(core, near, far, seed, parts)
+    return cleaned.reshape(64 * channels, 1, 1536)
 
 
 def solution(mesh):

time: 302 us -> 263 us (0.87)
  waiting for transfers between devices: 122 us -> 87.8 us
  Pallas kernels: 73.6 us -> 51.1 us
  starting transfers between devices: 22.9 us -> 36.8 us
    all_to_all x1 -> x2, waiting for transfers between devices: 72.4 us -> 40.3 us  [body(): data = lax.all_to_all(pieces, ('y', 'z', 'core'), 0, 0, tiled=True)]
    pallas_call x3 -> x4, Pallas kernels: 70 us -> 47.6 us  [the longest x1 22 us: clean(): pl.pallas_call(clean_kernel, out_shape=jax.ShapeDtypeStruct((count // 16,...]
    all_to_all x1 -> x2, starting transfers between devices: 13.2 us -> 23.4 us  [body(): data = lax.all_to_all(pieces, ('y', 'z', 'core'), 0, 0, tiled=True)]
    ppermute x1 -> x2, waiting for transfers between devices: 38.4 us -> 34.4 us  [body(): before = lax.ppermute(bottom, 'sky', [(i, i + 1) for i in range(3)])]
    ppermute x1 -> x2, waiting for transfers between devices: 4.92 us -> 8.51 us  [body(): after = lax.ppermute(top, 'sky', [(i + 1, i) for i in range(3)])]
    slice x1 -> x3, local copies, waits for them, and re-layouts: 3.96 us -> 6.2 us  [the longest x1 3.53 us: body(): top = strip[:, 0:16, :]]
    ppermute x1 -> x2, starting transfers between devices: 4.42 us -> 6.31 us  [body(): before = lax.ppermute(bottom, 'sky', [(i, i + 1) for i in range(3)])]
  transfers between devices with their start and end apart: 5 -> 8, of which waited for: 5 -> 8; matrix products, arithmetic and copies ran while one was open for 0% -> 1% of each run, Pallas kernels for 1% -> 5%
where the time goes in v2:
time: 263 us; the launch traced here: 262 us
  waiting for transfers between devices  87.8 us (33%)
  blocking collectives  75.1 us (29%)
  Pallas kernels  51.1 us (19%)
  starting transfers between devices  36.8 us (14%)
  local copies, waits for them, and re-layouts  9.57 us (4%)
    all_to_all x2, waiting for transfers between devices, body(): data = lax.all_to_all(pieces, ('y', 'z', 'core'), 0, 0, tiled=True)  40.3 us
    all_to_all x2, blocking collectives, everywhere(): return lax.all_to_all(copies, axes, 0, 0, tiled=True)  35.8 us
    ppermute x2, waiting for transfers between devices, body(): before = lax.ppermute(bottom, 'sky', [(i, i + 1) for i in range(3)])  34.4 us
    all_to_all x2, starting transfers between devices, body(): data = lax.all_to_all(pieces, ('y', 'z', 'core'), 0, 0, tiled=True)  23.4 us
    pallas_call x1, Pallas kernels, clean(): pl.pallas_call(clean_kernel, out_shape=jax.ShapeDtypeStruct((count // 16,...  22 us
    all_to_all x1, blocking collectives, reduce_all(): got = lax.all_to_all(half.reshape(4, 640, 128), 'sky', 0, 0, tiled=True)  19.9 us
    all_to_all x1, blocking collectives, reduce_all(): lax.all_to_all(quarter.reshape(32, 20, 128), ('y', 'z'), 0, 0, tiled=True)  19.4 us
    pallas_call x2, Pallas kernels, smooth(): pl.pallas_call(smooth_kernel, grid=(channels // 4,), out_shape=jax.ShapeD...  16.9 us
  transfers between devices with their start and end apart: 8, of which 8 were waited for; matrix products, arithmetic and copies ran while one was open for 1% of the time, Pallas kernels for 5%

profile of v2, /device:TPU:33, one launch (start us, length us, event | category | flops | bytes accessed | tf_op | source)
XLA Modules:
  0.0 262.3 jit_solution(951585047746499131)
XLA Ops:
  0.0 3.5 %fusion = (bf16[8,16,4096]{2,1,0:T(8,128)(2,1)S(1)}, bf16[8,16,4096]{2,1,0:T(8,128)(2,1)S(1)}, bf16[8,16,4096]{2,1,0:T(8,128)(2,1)}, bf16[8,16,4096]{2,1,0:T(8,128)(2,1)S(1)}) fusion(bf16[16,24,4096]{2,1,0:T(8,128)(2,1)} %param.4), kind=kLoop, calls=%fused_computation | loop fusion | bytes 8388608 | tf_op jit(solution)/shard_map/slice | solution.py:389
  3.5 4.1 %collective-permute-start.2 = (bf16[8,16,4096]{2,1,0:T(8,128)(2,1)S(1)}, bf16[8,16,4096]{2,1,0:T(8,128)(2,1)}, u32[]{:S(2)}, u32[]{:S(2)}) collective-permute-start(bf16[8,16,4096]{2,1,0:T(8,128)(2,1)S(1)} %get-tuple-element.18.bottom), channel_id=1, source_target_pairs={{0,1},{1,2},{2,3},{4,5},{5,6},{6,7},{8,9},{9,10},{10,11},{12,13},{... | collective-permute-start | bytes 3145736 | tf_op jit(solution)/shard_map/ppermute | solution.py:391
  7.7 1.3 collective-permute-start.3
  8.9 3.5 %prep.1 = (bf16[8,256,256]{2,1,0:T(8,128)(2,1)}, bf16[4,384,256]{2,1,0:T(8,128)(2,1)}, bf16[192,256]{1,0:T(8,128)(2,1)}) custom-call(s32[16]{0:T(128)} %index_ref.1, f32[8,31]{1,0:T(8,128)} %taps_ref.1), custom_call_target="tpu_custom_call" | custom-call | flops 1000000 | bytes 2000000 | tf_op jit(solution)/shard_map/prep/pallas_call | solution.py:76
  12.5 0.6 fusion.2
  13.0 2.1 fusion.1
  15.1 13.4 %collective-permute-done.2.before = bf16[8,16,4096]{2,1,0:T(8,128)(2,1)} collective-permute-done((bf16[8,16,4096]{2,1,0:T(8,128)(2,1)S(1)}, bf16[8,16,4096]{2,1,0:T(8,128)(2,1)}, u32[]{:S(2)}, u32[]{:S(2)}) %collective-permute-start.2) | collective-permute-done | bytes 1048608 | tf_op jit(solution)/shard_map/ppermute | solution.py:391
  28.5 4.9 %collective-permute-done.3.after = bf16[8,16,4096]{2,1,0:T(8,128)(2,1)} collective-permute-done((bf16[8,16,4096]{2,1,0:T(8,128)(2,1)S(1)}, bf16[8,16,4096]{2,1,0:T(8,128)(2,1)}, u32[]{:S(2)}, u32[]{:S(2)}) %collective-permute-start.3) | collective-permute-done | bytes 1048608 | tf_op jit(solution)/shard_map/ppermute | solution.py:392
  33.4 8.5 %smooth.3 = bf16[64,8,1536]{2,1,0:T(8,128)(2,1)} custom-call(s32[8]{0:T(128)} %get-tuple-element.21.index_ref, bf16[8,16,4096]{2,1,0:T(8,128)(2,1)} %collective-permute-done.2.before, bf16[8,16,4096]{2,1,0:T(8,128)(2,1)} %copy-done.3, bf16[8,16,4096]{2,1,0:T(8,128)(2,1)} %copy-done.4, bf16[8,16,4096]{2,1,0:T(8,128)(2,1)} %collective-permute-done.3.after, ...), custom_call_target="tpu_custom_call" | custom-call | flops 4000000000 | bytes 8000000 | tf_op jit(solution)/shard_map/smooth/pallas_call | solution.py:170
  41.9 13.2 %all-to-all-start.1 = ((bf16[64,8,1536]{2,1,0:T(8,128)(2,1)}), bf16[64,8,1536]{2,1,0:T(8,128)(2,1)S(1)}, u32[]{:S(2)}, u32[]{:S(2)}) async-start(bf16[64,8,1536]{2,1,0:T(8,128)(2,1)} %smooth.3), calls=%async_computation.1 | async-start | bytes 3145728 | tf_op jit(solution)/shard_map/all_to_all | solution.py:399
  55.1 2.2 collective-permute-start
  57.3 1.3 collective-permute-start.1
  58.6 21.0 %collective-permute-done.before = bf16[8,16,4096]{2,1,0:T(8,128)(2,1)S(1)} collective-permute-done((bf16[8,16,4096]{2,1,0:T(8,128)(2,1)}, bf16[8,16,4096]{2,1,0:T(8,128)(2,1)S(1)}, u32[]{:S(2)}, u32[]{:S(2)}) %collective-permute-start) | collective-permute-done | bytes 1048608 | tf_op jit(solution)/shard_map/ppermute | solution.py:391
  79.6 3.6 %collective-permute-done.1.after = bf16[8,16,4096]{2,1,0:T(8,128)(2,1)S(1)} collective-permute-done((bf16[8,16,4096]{2,1,0:T(8,128)(2,1)S(1)}, bf16[8,16,4096]{2,1,0:T(8,128)(2,1)S(1)}, u32[]{:S(2)}, u32[]{:S(2)}) %collective-permute-start.1) | collective-permute-done | bytes 1048608 | tf_op jit(solution)/shard_map/ppermute | solution.py:392
  83.2 1.0 copy-done.8
  84.2 8.4 %smooth.2 = bf16[64,8,1536]{2,1,0:T(8,128)(2,1)} custom-call(s32[8]{0:T(128)} %get-tuple-element.22.index_ref, bf16[8,16,4096]{2,1,0:T(8,128)(2,1)} %copy-done.7, bf16[8,16,4096]{2,1,0:T(8,128)(2,1)} %copy-done.2, bf16[8,16,4096]{2,1,0:T(8,128)(2,1)} %get-tuple-element.17.bottom, bf16[8,16,4096]{2,1,0:T(8,128)(2,1)} %copy-done.8, ...), custom_call_target="tpu_custom_call" | custom-call | flops 4000000000 | bytes 8000000 | tf_op jit(solution)/shard_map/smooth/pallas_call | solution.py:170
  92.7 1.4 all-to-all-done.1
  94.1 1.1 copy-done
  95.2 10.2 %all-to-all-start = ((bf16[64,8,1536]{2,1,0:T(8,128)(2,1)}), bf16[64,8,1536]{2,1,0:T(8,128)(2,1)}, u32[]{:S(2)}, u32[]{:S(2)}) async-start(bf16[64,8,1536]{2,1,0:T(8,128)(2,1)} %smooth.2), calls=%async_computation | async-start | bytes 3145728 | tf_op jit(solution)/shard_map/all_to_all | solution.py:399
  105.4 38.9 %all-to-all-done = bf16[64,8,1536]{2,1,0:T(8,128)(2,1)} async-done(((bf16[64,8,1536]{2,1,0:T(8,128)(2,1)}), bf16[64,8,1536]{2,1,0:T(8,128)(2,1)}, u32[]{:S(2)}, u32[]{:S(2)}) %all-to-all-start) | async-done | bytes 1572896 | tf_op jit(solution)/shard_map/all_to_all | solution.py:399
  144.4 8.7 %cov.1 = (f32[4,640,128]{2,1,0:T(8,128)}, f32[4,640,128]{2,1,0:T(8,128)}) custom-call(s32[1]{0:T(128)} %bitcast.core_ref, bf16[512,1536]{1,0:T(8,128)(2,1)} %bitcast.1.part0, bf16[512,1536]{1,0:T(8,128)(2,1)} %bitcast.11), custom_call_target="tpu_custom_call" | custom-call | flops 2000000000 | bytes 6000000 | tf_op jit(solution)/shard_map/cov/pallas_call | solution.py:238
  153.0 0.5 collective-permute-start.4
  153.6 2.9 %collective-permute-done.4 = f32[4,640,128]{2,1,0:T(8,128)S(1)} collective-permute-done((f32[4,640,128]{2,1,0:T(8,128)}, f32[4,640,128]{2,1,0:T(8,128)S(1)}, u32[]{:S(2)}, u32[]{:S(2)}) %collective-permute-start.4) | collective-permute-done | bytes 1310752 | tf_op jit(solution)/shard_map/ppermute | solution.py:262
  156.5 1.5 add.3
  158.0 19.9 %all_to_all.30 = f32[4,640,128]{2,1,0:T(8,128)S(1)} all-to-all(f32[4,640,128]{2,1,0:T(8,128)S(1)} %add.3), channel_id=1, replica_groups=mesh['y'=4,'z'=8,'core'=2,'sky'=4] {'sky'}, dimensions={0} | all-to-all | bytes 2621440 | tf_op jit(solution)/shard_map/all_to_all | solution.py:263
  178.0 19.4 %all_to_all.31 = f32[32,20,128]{2,1,0:T(8,128)S(1)} all-to-all(f32[32,20,128]{2,1,0:T(8,128)S(1)} %reshape.26), channel_id=1, replica_groups=mesh['y'=4,'z'=8,'core'=2,'sky'=4] {'y','z'}, dimensions={0} | all-to-all | bytes 655360 | tf_op jit(solution)/shard_map/all_to_all | solution.py:265
  197.4 18.4 %all_to_all.32 = f32[32,20,128]{2,1,0:T(8,128)S(1)} all-to-all(f32[32,20,128]{2,1,0:T(8,128)S(1)} %broadcast_in_dim.6), channel_id=1, replica_groups=mesh['y'=4,'z'=8,'core'=2,'sky'=4] {'y','z'}, dimensions={0} | all-to-all | bytes 655360 | tf_op jit(solution)/shard_map/all_to_all | solution.py:257
  215.9 17.5 %all_to_all.33.near_ref = f32[4,640,128]{2,1,0:T(8,128)S(1)} all-to-all(f32[4,640,128]{2,1,0:T(8,128)S(1)} %broadcast_in_dim.15), channel_id=1, replica_groups=mesh['y'=4,'z'=8,'core'=2,'sky'=4] {'sky'}, dimensions={0} | all-to-all | bytes 2621440 | tf_op jit(solution)/shard_map/all_to_all | solution.py:257
  233.4 4.0 %collective-permute-start.5 = (f32[4,640,128]{2,1,0:T(8,128)S(1)}, f32[4,640,128]{2,1,0:T(8,128)}, u32[]{:S(2)}, u32[]{:S(2)}) collective-permute-start(f32[4,640,128]{2,1,0:T(8,128)S(1)} %all_to_all.33.near_ref), channel_id=1, source_target_pairs={{0,4},{4,0},{1,5},{5,1},{2,6},{6,2},{3,7},{7,3},{8,12},{12,8},{9,1... | collective-permute-start | bytes 3932168 | tf_op jit(solution)/shard_map/ppermute | solution.py:269
  237.6 0.8 copy.8.seed_ref
  238.4 1.7 collective-permute-done.5.far_ref
  240.1 22.0 %clean.1 = bf16[64,16,1536]{2,1,0:T(8,128)(2,1)} custom-call(s32[1]{0:T(128)} %bitcast.core_ref, f32[4,640,128]{2,1,0:T(8,128)} %copy-done.1, f32[4,640,128]{2,1,0:T(8,128)} %collective-permute-done.5.far_ref, s32[16,1024]{1,0:T(8,128)} %copy.8.seed_ref, bf16[512,1536]{1,0:T(8,128)(2,1)} %bitcast.1.part0, bf16[512,1536]{1,0:T(8,128)(2,1)} %bitcast.12), custom_call_target="tpu_custom_call" | custom-call | flops 3000000000 | bytes 12000000 | tf_op jit(solution)/shard_map/clean/pallas_call | solution.py:361
  (24 shorter events, 0.6 us)
Async XLA Ops:
  0.0 12.5 %copy-start.6 = (s32[16]{0:T(128)S(1)}, s32[16]{0:T(128)}, u32[]{:S(2)}) copy-start(s32[16]{0:T(128)} %index_ref.1) | copy-start | bytes 196
  3.5 29.9 %copy-start.3 = (bf16[8,16,4096]{2,1,0:T(8,128)(2,1)}, bf16[8,16,4096]{2,1,0:T(8,128)(2,1)S(1)}, u32[]{:S(2)}) copy-start(bf16[8,16,4096]{2,1,0:T(8,128)(2,1)S(1)} %get-tuple-element.15.top) | copy-start | bytes 3145732
  3.5 29.9 %copy-start.4 = (bf16[8,16,4096]{2,1,0:T(8,128)(2,1)}, bf16[8,16,4096]{2,1,0:T(8,128)(2,1)S(1)}, u32[]{:S(2)}) copy-start(bf16[8,16,4096]{2,1,0:T(8,128)(2,1)S(1)} %get-tuple-element.18.bottom) | copy-start | bytes 3145732
  3.5 53.7 %copy-start.2 = (bf16[8,16,4096]{2,1,0:T(8,128)(2,1)}, bf16[8,16,4096]{2,1,0:T(8,128)(2,1)S(1)}, u32[]{:S(2)}) copy-start(bf16[8,16,4096]{2,1,0:T(8,128)(2,1)S(1)} %get-tuple-element.16.top) | copy-start | bytes 3145732
  3.5 24.9 %collective-permute-start.2 = (bf16[8,16,4096]{2,1,0:T(8,128)(2,1)S(1)}, bf16[8,16,4096]{2,1,0:T(8,128)(2,1)}, u32[]{:S(2)}, u32[]{:S(2)}) collective-permute-start(bf16[8,16,4096]{2,1,0:T(8,128)(2,1)S(1)} %get-tuple-element.18.bottom), channel_id=1, source_target_pairs={{0,1},{1,2},{2,3},{4,5},{5,6},{6,7},{8,9},{9,10},{10,11},{12,13},{... | collective-permute-start | bytes 3145736 | tf_op jit(solution)/shard_map/ppermute | solution.py:391
  7.7 25.8 %collective-permute-start.3 = (bf16[8,16,4096]{2,1,0:T(8,128)(2,1)S(1)}, bf16[8,16,4096]{2,1,0:T(8,128)(2,1)}, u32[]{:S(2)}, u32[]{:S(2)}) collective-permute-start(bf16[8,16,4096]{2,1,0:T(8,128)(2,1)S(1)} %get-tuple-element.15.top), channel_id=1, source_target_pairs={{1,0},{2,1},{3,2},{5,4},{6,5},{7,6},{9,8},{10,9},{11,10},{13,12},{... | collective-permute-start | bytes 3145736 | tf_op jit(solution)/shard_map/ppermute | solution.py:392
  41.9 52.2 %all-to-all-start.1 = ((bf16[64,8,1536]{2,1,0:T(8,128)(2,1)}), bf16[64,8,1536]{2,1,0:T(8,128)(2,1)S(1)}, u32[]{:S(2)}, u32[]{:S(2)}) async-start(bf16[64,8,1536]{2,1,0:T(8,128)(2,1)} %smooth.3), calls=%async_computation.1 | async-start | bytes 3145728 | tf_op jit(solution)/shard_map/all_to_all | solution.py:399
  55.1 24.6 %collective-permute-start = (bf16[8,16,4096]{2,1,0:T(8,128)(2,1)}, bf16[8,16,4096]{2,1,0:T(8,128)(2,1)S(1)}, u32[]{:S(2)}, u32[]{:S(2)}) collective-permute-start(bf16[8,16,4096]{2,1,0:T(8,128)(2,1)} %get-tuple-element.17.bottom), channel_id=1, source_target_pairs={{0,1},{1,2},{2,3},{4,5},{5,6},{6,7},{8,9},{9,10},{10,11},{12,13},{... | collective-permute-start | bytes 3145736 | tf_op jit(solution)/shard_map/ppermute | solution.py:391
  57.3 25.9 %collective-permute-start.1 = (bf16[8,16,4096]{2,1,0:T(8,128)(2,1)S(1)}, bf16[8,16,4096]{2,1,0:T(8,128)(2,1)S(1)}, u32[]{:S(2)}, u32[]{:S(2)}) collective-permute-start(bf16[8,16,4096]{2,1,0:T(8,128)(2,1)S(1)} %get-tuple-element.16.top), channel_id=1, source_target_pairs={{1,0},{2,1},{3,2},{5,4},{6,5},{7,6},{9,8},{10,9},{11,10},{13,12},{... | collective-permute-start | bytes 3145736 | tf_op jit(solution)/shard_map/ppermute | solution.py:392
  79.6 3.6 %copy-start.7 = (bf16[8,16,4096]{2,1,0:T(8,128)(2,1)}, bf16[8,16,4096]{2,1,0:T(8,128)(2,1)S(1)}, u32[]{:S(2)}) copy-start(bf16[8,16,4096]{2,1,0:T(8,128)(2,1)S(1)} %collective-permute-done.before) | copy-start | bytes 3145732
  83.2 1.0 copy-start.8
  94.1 1.1 copy-start
  95.2 49.2 %all-to-all-start = ((bf16[64,8,1536]{2,1,0:T(8,128)(2,1)}), bf16[64,8,1536]{2,1,0:T(8,128)(2,1)}, u32[]{:S(2)}, u32[]{:S(2)}) async-start(bf16[64,8,1536]{2,1,0:T(8,128)(2,1)} %smooth.2), calls=%async_computation | async-start | bytes 3145728 | tf_op jit(solution)/shard_map/all_to_all | solution.py:399
  153.0 3.4 %collective-permute-start.4 = (f32[4,640,128]{2,1,0:T(8,128)}, f32[4,640,128]{2,1,0:T(8,128)S(1)}, u32[]{:S(2)}, u32[]{:S(2)}) collective-permute-start(f32[4,640,128]{2,1,0:T(8,128)} %get-tuple-element.14), channel_id=1, source_target_pairs={{0,4},{4,0},{1,5},{5,1},{2,6},{6,2},{3,7},{7,3},{8,12},{12,8},{9,1... | collective-permute-start | bytes 3932168 | tf_op jit(solution)/shard_map/ppermute | solution.py:262
  215.9 21.4 %copy-start.5 = (s32[1024,16]{0,1:T(8,128)S(1)}, s32[1024,16]{0,1:T(8,128)}, u32[]{:S(2)}) copy-start(s32[1024,16]{0,1:T(8,128)} %param.7) | copy-start | bytes 196612
  233.4 6.8 %copy-start.1 = (f32[4,640,128]{2,1,0:T(8,128)}, f32[4,640,128]{2,1,0:T(8,128)S(1)}, u32[]{:S(2)}) copy-start(f32[4,640,128]{2,1,0:T(8,128)S(1)} %all_to_all.33.near_ref) | copy-start | bytes 3932164
  233.4 6.8 %collective-permute-start.5 = (f32[4,640,128]{2,1,0:T(8,128)S(1)}, f32[4,640,128]{2,1,0:T(8,128)}, u32[]{:S(2)}, u32[]{:S(2)}) collective-permute-start(f32[4,640,128]{2,1,0:T(8,128)S(1)} %all_to_all.33.near_ref), channel_id=1, source_target_pairs={{0,4},{4,0},{1,5},{5,1},{2,6},{6,2},{3,7},{7,3},{8,12},{12,8},{9,1... | collective-permute-start | bytes 3932168 | tf_op jit(solution)/shard_map/ppermute | solution.py:269

commit v3 on v2

--- a/solution.py
+++ b/solution.py
@@ -4,6 +4,7 @@
 from jax.experimental import pallas as pl
 from jax.experimental.pallas import tpu as pltpu
 from jax.sharding import Mesh, PartitionSpec as P
+
 
 ITERS = 8
 F32 = jnp.float32
@@ -206,23 +207,21 @@
 
 
 def cov_kernel(core_ref, part0, part1, keep_ref, send_ref, data_ref, sems):
-    for copy in load_parts((part0, part1), data_ref, sems):
+    for copy in load_parts((part0, part1, part0), data_ref, sems):
         copy.wait()
     core = core_ref[0]
 
     def fill(out_ref, first):
-        def step(i, carry):
-            block = first + i
-            left = data_ref[pl.ds(pl.multiple_of(block * 128, 128), 128), :]
-            for d in range(5):
-                other = lax.rem(block + d, 8)
-                right = data_ref[pl.ds(pl.multiple_of(other * 128, 128), 128), :]
-                out_ref[i, d * 128 : d * 128 + 128, :] = lax.dot_general(
-                    left, right, NT, preferred_element_type=F32
-                )
-            return carry
-
-        lax.fori_loop(0, 4, step, 0)
+        for unit in range(2):
+            start = pl.multiple_of((first + 2 * unit) * 128, 256)
+            wide = lax.dot_general(
+                data_ref[pl.ds(start, 768), :],
+                data_ref[pl.ds(start, 256), :],
+                NT,
+                preferred_element_type=F32,
+            ).astype(out_ref.dtype)
+            out_ref[2 * unit] = wide[0:640, 0:128]
+            out_ref[2 * unit + 1] = wide[128:768, 128:256]
 
     fill(keep_ref, core * 4)
     fill(send_ref, (1 - core) * 4)
@@ -233,16 +232,18 @@
 
 
 def local_covariance(core, parts):
-    shape = jax.ShapeDtypeStruct((4, 640, 128), F32)
     rows = sum(part.shape[0] for part in parts)
     return pl.pallas_call(
         cov_kernel,
-        out_shape=(shape, shape),
+        out_shape=(
+            jax.ShapeDtypeStruct((4, 640, 128), F32),
+            jax.ShapeDtypeStruct((4, 640, 128), BF16),
+        ),
         in_specs=[smem(), anywhere(), anywhere()],
         out_specs=(vmem(), vmem()),
         scratch_shapes=[
-            pltpu.VMEM((rows, parts[0].shape[1]), BF16),
-            pltpu.SemaphoreType.DMA((2,)),
+            pltpu.VMEM((rows + parts[0].shape[0], parts[0].shape[1]), BF16),
+            pltpu.SemaphoreType.DMA((3,)),
         ],
         compiler_params=pltpu.CompilerParams(vmem_limit_bytes=VMEM_LIMIT),
         cost_estimate=pl.CostEstimate(
@@ -259,11 +260,11 @@
 
 def reduce_all(keep, send):
     swap = [(0, 1), (1, 0)]
-    half = keep + lax.ppermute(send, "core", swap)
+    half = (keep + lax.ppermute(send, "core", swap).astype(F32)).astype(BF16)
     got = lax.all_to_all(half.reshape(4, 640, 128), "sky", 0, 0, tiled=True)
-    quarter = jnp.sum(got, axis=0)
+    quarter = jnp.sum(got.astype(F32), axis=0).astype(BF16)
     got = lax.all_to_all(quarter.reshape(32, 20, 128), ("y", "z"), 0, 0, tiled=True)
-    mine = jnp.sum(got, axis=0)
+    mine = jnp.sum(got.astype(F32), axis=0)
     quarter = everywhere(mine, ("y", "z"), 32).reshape(640, 128)
     half = everywhere(quarter, "sky", 4).reshape(4, 640, 128)
     other = lax.ppermute(half, "core", swap)
@@ -291,7 +292,7 @@
 ):
     core = core_ref[0]
     copies = load_parts((part0, part1), data_ref, sems)
-    modes = seed_ref.shape[0]
+    modes = seed_ref.shape[0] // 3
     count = seed_ref.shape[1]
     pixels = data_ref.shape[1]
     scale = 1.0 / (256 * pixels)
@@ -302,12 +303,12 @@
             block = jnp.where(core == i // 4, near, far) * scale
             j = (i + d) % 8
             hi, mid = split2(block)
-            cov_ref[i * 128 : i * 128 + 128, j * 128 : j * 128 + 128] = hi
-            cov_ref[i * 128 : i * 128 + 128, count + j * 128 : count + j * 128 + 128] = mid
+            cov_ref[j * 128 : j * 128 + 128, i * 128 : i * 128 + 128] = hi
+            cov_ref[j * 128 : j * 128 + 128, count + i * 128 : count + i * 128 + 128] = mid
             if d in (1, 2, 3):
                 hi, mid = split2(block.T)
-                cov_ref[j * 128 : j * 128 + 128, i * 128 : i * 128 + 128] = hi
-                cov_ref[j * 128 : j * 128 + 128, count + i * 128 : count + i * 128 + 128] = mid
+                cov_ref[i * 128 : i * 128 + 128, j * 128 : j * 128 + 128] = hi
+                cov_ref[i * 128 : i * 128 + 128, count + j * 128 : count + j * 128 + 128] = mid
 
     def fold(x):
         return x[0:modes] + x[modes : 2 * modes] + x[2 * modes : 3 * modes]
@@ -326,7 +327,7 @@
     def exact_dot(a, b):
         return lax.dot(a, b, precision=lax.Precision.HIGHEST, preferred_element_type=F32)
 
-    images = times_cov(stack(seed_ref[...].astype(F32)))
+    images = times_cov(seed_ref[...])
 
     def sweep(step, images):
         parts = stack(images)
@@ -355,8 +356,24 @@
         out_ref[first : first + 16, chunk * 8 : chunk * 8 + 8, :] = value.reshape(16, 8, pixels)
 
 
+def seeds_kernel(seed_ref, out_ref):
+    out_ref[...] = jnp.concatenate(split3(seed_ref[...].astype(F32)), axis=0)
+
+
+def split_seed(seed):
+    modes, count = seed.shape
+    return pl.pallas_call(
+        seeds_kernel,
+        out_shape=jax.ShapeDtypeStruct((3 * modes, count), BF16),
+        in_specs=[vmem()],
+        out_specs=vmem(),
+        name="seeds",
+    )(seed)
+
+
 def clean(core, near, far, seed, parts):
     modes, count = seed.shape
+    modes = modes // 3
     pixels = parts[0].shape[1]
     return pl.pallas_call(
         clean_kernel,
@@ -379,15 +396,17 @@
 
 
 def body(sky_maps, beam_index, beam_taps, start_seed):
-    channels, strip_rows, columns = sky_maps.shape
+    channels, strip_rows, _ = sky_maps.shape
     modes = start_seed.shape[1]
     core = lax.axis_index("core").astype(jnp.int32).reshape(1)
     col, row, order = prepare(beam_index, beam_taps, CHUNK)
     halos = []
     for first in range(0, channels, CHUNK):
-        strip = sky_maps[first : first + CHUNK]
+        strip = sky_maps if first == 0 else lax.optimization_barrier(sky_maps)
+        strip = strip[first : first + CHUNK]
         top = strip[:, 0:16, :]
         bottom = strip[:, strip_rows - 16 : strip_rows, :]
+        k = first // CHUNK
         before = lax.ppermute(bottom, "sky", [(i, i + 1) for i in range(3)])
         after = lax.ppermute(top, "sky", [(i + 1, i) for i in range(3)])
         halos.append((before, top, bottom, after))
@@ -400,6 +419,7 @@
         parts.append(data.reshape(64 * CHUNK, 1536))
     seed = start_seed.T.reshape(modes, 64, channels // CHUNK, CHUNK)
     seed = seed.transpose(0, 2, 1, 3).reshape(modes, 64 * channels)
+    seed = split_seed(seed)
     keep, send = local_covariance(core, parts)
     near, far = reduce_all(keep, send)
     cleaned = clean(core, near, far, seed, parts)
@@ -409,6 +429,7 @@
 def solution(mesh):
     fine = Mesh(mesh.devices.reshape(4, 8, 2, 4), ("y", "z", "core", "sky"))
     freq = ("y", "z", "core")
+
     return jax.shard_map(
         body,
         mesh=fine,

time: 263 us -> 245 us (0.932)
  blocking collectives: 75.1 us -> 63.4 us
  waiting for transfers between devices: 87.8 us -> 77.4 us
  starting transfers between devices: 36.8 us -> 42.7 us
    ppermute x2, waiting for transfers between devices: 34.4 us -> 1.69 us  [body(): before = lax.ppermute(bottom, 'sky', [(i, i + 1) for i in range(3)])]
    ppermute x2, waiting for transfers between devices: 8.51 us -> 34.6 us  [body(): after = lax.ppermute(top, 'sky', [(i + 1, i) for i in range(3)])]
    all_to_all x1, blocking collectives: 19.9 us -> 15.2 us  [reduce_all(): got = lax.all_to_all(half.reshape(4, 640, 128), 'sky', 0, 0, tiled=True)]
    all_to_all x1, blocking collectives: 19.4 us -> 15.6 us  [reduce_all(): lax.all_to_all(quarter.reshape(32, 20, 128), ('y', 'z'), 0, 0, tiled=True)]
    ppermute x2, starting transfers between devices: 6.31 us -> 9.91 us  [body(): before = lax.ppermute(bottom, 'sky', [(i, i + 1) for i in range(3)])]
    all_to_all x2, blocking collectives: 35.8 us -> 32.6 us  [everywhere(): return lax.all_to_all(copies, axes, 0, 0, tiled=True)]
    pallas_call x1 -> x2, Pallas kernels: 8.68 us -> 7.37 us  [the longest x1 5.87 us: local_covariance(): pl.pallas_call(cov_kernel, out_shape=(jax.ShapeDtypeStruct((4, 640, 128),...]
  transfers between devices with their start and end apart: 8 -> 8, of which waited for: 8 -> 7; matrix products, arithmetic and copies ran while one was open for 1% -> 2% of each run, Pallas kernels for 5% -> 6%
where the time goes in v3:
time: 245 us; the launch traced here: 244 us
  waiting for transfers between devices  77.4 us (32%)
  blocking collectives  63.4 us (26%)
  Pallas kernels  49.9 us (20%)
  starting transfers between devices  42.7 us (17%)
  local copies, waits for them, and re-layouts  9.17 us (4%)
    all_to_all x2, waiting for transfers between devices, body(): data = lax.all_to_all(pieces, ('y', 'z', 'core'), 0, 0, tiled=True)  39 us
    ppermute x2, waiting for transfers between devices, body(): after = lax.ppermute(top, 'sky', [(i + 1, i) for i in range(3)])  34.6 us
    all_to_all x2, blocking collectives, everywhere(): return lax.all_to_all(copies, axes, 0, 0, tiled=True)  32.6 us
    all_to_all x2, starting transfers between devices, body(): data = lax.all_to_all(pieces, ('y', 'z', 'core'), 0, 0, tiled=True)  24.7 us
    pallas_call x1, Pallas kernels, clean(): pl.pallas_call(clean_kernel, out_shape=jax.ShapeDtypeStruct((count // 16,...  22 us
    pallas_call x2, Pallas kernels, smooth(): pl.pallas_call(smooth_kernel, grid=(channels // 4,), out_shape=jax.ShapeD...  16.9 us
    all_to_all x1, blocking collectives, reduce_all(): lax.all_to_all(quarter.reshape(32, 20, 128), ('y', 'z'), 0, 0, tiled=True)  15.6 us
    all_to_all x1, blocking collectives, reduce_all(): got = lax.all_to_all(half.reshape(4, 640, 128), 'sky', 0, 0, tiled=True)  15.2 us
  transfers between devices with their start and end apart: 8, of which 7 were waited for; matrix products, arithmetic and copies ran while one was open for 2% of the time, Pallas kernels for 6%

profile of v3, /device:TPU:33, one launch (start us, length us, event | category | flops | bytes accessed | tf_op | source)
XLA Modules:
  0.0 244.5 jit_solution(8023267745537034697)
XLA Ops:
  0.0 1.7 fusion
  1.7 1.3 collective-permute-start.3
  3.0 5.0 %collective-permute-start.2 = (bf16[8,16,4096]{2,1,0:T(8,128)(2,1)S(1)}, bf16[8,16,4096]{2,1,0:T(8,128)(2,1)}, u32[]{:S(2)}, u32[]{:S(2)}) collective-permute-start(bf16[8,16,4096]{2,1,0:T(8,128)(2,1)S(1)} %get-tuple-element.16.bottom), channel_id=1, source_target_pairs={{0,1},{1,2},{2,3},{4,5},{5,6},{6,7},{8,9},{9,10},{10,11},{12,13},{... | collective-permute-start | bytes 3145736 | tf_op jit(solution)/shard_map/ppermute | solution.py:410
  8.0 3.6 %prep.1 = (bf16[8,256,256]{2,1,0:T(8,128)(2,1)}, bf16[4,384,256]{2,1,0:T(8,128)(2,1)}, bf16[192,256]{1,0:T(8,128)(2,1)}) custom-call(s32[16]{0:T(128)} %index_ref.1, f32[8,31]{1,0:T(8,128)} %taps_ref.1), custom_call_target="tpu_custom_call" | custom-call | flops 1000000 | bytes 2000000 | tf_op jit(solution)/shard_map/prep/pallas_call | solution.py:77
  11.6 0.7 fusion.3
  12.3 2.1 fusion.2
  14.3 13.3 %collective-permute-done.3.after = bf16[8,16,4096]{2,1,0:T(8,128)(2,1)S(1)} collective-permute-done((bf16[8,16,4096]{2,1,0:T(8,128)(2,1)S(1)}, bf16[8,16,4096]{2,1,0:T(8,128)(2,1)S(1)}, u32[]{:S(2)}, u32[]{:S(2)}) %collective-permute-start.3) | collective-permute-done | bytes 1048608 | tf_op jit(solution)/shard_map/ppermute | solution.py:411
  27.7 0.9 collective-permute-done.2.before
  28.7 8.4 %smooth.3 = bf16[64,8,1536]{2,1,0:T(8,128)(2,1)} custom-call(s32[8]{0:T(128)} %get-tuple-element.21.index_ref, bf16[8,16,4096]{2,1,0:T(8,128)(2,1)} %collective-permute-done.2.before, bf16[8,16,4096]{2,1,0:T(8,128)(2,1)} %copy-done.3, bf16[8,16,4096]{2,1,0:T(8,128)(2,1)} %copy-done.4, bf16[8,16,4096]{2,1,0:T(8,128)(2,1)} %copy-done.9, ...), custom_call_target="tpu_custom_call" | custom-call | flops 4000000000 | bytes 8000000 | tf_op jit(solution)/shard_map/smooth/pallas_call | solution.py:171
  37.1 13.5 %all-to-all-start.1 = ((bf16[64,8,1536]{2,1,0:T(8,128)(2,1)}), bf16[64,8,1536]{2,1,0:T(8,128)(2,1)}, u32[]{:S(2)}, u32[]{:S(2)}) async-start(bf16[64,8,1536]{2,1,0:T(8,128)(2,1)} %smooth.3), calls=%async_computation.1 | async-start | bytes 3145728 | tf_op jit(solution)/shard_map/all_to_all | solution.py:418
  50.9 1.0 copy-done.5
  51.9 1.3 collective-permute-start.1
  53.2 4.9 %collective-permute-start = (bf16[8,16,4096]{2,1,0:T(8,128)(2,1)S(1)}, bf16[8,16,4096]{2,1,0:T(8,128)(2,1)S(1)}, u32[]{:S(2)}, u32[]{:S(2)}) collective-permute-start(bf16[8,16,4096]{2,1,0:T(8,128)(2,1)S(1)} %get-tuple-element.18.bottom), channel_id=1, source_target_pairs={{0,1},{1,2},{2,3},{4,5},{5,6},{6,7},{8,9},{9,10},{10,11},{12,13},{... | collective-permute-start | bytes 3145736 | tf_op jit(solution)/shard_map/ppermute | solution.py:410
  58.1 21.2 %collective-permute-done.1.after = bf16[8,16,4096]{2,1,0:T(8,128)(2,1)S(1)} collective-permute-done((bf16[8,16,4096]{2,1,0:T(8,128)(2,1)S(1)}, bf16[8,16,4096]{2,1,0:T(8,128)(2,1)S(1)}, u32[]{:S(2)}, u32[]{:S(2)}) %collective-permute-start.1) | collective-permute-done | bytes 1048608 | tf_op jit(solution)/shard_map/ppermute | solution.py:411
  79.4 0.8 collective-permute-done.before
  80.4 0.7 copy-done.11
  81.2 8.4 %smooth.2 = bf16[64,8,1536]{2,1,0:T(8,128)(2,1)} custom-call(s32[8]{0:T(128)} %get-tuple-element.22.index_ref, bf16[8,16,4096]{2,1,0:T(8,128)(2,1)} %copy-done.11, bf16[8,16,4096]{2,1,0:T(8,128)(2,1)} %copy-done.5, bf16[8,16,4096]{2,1,0:T(8,128)(2,1)} %copy-done.6, bf16[8,16,4096]{2,1,0:T(8,128)(2,1)} %copy-done.10, ...), custom_call_target="tpu_custom_call" | custom-call | flops 4000000000 | bytes 8000000 | tf_op jit(solution)/shard_map/smooth/pallas_call | solution.py:171
  89.6 11.2 %all-to-all-start = ((bf16[64,8,1536]{2,1,0:T(8,128)(2,1)}), bf16[64,8,1536]{2,1,0:T(8,128)(2,1)S(1)}, u32[]{:S(2)}, u32[]{:S(2)}) async-start(bf16[64,8,1536]{2,1,0:T(8,128)(2,1)} %smooth.2), calls=%async_computation | async-start | bytes 3145728 | tf_op jit(solution)/shard_map/all_to_all | solution.py:418
  100.8 39.0 %all-to-all-done = bf16[64,8,1536]{2,1,0:T(8,128)(2,1)S(1)} async-done(((bf16[64,8,1536]{2,1,0:T(8,128)(2,1)}), bf16[64,8,1536]{2,1,0:T(8,128)(2,1)S(1)}, u32[]{:S(2)}, u32[]{:S(2)}) %all-to-all-start) | async-done | bytes 1572896 | tf_op jit(solution)/shard_map/all_to_all | solution.py:418
  139.8 1.1 copy-done.1
  140.9 5.9 %cov.1 = (f32[4,640,128]{2,1,0:T(8,128)}, bf16[4,640,128]{2,1,0:T(8,128)(2,1)}) custom-call(s32[1]{0:T(128)} %bitcast.core_ref, bf16[512,1536]{1,0:T(8,128)(2,1)} %bitcast.11, bf16[512,1536]{1,0:T(8,128)(2,1)} %bitcast.2.part1), custom_call_target="tpu_custom_call" | custom-call | flops 2000000000 | bytes 6000000 | tf_op jit(solution)/shard_map/cov/pallas_call | solution.py:236
  146.8 0.6 collective-permute-start.4
  147.4 1.9 collective-permute-done.4
  149.4 1.5 add_convert_fusion
  150.8 15.2 %all_to_all.30 = bf16[4,640,128]{2,1,0:T(8,128)(2,1)S(1)} all-to-all(bf16[4,640,128]{2,1,0:T(8,128)(2,1)S(1)} %add_convert_fusion), channel_id=1, replica_groups=mesh['y'=4,'z'=8,'core'=2,'sky'=4] {'sky'}, dimensions={0} | all-to-all | bytes 1310720 | tf_op jit(solution)/shard_map/all_to_all | solution.py:264
  166.2 15.6 %all_to_all.31 = bf16[32,20,128]{2,1,0:T(8,128)(2,1)S(1)} all-to-all(bf16[32,20,128]{2,1,0:T(8,128)(2,1)S(1)} %reshape.26), channel_id=1, replica_groups=mesh['y'=4,'z'=8,'core'=2,'sky'=4] {'y','z'}, dimensions={0} | all-to-all | bytes 327680 | tf_op jit(solution)/shard_map/all_to_all | solution.py:266
  181.9 16.0 %all_to_all.32 = f32[32,20,128]{2,1,0:T(8,128)S(1)} all-to-all(f32[32,20,128]{2,1,0:T(8,128)S(1)} %broadcast_in_dim.6), channel_id=1, replica_groups=mesh['y'=4,'z'=8,'core'=2,'sky'=4] {'y','z'}, dimensions={0} | all-to-all | bytes 655360 | tf_op jit(solution)/shard_map/all_to_all | solution.py:258
  198.0 16.6 %all_to_all.33.near_ref = f32[4,640,128]{2,1,0:T(8,128)S(1)} all-to-all(f32[4,640,128]{2,1,0:T(8,128)S(1)} %broadcast_in_dim.15), channel_id=1, replica_groups=mesh['y'=4,'z'=8,'core'=2,'sky'=4] {'sky'}, dimensions={0} | all-to-all | bytes 2621440 | tf_op jit(solution)/shard_map/all_to_all | solution.py:258
  214.6 4.8 %collective-permute-start.5 = (f32[4,640,128]{2,1,0:T(8,128)S(1)}, f32[4,640,128]{2,1,0:T(8,128)}, u32[]{:S(2)}, u32[]{:S(2)}) collective-permute-start(f32[4,640,128]{2,1,0:T(8,128)S(1)} %all_to_all.33.near_ref), channel_id=1, source_target_pairs={{0,4},{4,0},{1,5},{5,1},{2,6},{6,2},{3,7},{7,3},{8,12},{12,8},{9,1... | collective-permute-start | bytes 3932168 | tf_op jit(solution)/shard_map/ppermute | solution.py:270
  219.7 0.8 copy.8.seed_ref
  220.5 1.5 seeds.1.seed_ref
  222.3 22.0 %clean.1 = bf16[64,16,1536]{2,1,0:T(8,128)(2,1)} custom-call(s32[1]{0:T(128)} %bitcast.core_ref, f32[4,640,128]{2,1,0:T(8,128)} %copy-done.2, f32[4,640,128]{2,1,0:T(8,128)} %collective-permute-done.5.far_ref, bf16[48,1024]{1,0:T(8,128)(2,1)} %seeds.1.seed_ref, bf16[512,1536]{1,0:T(8,128)(2,1)} %bitcast.12, bf16[512,1536]{1,0:T(8,128)(2,1)} %bitcast.2.part1), custom_call_target="tpu_custom_call" | custom-call | flops 3000000000 | bytes 12000000 | tf_op jit(solution)/shard_map/clean/pallas_call | solution.py:378
  (32 shorter events, 1.5 us)
Async XLA Ops:
  0.0 11.6 %copy-start.8 = (s32[16]{0:T(128)S(1)}, s32[16]{0:T(128)}, u32[]{:S(2)}) copy-start(s32[16]{0:T(128)} %index_ref.1) | copy-start | bytes 196
  1.7 26.9 %copy-start.3 = (bf16[8,16,4096]{2,1,0:T(8,128)(2,1)}, bf16[8,16,4096]{2,1,0:T(8,128)(2,1)S(1)}, u32[]{:S(2)}) copy-start(bf16[8,16,4096]{2,1,0:T(8,128)(2,1)S(1)} %get-tuple-element.15.top) | copy-start | bytes 3145732
  1.7 26.9 %copy-start.4 = (bf16[8,16,4096]{2,1,0:T(8,128)(2,1)}, bf16[8,16,4096]{2,1,0:T(8,128)(2,1)S(1)}, u32[]{:S(2)}) copy-start(bf16[8,16,4096]{2,1,0:T(8,128)(2,1)S(1)} %get-tuple-element.16.bottom) | copy-start | bytes 3145732
  1.7 25.9 %collective-permute-start.3 = (bf16[8,16,4096]{2,1,0:T(8,128)(2,1)S(1)}, bf16[8,16,4096]{2,1,0:T(8,128)(2,1)S(1)}, u32[]{:S(2)}, u32[]{:S(2)}) collective-permute-start(bf16[8,16,4096]{2,1,0:T(8,128)(2,1)S(1)} %get-tuple-element.15.top), channel_id=1, source_target_pairs={{1,0},{2,1},{3,2},{5,4},{6,5},{7,6},{9,8},{10,9},{11,10},{13,12},{... | collective-permute-start | bytes 3145736 | tf_op jit(solution)/shard_map/ppermute | solution.py:411
  3.0 25.5 %collective-permute-start.2 = (bf16[8,16,4096]{2,1,0:T(8,128)(2,1)S(1)}, bf16[8,16,4096]{2,1,0:T(8,128)(2,1)}, u32[]{:S(2)}, u32[]{:S(2)}) collective-permute-start(bf16[8,16,4096]{2,1,0:T(8,128)(2,1)S(1)} %get-tuple-element.16.bottom), channel_id=1, source_target_pairs={{0,1},{1,2},{2,3},{4,5},{5,6},{6,7},{8,9},{9,10},{10,11},{12,13},{... | collective-permute-start | bytes 3145736 | tf_op jit(solution)/shard_map/ppermute | solution.py:410
  27.7 1.0 copy-start.9
  37.1 13.5 %copy-start = (bf16[16,24,4096]{2,1,0:T(8,128)(2,1)S(1)}, bf16[16,24,4096]{2,1,0:T(8,128)(2,1)}, u32[]{:S(2)}) copy-start(bf16[16,24,4096]{2,1,0:T(8,128)(2,1)} %param.4) | copy-start | bytes 9437188
  37.1 52.5 %all-to-all-start.1 = ((bf16[64,8,1536]{2,1,0:T(8,128)(2,1)}), bf16[64,8,1536]{2,1,0:T(8,128)(2,1)}, u32[]{:S(2)}, u32[]{:S(2)}) async-start(bf16[64,8,1536]{2,1,0:T(8,128)(2,1)} %smooth.3), calls=%async_computation.1 | async-start | bytes 3145728 | tf_op jit(solution)/shard_map/all_to_all | solution.py:418
  50.9 1.0 copy-start.5
  50.9 28.5 %copy-start.6 = (bf16[8,16,4096]{2,1,0:T(8,128)(2,1)}, bf16[8,16,4096]{2,1,0:T(8,128)(2,1)S(1)}, u32[]{:S(2)}) copy-start(bf16[8,16,4096]{2,1,0:T(8,128)(2,1)S(1)} %get-tuple-element.18.bottom) | copy-start | bytes 3145732
  51.9 27.5 %collective-permute-start.1 = (bf16[8,16,4096]{2,1,0:T(8,128)(2,1)S(1)}, bf16[8,16,4096]{2,1,0:T(8,128)(2,1)S(1)}, u32[]{:S(2)}, u32[]{:S(2)}) collective-permute-start(bf16[8,16,4096]{2,1,0:T(8,128)(2,1)S(1)} %get-tuple-element.17.top), channel_id=1, source_target_pairs={{1,0},{2,1},{3,2},{5,4},{6,5},{7,6},{9,8},{10,9},{11,10},{13,12},{... | collective-permute-start | bytes 3145736 | tf_op jit(solution)/shard_map/ppermute | solution.py:411
  53.2 27.0 %collective-permute-start = (bf16[8,16,4096]{2,1,0:T(8,128)(2,1)S(1)}, bf16[8,16,4096]{2,1,0:T(8,128)(2,1)S(1)}, u32[]{:S(2)}, u32[]{:S(2)}) collective-permute-start(bf16[8,16,4096]{2,1,0:T(8,128)(2,1)S(1)} %get-tuple-element.18.bottom), channel_id=1, source_target_pairs={{0,1},{1,2},{2,3},{4,5},{5,6},{6,7},{8,9},{9,10},{10,11},{12,13},{... | collective-permute-start | bytes 3145736 | tf_op jit(solution)/shard_map/ppermute | solution.py:410
  79.4 1.1 copy-start.10
  80.2 1.0 copy-start.11
  89.6 50.2 %all-to-all-start = ((bf16[64,8,1536]{2,1,0:T(8,128)(2,1)}), bf16[64,8,1536]{2,1,0:T(8,128)(2,1)S(1)}, u32[]{:S(2)}, u32[]{:S(2)}) async-start(bf16[64,8,1536]{2,1,0:T(8,128)(2,1)} %smooth.2), calls=%async_computation | async-start | bytes 3145728 | tf_op jit(solution)/shard_map/all_to_all | solution.py:418
  139.8 1.1 copy-start.1
  146.8 2.6 %collective-permute-start.4 = (bf16[4,640,128]{2,1,0:T(8,128)(2,1)}, bf16[4,640,128]{2,1,0:T(8,128)(2,1)S(1)}, u32[]{:S(2)}, u32[]{:S(2)}) collective-permute-start(bf16[4,640,128]{2,1,0:T(8,128)(2,1)} %get-tuple-element.14), channel_id=1, source_target_pairs={{0,4},{4,0},{1,5},{5,1},{2,6},{6,2},{3,7},{7,3},{8,12},{12,8},{9,1... | collective-permute-start | bytes 1966088 | tf_op jit(solution)/shard_map/ppermute | solution.py:263
  198.0 21.4 %copy-start.7 = (s32[1024,16]{0,1:T(8,128)S(1)}, s32[1024,16]{0,1:T(8,128)}, u32[]{:S(2)}) copy-start(s32[1024,16]{0,1:T(8,128)} %param.7) | copy-start | bytes 196612
  214.6 7.6 %copy-start.2 = (f32[4,640,128]{2,1,0:T(8,128)}, f32[4,640,128]{2,1,0:T(8,128)S(1)}, u32[]{:S(2)}) copy-start(f32[4,640,128]{2,1,0:T(8,128)S(1)} %all_to_all.33.near_ref) | copy-start | bytes 3932164
  214.6 7.6 %collective-permute-start.5 = (f32[4,640,128]{2,1,0:T(8,128)S(1)}, f32[4,640,128]{2,1,0:T(8,128)}, u32[]{:S(2)}, u32[]{:S(2)}) collective-permute-start(f32[4,640,128]{2,1,0:T(8,128)S(1)} %all_to_all.33.near_ref), channel_id=1, source_target_pairs={{0,4},{4,0},{1,5},{5,1},{2,6},{6,2},{3,7},{7,3},{8,12},{12,8},{9,1... | collective-permute-start | bytes 3932168 | tf_op jit(solution)/shard_map/ppermute | solution.py:270

commit v4 on v3

--- a/solution.py
+++ b/solution.py
@@ -271,20 +271,34 @@
     return half, other
 
 
-def inverse_factor(gram):
+def start_factor(gram):
     size = gram.shape[0]
     row = lax.broadcasted_iota(jnp.int32, (size, 128), 0)
     lane = lax.broadcasted_iota(jnp.int32, (size, 128), 1)
-    unit = jnp.where(lane == row + size, 1.0, 0.0).astype(F32)
-    work = jnp.concatenate([gram, jnp.zeros((size, 128 - size), F32)], axis=1) + unit
-    for j in range(size):
-        column = work[:, j : j + 1]
-        factor = jnp.where(row[:, 0:1] > j, column, 0.0) * (1.0 / work[j : j + 1, j : j + 1])
-        work = work - factor * work[j : j + 1, :]
-    pivot = jnp.sum(jnp.where(lane == row, work, 0.0), axis=1, keepdims=True)
+    unit = jnp.where(lane == row, 1.0, 0.0).astype(F32)
+    columns = [jnp.broadcast_to(gram[:, j : j + 1], (size, 128)) for j in range(size)]
+    return columns + [unit, jnp.ones((size, 128), F32)]
+
+
+def eliminate(work, j):
+    size = len(work) - 2
+    shape = work[0].shape
+    row = lax.broadcasted_iota(jnp.int32, shape, 0)
+    pivot = jnp.broadcast_to(work[j][j : j + 1, :], shape)
+    factor = jnp.where(row > j, work[j], 0.0) * (1.0 / pivot)
+    new = list(work)
+    for k in list(range(j + 1, size)) + [size]:
+        new[k] = work[k] - factor * jnp.broadcast_to(work[k][j : j + 1, :], shape)
+    new[size + 1] = jnp.where(row == j, pivot, work[size + 1])
+    return new
+
+
+def end_factor(work):
+    inverse, pivot = work[-2], work[-1]
+    size = inverse.shape[0]
     scale = lax.rsqrt(pivot)
     scale = scale * (1.5 - 0.5 * pivot * scale * scale)
-    return (work * scale)[:, size : 2 * size]
+    return (inverse * scale)[:, 0:size]
 
 
 def clean_kernel(
@@ -303,12 +317,12 @@
             block = jnp.where(core == i // 4, near, far) * scale
             j = (i + d) % 8
             hi, mid = split2(block)
-            cov_ref[j * 128 : j * 128 + 128, i * 128 : i * 128 + 128] = hi
-            cov_ref[j * 128 : j * 128 + 128, count + i * 128 : count + i * 128 + 128] = mid
+            cov_ref[j * 128 : j * 128 + 128, i * 256 : i * 256 + 128] = hi
+            cov_ref[j * 128 : j * 128 + 128, i * 256 + 128 : i * 256 + 256] = mid
             if d in (1, 2, 3):
                 hi, mid = split2(block.T)
-                cov_ref[i * 128 : i * 128 + 128, j * 128 : j * 128 + 128] = hi
-                cov_ref[i * 128 : i * 128 + 128, count + j * 128 : count + j * 128 + 128] = mid
+                cov_ref[i * 128 : i * 128 + 128, j * 256 : j * 256 + 128] = hi
+                cov_ref[i * 128 : i * 128 + 128, j * 256 + 128 : j * 256 + 256] = mid
 
     def fold(x):
         return x[0:modes] + x[modes : 2 * modes] + x[2 * modes : 3 * modes]
@@ -316,9 +330,11 @@
     def stack(x):
         return jnp.concatenate(split3(x), axis=0)
 
-    def times_cov(parts):
-        wide = fold(jnp.dot(parts, cov_ref[...], preferred_element_type=F32))
-        return wide[:, 0:count] + wide[:, count : 2 * count]
+    def cov_block(parts, q):
+        wide = fold(
+            jnp.dot(parts, cov_ref[:, q * 256 : q * 256 + 256], preferred_element_type=F32)
+        )
+        return wide[:, 0:128] + wide[:, 128:256]
 
     def gram_of(parts):
         tall = fold(lax.dot_general(parts, parts, NT, preferred_element_type=F32))
@@ -327,15 +343,23 @@
     def exact_dot(a, b):
         return lax.dot(a, b, precision=lax.Precision.HIGHEST, preferred_element_type=F32)
 
-    images = times_cov(seed_ref[...])
+    seeds = seed_ref[...]
+    images = jnp.concatenate([cov_block(seeds, q) for q in range(8)], axis=1)
 
     def sweep(step, images):
         parts = stack(images)
-        inverse = inverse_factor(gram_of(parts))
-        return exact_dot(inverse, times_cov(parts))
+        work = start_factor(gram_of(parts))
+        blocks = []
+        for q in range(8):
+            blocks.append(cov_block(parts, q))
+            work = eliminate(eliminate(work, 2 * q), 2 * q + 1)
+        return exact_dot(end_factor(work), jnp.concatenate(blocks, axis=1))
 
     images = lax.fori_loop(0, ITERS - 1, sweep, images)
-    basis = exact_dot(inverse_factor(gram_of(stack(images))), images)
+    work = start_factor(gram_of(stack(images)))
+    for j in range(modes):
+        work = eliminate(work, j)
+    basis = exact_dot(end_factor(work), images)
     hi, mid, low = split3(basis)
     basis_ref[...] = jnp.concatenate([hi, hi, mid, mid, hi, low], axis=0)
     for copy in copies:

time: 245 us -> 238 us (0.971)
  Pallas kernels: 49.9 us -> 42.2 us
    pallas_call x1, Pallas kernels: 22 us -> 14.3 us  [clean(): pl.pallas_call(clean_kernel, out_shape=jax.ShapeDtypeStruct((count // 16,...]
where the time goes in v4:
time: 238 us; the launch traced here: 237 us
  waiting for transfers between devices  77.4 us (33%)
  blocking collectives  63.4 us (27%)
  starting transfers between devices  42.7 us (18%)
  Pallas kernels  42.2 us (18%)
  local copies, waits for them, and re-layouts  9.17 us (4%)
    all_to_all x2, waiting for transfers between devices, body(): data = lax.all_to_all(pieces, ('y', 'z', 'core'), 0, 0, tiled=True)  39 us
    ppermute x2, waiting for transfers between devices, body(): after = lax.ppermute(top, 'sky', [(i + 1, i) for i in range(3)])  34.6 us
    all_to_all x2, blocking collectives, everywhere(): return lax.all_to_all(copies, axes, 0, 0, tiled=True)  32.6 us
    all_to_all x2, starting transfers between devices, body(): data = lax.all_to_all(pieces, ('y', 'z', 'core'), 0, 0, tiled=True)  24.7 us
    pallas_call x2, Pallas kernels, smooth(): pl.pallas_call(smooth_kernel, grid=(channels // 4,), out_shape=jax.ShapeD...  16.9 us
    all_to_all x1, blocking collectives, reduce_all(): lax.all_to_all(quarter.reshape(32, 20, 128), ('y', 'z'), 0, 0, tiled=True)  15.6 us
    all_to_all x1, blocking collectives, reduce_all(): got = lax.all_to_all(half.reshape(4, 640, 128), 'sky', 0, 0, tiled=True)  15.2 us
    pallas_call x1, Pallas kernels, clean(): pl.pallas_call(clean_kernel, out_shape=jax.ShapeDtypeStruct((count // 16,...  14.3 us
  transfers between devices with their start and end apart: 8, of which 7 were waited for; matrix products, arithmetic and copies ran while one was open for 2% of the time, Pallas kernels for 6%

profile of v4, /device:TPU:33, one launch (start us, length us, event | category | flops | bytes accessed | tf_op | source)
XLA Modules:
  0.0 236.8 jit_solution(4268510170284165478)
XLA Ops:
  0.0 1.7 fusion
  1.7 1.3 collective-permute-start.3
  3.0 5.0 %collective-permute-start.2 = (bf16[8,16,4096]{2,1,0:T(8,128)(2,1)S(1)}, bf16[8,16,4096]{2,1,0:T(8,128)(2,1)}, u32[]{:S(2)}, u32[]{:S(2)}) collective-permute-start(bf16[8,16,4096]{2,1,0:T(8,128)(2,1)S(1)} %get-tuple-element.16.bottom), channel_id=1, source_target_pairs={{0,1},{1,2},{2,3},{4,5},{5,6},{6,7},{8,9},{9,10},{10,11},{12,13},{... | collective-permute-start | bytes 3145736 | tf_op jit(solution)/shard_map/ppermute | solution.py:434
  8.0 3.6 %prep.1 = (bf16[8,256,256]{2,1,0:T(8,128)(2,1)}, bf16[4,384,256]{2,1,0:T(8,128)(2,1)}, bf16[192,256]{1,0:T(8,128)(2,1)}) custom-call(s32[16]{0:T(128)} %index_ref.1, f32[8,31]{1,0:T(8,128)} %taps_ref.1), custom_call_target="tpu_custom_call" | custom-call | flops 1000000 | bytes 2000000 | tf_op jit(solution)/shard_map/prep/pallas_call | solution.py:77
  11.6 0.7 fusion.3
  12.3 2.1 fusion.2
  14.3 13.3 %collective-permute-done.3.after = bf16[8,16,4096]{2,1,0:T(8,128)(2,1)S(1)} collective-permute-done((bf16[8,16,4096]{2,1,0:T(8,128)(2,1)S(1)}, bf16[8,16,4096]{2,1,0:T(8,128)(2,1)S(1)}, u32[]{:S(2)}, u32[]{:S(2)}) %collective-permute-start.3) | collective-permute-done | bytes 1048608 | tf_op jit(solution)/shard_map/ppermute | solution.py:435
  27.7 0.9 collective-permute-done.2.before
  28.7 8.4 %smooth.3 = bf16[64,8,1536]{2,1,0:T(8,128)(2,1)} custom-call(s32[8]{0:T(128)} %get-tuple-element.21.index_ref, bf16[8,16,4096]{2,1,0:T(8,128)(2,1)} %collective-permute-done.2.before, bf16[8,16,4096]{2,1,0:T(8,128)(2,1)} %copy-done.3, bf16[8,16,4096]{2,1,0:T(8,128)(2,1)} %copy-done.4, bf16[8,16,4096]{2,1,0:T(8,128)(2,1)} %copy-done.9, ...), custom_call_target="tpu_custom_call" | custom-call | flops 4000000000 | bytes 8000000 | tf_op jit(solution)/shard_map/smooth/pallas_call | solution.py:171
  37.1 13.5 %all-to-all-start.1 = ((bf16[64,8,1536]{2,1,0:T(8,128)(2,1)}), bf16[64,8,1536]{2,1,0:T(8,128)(2,1)}, u32[]{:S(2)}, u32[]{:S(2)}) async-start(bf16[64,8,1536]{2,1,0:T(8,128)(2,1)} %smooth.3), calls=%async_computation.1 | async-start | bytes 3145728 | tf_op jit(solution)/shard_map/all_to_all | solution.py:442
  50.9 1.0 copy-done.5
  51.9 1.3 collective-permute-start.1
  53.2 4.9 %collective-permute-start = (bf16[8,16,4096]{2,1,0:T(8,128)(2,1)S(1)}, bf16[8,16,4096]{2,1,0:T(8,128)(2,1)S(1)}, u32[]{:S(2)}, u32[]{:S(2)}) collective-permute-start(bf16[8,16,4096]{2,1,0:T(8,128)(2,1)S(1)} %get-tuple-element.18.bottom), channel_id=1, source_target_pairs={{0,1},{1,2},{2,3},{4,5},{5,6},{6,7},{8,9},{9,10},{10,11},{12,13},{... | collective-permute-start | bytes 3145736 | tf_op jit(solution)/shard_map/ppermute | solution.py:434
  58.1 21.2 %collective-permute-done.1.after = bf16[8,16,4096]{2,1,0:T(8,128)(2,1)S(1)} collective-permute-done((bf16[8,16,4096]{2,1,0:T(8,128)(2,1)S(1)}, bf16[8,16,4096]{2,1,0:T(8,128)(2,1)S(1)}, u32[]{:S(2)}, u32[]{:S(2)}) %collective-permute-start.1) | collective-permute-done | bytes 1048608 | tf_op jit(solution)/shard_map/ppermute | solution.py:435
  79.4 0.8 collective-permute-done.before
  80.4 0.7 copy-done.11
  81.2 8.4 %smooth.2 = bf16[64,8,1536]{2,1,0:T(8,128)(2,1)} custom-call(s32[8]{0:T(128)} %get-tuple-element.22.index_ref, bf16[8,16,4096]{2,1,0:T(8,128)(2,1)} %copy-done.11, bf16[8,16,4096]{2,1,0:T(8,128)(2,1)} %copy-done.5, bf16[8,16,4096]{2,1,0:T(8,128)(2,1)} %copy-done.6, bf16[8,16,4096]{2,1,0:T(8,128)(2,1)} %copy-done.10, ...), custom_call_target="tpu_custom_call" | custom-call | flops 4000000000 | bytes 8000000 | tf_op jit(solution)/shard_map/smooth/pallas_call | solution.py:171
  89.6 11.2 %all-to-all-start = ((bf16[64,8,1536]{2,1,0:T(8,128)(2,1)}), bf16[64,8,1536]{2,1,0:T(8,128)(2,1)S(1)}, u32[]{:S(2)}, u32[]{:S(2)}) async-start(bf16[64,8,1536]{2,1,0:T(8,128)(2,1)} %smooth.2), calls=%async_computation | async-start | bytes 3145728 | tf_op jit(solution)/shard_map/all_to_all | solution.py:442
  100.8 39.0 %all-to-all-done = bf16[64,8,1536]{2,1,0:T(8,128)(2,1)S(1)} async-done(((bf16[64,8,1536]{2,1,0:T(8,128)(2,1)}), bf16[64,8,1536]{2,1,0:T(8,128)(2,1)S(1)}, u32[]{:S(2)}, u32[]{:S(2)}) %all-to-all-start) | async-done | bytes 1572896 | tf_op jit(solution)/shard_map/all_to_all | solution.py:442
  139.8 1.1 copy-done.1
  140.9 5.9 %cov.1 = (f32[4,640,128]{2,1,0:T(8,128)}, bf16[4,640,128]{2,1,0:T(8,128)(2,1)}) custom-call(s32[1]{0:T(128)} %bitcast.core_ref, bf16[512,1536]{1,0:T(8,128)(2,1)} %bitcast.11, bf16[512,1536]{1,0:T(8,128)(2,1)} %bitcast.2.part1), custom_call_target="tpu_custom_call" | custom-call | flops 2000000000 | bytes 6000000 | tf_op jit(solution)/shard_map/cov/pallas_call | solution.py:236
  146.8 0.6 collective-permute-start.4
  147.4 1.9 collective-permute-done.4
  149.4 1.5 add_convert_fusion
  150.8 15.2 %all_to_all.30 = bf16[4,640,128]{2,1,0:T(8,128)(2,1)S(1)} all-to-all(bf16[4,640,128]{2,1,0:T(8,128)(2,1)S(1)} %add_convert_fusion), channel_id=1, replica_groups=mesh['y'=4,'z'=8,'core'=2,'sky'=4] {'sky'}, dimensions={0} | all-to-all | bytes 1310720 | tf_op jit(solution)/shard_map/all_to_all | solution.py:264
  166.2 15.6 %all_to_all.31 = bf16[32,20,128]{2,1,0:T(8,128)(2,1)S(1)} all-to-all(bf16[32,20,128]{2,1,0:T(8,128)(2,1)S(1)} %reshape.26), channel_id=1, replica_groups=mesh['y'=4,'z'=8,'core'=2,'sky'=4] {'y','z'}, dimensions={0} | all-to-all | bytes 327680 | tf_op jit(solution)/shard_map/all_to_all | solution.py:266
  181.9 16.0 %all_to_all.32 = f32[32,20,128]{2,1,0:T(8,128)S(1)} all-to-all(f32[32,20,128]{2,1,0:T(8,128)S(1)} %broadcast_in_dim.6), channel_id=1, replica_groups=mesh['y'=4,'z'=8,'core'=2,'sky'=4] {'y','z'}, dimensions={0} | all-to-all | bytes 655360 | tf_op jit(solution)/shard_map/all_to_all | solution.py:258
  198.0 16.6 %all_to_all.33.near_ref = f32[4,640,128]{2,1,0:T(8,128)S(1)} all-to-all(f32[4,640,128]{2,1,0:T(8,128)S(1)} %broadcast_in_dim.15), channel_id=1, replica_groups=mesh['y'=4,'z'=8,'core'=2,'sky'=4] {'sky'}, dimensions={0} | all-to-all | bytes 2621440 | tf_op jit(solution)/shard_map/all_to_all | solution.py:258
  214.6 4.8 %collective-permute-start.5 = (f32[4,640,128]{2,1,0:T(8,128)S(1)}, f32[4,640,128]{2,1,0:T(8,128)}, u32[]{:S(2)}, u32[]{:S(2)}) collective-permute-start(f32[4,640,128]{2,1,0:T(8,128)S(1)} %all_to_all.33.near_ref), channel_id=1, source_target_pairs={{0,4},{4,0},{1,5},{5,1},{2,6},{6,2},{3,7},{7,3},{8,12},{12,8},{9,1... | collective-permute-start | bytes 3932168 | tf_op jit(solution)/shard_map/ppermute | solution.py:270
  219.7 0.8 copy.8.seed_ref
  220.5 1.5 seeds.1.seed_ref
  222.3 14.3 %clean.1 = bf16[64,16,1536]{2,1,0:T(8,128)(2,1)} custom-call(s32[1]{0:T(128)} %bitcast.core_ref, f32[4,640,128]{2,1,0:T(8,128)} %copy-done.2, f32[4,640,128]{2,1,0:T(8,128)} %collective-permute-done.5.far_ref, bf16[48,1024]{1,0:T(8,128)(2,1)} %seeds.1.seed_ref, bf16[512,1536]{1,0:T(8,128)(2,1)} %bitcast.12, bf16[512,1536]{1,0:T(8,128)(2,1)} %bitcast.2.part1), custom_call_target="tpu_custom_call" | custom-call | flops 3000000000 | bytes 12000000 | tf_op jit(solution)/shard_map/clean/pallas_call | solution.py:402
  (32 shorter events, 1.5 us)
Async XLA Ops:
  0.0 11.6 %copy-start.8 = (s32[16]{0:T(128)S(1)}, s32[16]{0:T(128)}, u32[]{:S(2)}) copy-start(s32[16]{0:T(128)} %index_ref.1) | copy-start | bytes 196
  1.7 26.9 %copy-start.3 = (bf16[8,16,4096]{2,1,0:T(8,128)(2,1)}, bf16[8,16,4096]{2,1,0:T(8,128)(2,1)S(1)}, u32[]{:S(2)}) copy-start(bf16[8,16,4096]{2,1,0:T(8,128)(2,1)S(1)} %get-tuple-element.15.top) | copy-start | bytes 3145732
  1.7 26.9 %copy-start.4 = (bf16[8,16,4096]{2,1,0:T(8,128)(2,1)}, bf16[8,16,4096]{2,1,0:T(8,128)(2,1)S(1)}, u32[]{:S(2)}) copy-start(bf16[8,16,4096]{2,1,0:T(8,128)(2,1)S(1)} %get-tuple-element.16.bottom) | copy-start | bytes 3145732
  1.7 25.9 %collective-permute-start.3 = (bf16[8,16,4096]{2,1,0:T(8,128)(2,1)S(1)}, bf16[8,16,4096]{2,1,0:T(8,128)(2,1)S(1)}, u32[]{:S(2)}, u32[]{:S(2)}) collective-permute-start(bf16[8,16,4096]{2,1,0:T(8,128)(2,1)S(1)} %get-tuple-element.15.top), channel_id=1, source_target_pairs={{1,0},{2,1},{3,2},{5,4},{6,5},{7,6},{9,8},{10,9},{11,10},{13,12},{... | collective-permute-start | bytes 3145736 | tf_op jit(solution)/shard_map/ppermute | solution.py:435
  3.0 25.5 %collective-permute-start.2 = (bf16[8,16,4096]{2,1,0:T(8,128)(2,1)S(1)}, bf16[8,16,4096]{2,1,0:T(8,128)(2,1)}, u32[]{:S(2)}, u32[]{:S(2)}) collective-permute-start(bf16[8,16,4096]{2,1,0:T(8,128)(2,1)S(1)} %get-tuple-element.16.bottom), channel_id=1, source_target_pairs={{0,1},{1,2},{2,3},{4,5},{5,6},{6,7},{8,9},{9,10},{10,11},{12,13},{... | collective-permute-start | bytes 3145736 | tf_op jit(solution)/shard_map/ppermute | solution.py:434
  27.7 1.0 copy-start.9
  37.1 13.5 %copy-start = (bf16[16,24,4096]{2,1,0:T(8,128)(2,1)S(1)}, bf16[16,24,4096]{2,1,0:T(8,128)(2,1)}, u32[]{:S(2)}) copy-start(bf16[16,24,4096]{2,1,0:T(8,128)(2,1)} %param.4) | copy-start | bytes 9437188
  37.1 52.5 %all-to-all-start.1 = ((bf16[64,8,1536]{2,1,0:T(8,128)(2,1)}), bf16[64,8,1536]{2,1,0:T(8,128)(2,1)}, u32[]{:S(2)}, u32[]{:S(2)}) async-start(bf16[64,8,1536]{2,1,0:T(8,128)(2,1)} %smooth.3), calls=%async_computation.1 | async-start | bytes 3145728 | tf_op jit(solution)/shard_map/all_to_all | solution.py:442
  50.9 1.0 copy-start.5
  50.9 28.5 %copy-start.6 = (bf16[8,16,4096]{2,1,0:T(8,128)(2,1)}, bf16[8,16,4096]{2,1,0:T(8,128)(2,1)S(1)}, u32[]{:S(2)}) copy-start(bf16[8,16,4096]{2,1,0:T(8,128)(2,1)S(1)} %get-tuple-element.18.bottom) | copy-start | bytes 3145732
  51.9 27.5 %collective-permute-start.1 = (bf16[8,16,4096]{2,1,0:T(8,128)(2,1)S(1)}, bf16[8,16,4096]{2,1,0:T(8,128)(2,1)S(1)}, u32[]{:S(2)}, u32[]{:S(2)}) collective-permute-start(bf16[8,16,4096]{2,1,0:T(8,128)(2,1)S(1)} %get-tuple-element.17.top), channel_id=1, source_target_pairs={{1,0},{2,1},{3,2},{5,4},{6,5},{7,6},{9,8},{10,9},{11,10},{13,12},{... | collective-permute-start | bytes 3145736 | tf_op jit(solution)/shard_map/ppermute | solution.py:435
  53.2 27.0 %collective-permute-start = (bf16[8,16,4096]{2,1,0:T(8,128)(2,1)S(1)}, bf16[8,16,4096]{2,1,0:T(8,128)(2,1)S(1)}, u32[]{:S(2)}, u32[]{:S(2)}) collective-permute-start(bf16[8,16,4096]{2,1,0:T(8,128)(2,1)S(1)} %get-tuple-element.18.bottom), channel_id=1, source_target_pairs={{0,1},{1,2},{2,3},{4,5},{5,6},{6,7},{8,9},{9,10},{10,11},{12,13},{... | collective-permute-start | bytes 3145736 | tf_op jit(solution)/shard_map/ppermute | solution.py:434
  79.4 1.1 copy-start.10
  80.2 1.0 copy-start.11
  89.6 50.2 %all-to-all-start = ((bf16[64,8,1536]{2,1,0:T(8,128)(2,1)}), bf16[64,8,1536]{2,1,0:T(8,128)(2,1)S(1)}, u32[]{:S(2)}, u32[]{:S(2)}) async-start(bf16[64,8,1536]{2,1,0:T(8,128)(2,1)} %smooth.2), calls=%async_computation | async-start | bytes 3145728 | tf_op jit(solution)/shard_map/all_to_all | solution.py:442
  139.8 1.1 copy-start.1
  146.8 2.6 %collective-permute-start.4 = (bf16[4,640,128]{2,1,0:T(8,128)(2,1)}, bf16[4,640,128]{2,1,0:T(8,128)(2,1)S(1)}, u32[]{:S(2)}, u32[]{:S(2)}) collective-permute-start(bf16[4,640,128]{2,1,0:T(8,128)(2,1)} %get-tuple-element.14), channel_id=1, source_target_pairs={{0,4},{4,0},{1,5},{5,1},{2,6},{6,2},{3,7},{7,3},{8,12},{12,8},{9,1... | collective-permute-start | bytes 1966088 | tf_op jit(solution)/shard_map/ppermute | solution.py:263
  198.0 21.4 %copy-start.7 = (s32[1024,16]{0,1:T(8,128)S(1)}, s32[1024,16]{0,1:T(8,128)}, u32[]{:S(2)}) copy-start(s32[1024,16]{0,1:T(8,128)} %param.7) | copy-start | bytes 196612
  214.6 7.6 %copy-start.2 = (f32[4,640,128]{2,1,0:T(8,128)}, f32[4,640,128]{2,1,0:T(8,128)S(1)}, u32[]{:S(2)}) copy-start(f32[4,640,128]{2,1,0:T(8,128)S(1)} %all_to_all.33.near_ref) | copy-start | bytes 3932164
  214.6 7.6 %collective-permute-start.5 = (f32[4,640,128]{2,1,0:T(8,128)S(1)}, f32[4,640,128]{2,1,0:T(8,128)}, u32[]{:S(2)}, u32[]{:S(2)}) collective-permute-start(f32[4,640,128]{2,1,0:T(8,128)S(1)} %all_to_all.33.near_ref), channel_id=1, source_target_pairs={{0,4},{4,0},{1,5},{5,1},{2,6},{6,2},{3,7},{7,3},{8,12},{12,8},{9,1... | collective-permute-start | bytes 3932168 | tf_op jit(solution)/shard_map/ppermute | solution.py:270

commit v5 on v4

--- a/solution.py
+++ b/solution.py
@@ -13,7 +13,7 @@
 TN = (((0,), (0,)), ((), ()))
 ROW_UNROLL, COL_UNROLL, PLACE_UNROLL, COL_RUN = 16, 4, 16, 16
 CHUNK = 8
-VMEM_LIMIT = 60 * 1024 * 1024
+VMEM_LIMIT = 20 * 1024 * 1024
 
 
 def vmem():
@@ -302,7 +302,7 @@
 
 
 def clean_kernel(
-    core_ref, near_ref, far_ref, seed_ref, part0, part1, out_ref, data_ref, cov_ref, basis_ref, coef_ref, sems
+    core_ref, near_ref, far_ref, seed_ref, part0, part1, out_ref, data_ref, cov_ref, basis_ref, coef_ref, done_ref, sems, out_sems
 ):
     core = core_ref[0]
     copies = load_parts((part0, part1), data_ref, sems)
@@ -370,6 +370,7 @@
     )
     hi, mid, low = split3(coef)
     coef_ref[...] = jnp.concatenate([hi, mid, hi, mid, low, hi], axis=0)
+    sent = []
     for m in range(count // 128):
         rows = slice(m * 128, m * 128 + 128)
         part = lax.dot_general(
@@ -377,7 +378,16 @@
         )
         value = (data_ref[rows, :].astype(F32) - part).astype(BF16)
         chunk, first = m // 4, (m % 4) * 16
-        out_ref[first : first + 16, chunk * 8 : chunk * 8 + 8, :] = value.reshape(16, 8, pixels)
+        done_ref[m] = value.reshape(16, 8, pixels)
+        copy = pltpu.make_async_copy(
+            done_ref.at[m],
+            out_ref.at[first : first + 16, chunk * 8 : chunk * 8 + 8, :],
+            out_sems.at[m],
+        )
+        copy.start()
+        sent.append(copy)
+    for copy in sent:
+        copy.wait()
 
 
 def seeds_kernel(seed_ref, out_ref):
@@ -403,13 +413,15 @@
         clean_kernel,
         out_shape=jax.ShapeDtypeStruct((count // 16, 16, pixels), BF16),
         in_specs=[smem()] + [vmem()] * 3 + [anywhere(), anywhere()],
-        out_specs=vmem(),
+        out_specs=anywhere(),
         scratch_shapes=[
             pltpu.VMEM((count, pixels), BF16),
             pltpu.VMEM((count, 2 * count), BF16),
             pltpu.VMEM((6 * modes, count), BF16),
             pltpu.VMEM((6 * modes, pixels), BF16),
+            pltpu.VMEM((count // 128, 16, 8, pixels), BF16),
             pltpu.SemaphoreType.DMA((2,)),
+            pltpu.SemaphoreType.DMA((count // 128,)),
         ],
         compiler_params=pltpu.CompilerParams(vmem_limit_bytes=VMEM_LIMIT),
         cost_estimate=pl.CostEstimate(

time: 238 us -> 237 us (level)
  Pallas kernels: 42.2 us -> 34.8 us
  local copies, waits for them, and re-layouts: 9.17 us -> 14.8 us
  waiting for transfers between devices: 77.4 us -> 80.6 us
  starting transfers between devices: 42.7 us -> 40.2 us
    pallas_call x2, Pallas kernels: 16.9 us -> 13 us  [smooth(): pl.pallas_call(smooth_kernel, grid=(channels // 4,), out_shape=jax.ShapeD...]
    pallas_call x1, Pallas kernels: 5.87 us -> 2.97 us  [local_covariance(): pl.pallas_call(cov_kernel, out_shape=(jax.ShapeDtypeStruct((4, 640, 128),...]
    all_to_all x2, starting transfers between devices: 24.7 us -> 22.2 us  [body(): data = lax.all_to_all(pieces, ('y', 'z', 'core'), 0, 0, tiled=True)]
  transfers between devices with their start and end apart: 8 -> 8, of which waited for: 7 -> 7; matrix products, arithmetic and copies ran while one was open for 2% -> 3% of each run, Pallas kernels for 6% -> 4%
where the time goes in v5:
time: 237 us; the launch traced here: 236 us
  waiting for transfers between devices  80.6 us (34%)
  blocking collectives  64.3 us (27%)
  starting transfers between devices  40.2 us (17%)
  Pallas kernels  34.8 us (15%)
  local copies, waits for them, and re-layouts  14.8 us (6%)
    all_to_all x2, waiting for transfers between devices, body(): data = lax.all_to_all(pieces, ('y', 'z', 'core'), 0, 0, tiled=True)  41.1 us
    ppermute x2, waiting for transfers between devices, body(): after = lax.ppermute(top, 'sky', [(i + 1, i) for i in range(3)])  36.1 us
    all_to_all x2, blocking collectives, everywhere(): return lax.all_to_all(copies, axes, 0, 0, tiled=True)  33.3 us
    all_to_all x2, starting transfers between devices, body(): data = lax.all_to_all(pieces, ('y', 'z', 'core'), 0, 0, tiled=True)  22.2 us
    all_to_all x1, blocking collectives, reduce_all(): lax.all_to_all(quarter.reshape(32, 20, 128), ('y', 'z'), 0, 0, tiled=True)  15.6 us
    all_to_all x1, blocking collectives, reduce_all(): got = lax.all_to_all(half.reshape(4, 640, 128), 'sky', 0, 0, tiled=True)  15.4 us
    pallas_call x1, Pallas kernels, clean(): pl.pallas_call(clean_kernel, out_shape=jax.ShapeDtypeStruct((count // 16,...  13.9 us
    pallas_call x2, Pallas kernels, smooth(): pl.pallas_call(smooth_kernel, grid=(channels // 4,), out_shape=jax.ShapeD...  13 us
  transfers between devices with their start and end apart: 8, of which 7 were waited for; matrix products, arithmetic and copies ran while one was open for 3% of the time, Pallas kernels for 4%

profile of v5, /device:TPU:33, one launch (start us, length us, event | category | flops | bytes accessed | tf_op | source)
XLA Modules:
  0.0 236.4 jit_solution(1361202838162506244)
XLA Ops:
  0.0 1.7 fusion
  1.7 1.3 collective-permute-start.3
  3.0 5.0 %collective-permute-start.2 = (bf16[8,16,4096]{2,1,0:T(8,128)(2,1)S(1)}, bf16[8,16,4096]{2,1,0:T(8,128)(2,1)}, u32[]{:S(2)}, u32[]{:S(2)}) collective-permute-start(bf16[8,16,4096]{2,1,0:T(8,128)(2,1)S(1)} %get-tuple-element.16.bottom), channel_id=1, source_target_pairs={{0,1},{1,2},{2,3},{4,5},{5,6},{6,7},{8,9},{9,10},{10,11},{12,13},{... | collective-permute-start | bytes 3145736 | tf_op jit(solution)/shard_map/ppermute | solution.py:446
  8.0 3.5 %prep.1 = (bf16[8,256,256]{2,1,0:T(8,128)(2,1)}, bf16[4,384,256]{2,1,0:T(8,128)(2,1)}, bf16[192,256]{1,0:T(8,128)(2,1)}) custom-call(s32[16]{0:T(128)} %index_ref.1, f32[8,31]{1,0:T(8,128)} %taps_ref.1), custom_call_target="tpu_custom_call" | custom-call | flops 1000000 | bytes 2000000 | tf_op jit(solution)/shard_map/prep/pallas_call | solution.py:77
  11.6 1.2 fusion.2
  12.9 14.9 %collective-permute-done.3.after = bf16[8,16,4096]{2,1,0:T(8,128)(2,1)} collective-permute-done((bf16[8,16,4096]{2,1,0:T(8,128)(2,1)S(1)}, bf16[8,16,4096]{2,1,0:T(8,128)(2,1)}, u32[]{:S(2)}, u32[]{:S(2)}) %collective-permute-start.3) | collective-permute-done | bytes 1048608 | tf_op jit(solution)/shard_map/ppermute | solution.py:447
  28.6 1.2 copy-done.2
  29.8 7.4 %smooth.3 = bf16[64,8,1536]{2,1,0:T(8,128)(2,1)} custom-call(s32[8]{0:T(128)S(1)} %get-tuple-element.21.index_ref, bf16[8,16,4096]{2,1,0:T(8,128)(2,1)} %collective-permute-done.2.before, bf16[8,16,4096]{2,1,0:T(8,128)(2,1)S(1)} %get-tuple-element.15.top, bf16[8,16,4096]{2,1,0:T(8,128)(2,1)S(1)} %copy-done.2, ...), custom_call_target="tpu_custom_call" | custom-call | flops 4000000000 | bytes 8000000 | tf_op jit(solution)/shard_map/smooth/pallas_call | solution.py:171
  37.2 13.2 %all-to-all-start.1 = ((bf16[64,8,1536]{2,1,0:T(8,128)(2,1)}), bf16[64,8,1536]{2,1,0:T(8,128)(2,1)S(1)}, u32[]{:S(2)}, u32[]{:S(2)}) async-start(bf16[64,8,1536]{2,1,0:T(8,128)(2,1)} %smooth.3), calls=%async_computation.1 | async-start | bytes 3145728 | tf_op jit(solution)/shard_map/all_to_all | solution.py:454
  50.4 1.8 fusion.1
  52.3 1.3 collective-permute-start.1
  53.6 4.9 %collective-permute-start = (bf16[8,16,4096]{2,1,0:T(8,128)(2,1)S(1)}, bf16[8,16,4096]{2,1,0:T(8,128)(2,1)S(1)}, u32[]{:S(2)}, u32[]{:S(2)}) collective-permute-start(bf16[8,16,4096]{2,1,0:T(8,128)(2,1)S(1)} %get-tuple-element.18.bottom), channel_id=1, source_target_pairs={{0,1},{1,2},{2,3},{4,5},{5,6},{6,7},{8,9},{9,10},{10,11},{12,13},{... | collective-permute-start | bytes 3145736 | tf_op jit(solution)/shard_map/ppermute | solution.py:446
  58.5 21.1 %collective-permute-done.1.after = bf16[8,16,4096]{2,1,0:T(8,128)(2,1)S(1)} collective-permute-done((bf16[8,16,4096]{2,1,0:T(8,128)(2,1)S(1)}, bf16[8,16,4096]{2,1,0:T(8,128)(2,1)S(1)}, u32[]{:S(2)}, u32[]{:S(2)}) %collective-permute-start.1) | collective-permute-done | bytes 1048608 | tf_op jit(solution)/shard_map/ppermute | solution.py:447
  80.5 5.6 %smooth.2 = bf16[64,8,1536]{2,1,0:T(8,128)(2,1)S(1)} custom-call(s32[8]{0:T(128)S(1)} %get-tuple-element.22.index_ref, bf16[8,16,4096]{2,1,0:T(8,128)(2,1)S(1)} %collective-permute-done.before, bf16[8,16,4096]{2,1,0:T(8,128)(2,1)S(1)} %get-tuple-element.17.top, bf16[8,16,4096]{2,1,0:T(8,128)(2,1)S(1)} %get-tuple-element.18.bottom, ...), custom_call_target="tpu_custom_call" | custom-call | flops 4000000000 | bytes 8000000 | tf_op jit(solution)/shard_map/smooth/pallas_call | solution.py:171
  86.1 1.1 copy-done
  87.2 2.1 all-to-all-done.1
  89.4 9.1 %all-to-all-start = ((bf16[64,8,1536]{2,1,0:T(8,128)(2,1)}), bf16[64,8,1536]{2,1,0:T(8,128)(2,1)S(1)}, u32[]{:S(2)}, u32[]{:S(2)}) async-start(bf16[64,8,1536]{2,1,0:T(8,128)(2,1)} %copy-done), calls=%async_computation | async-start | bytes 3145728 | tf_op jit(solution)/shard_map/all_to_all | solution.py:454
  98.4 39.0 %all-to-all-done = bf16[64,8,1536]{2,1,0:T(8,128)(2,1)S(1)} async-done(((bf16[64,8,1536]{2,1,0:T(8,128)(2,1)}), bf16[64,8,1536]{2,1,0:T(8,128)(2,1)S(1)}, u32[]{:S(2)}, u32[]{:S(2)}) %all-to-all-start) | async-done | bytes 1572896 | tf_op jit(solution)/shard_map/all_to_all | solution.py:454
  137.4 3.0 %cov.1 = (f32[4,640,128]{2,1,0:T(8,128)S(1)}, bf16[4,640,128]{2,1,0:T(8,128)(2,1)S(1)}) custom-call(s32[1]{0:T(128)} %bitcast.core_ref, bf16[512,1536]{1,0:T(8,128)(2,1)S(1)} %bitcast.11, bf16[512,1536]{1,0:T(8,128)(2,1)S(1)} %bitcast.9), custom_call_target="tpu_custom_call" | custom-call | flops 2000000000 | bytes 6000000 | tf_op jit(solution)/shard_map/cov/pallas_call | solution.py:236
  141.0 1.7 collective-permute-done.4
  142.9 15.4 %all_to_all.30 = bf16[4,640,128]{2,1,0:T(8,128)(2,1)} all-to-all(bf16[4,640,128]{2,1,0:T(8,128)(2,1)S(1)} %add_convert_fusion), channel_id=1, replica_groups=mesh['y'=4,'z'=8,'core'=2,'sky'=4] {'sky'}, dimensions={0} | all-to-all | bytes 1310720 | tf_op jit(solution)/shard_map/all_to_all | solution.py:264
  158.3 1.2 reduce_sum.21
  159.6 15.6 %all_to_all.31 = bf16[32,20,128]{2,1,0:T(8,128)(2,1)S(1)} all-to-all(bf16[32,20,128]{2,1,0:T(8,128)(2,1)S(1)} %reshape.26), channel_id=1, replica_groups=mesh['y'=4,'z'=8,'core'=2,'sky'=4] {'y','z'}, dimensions={0} | all-to-all | bytes 327680 | tf_op jit(solution)/shard_map/all_to_all | solution.py:266
  175.3 16.0 %all_to_all.32 = f32[32,20,128]{2,1,0:T(8,128)S(1)} all-to-all(f32[32,20,128]{2,1,0:T(8,128)S(1)} %broadcast_in_dim.6), channel_id=1, replica_groups=mesh['y'=4,'z'=8,'core'=2,'sky'=4] {'y','z'}, dimensions={0} | all-to-all | bytes 655360 | tf_op jit(solution)/shard_map/all_to_all | solution.py:258
  192.0 1.1 broadcast_in_dim.15
  193.1 17.3 %all_to_all.33.near_ref = f32[4,640,128]{2,1,0:T(8,128)} all-to-all(f32[4,640,128]{2,1,0:T(8,128)S(1)} %broadcast_in_dim.15), channel_id=1, replica_groups=mesh['y'=4,'z'=8,'core'=2,'sky'=4] {'sky'}, dimensions={0} | all-to-all | bytes 2621440 | tf_op jit(solution)/shard_map/all_to_all | solution.py:258
  210.4 4.8 %collective-permute-start.5 = (f32[4,640,128]{2,1,0:T(8,128)}, f32[4,640,128]{2,1,0:T(8,128)}, u32[]{:S(2)}, u32[]{:S(2)}) collective-permute-start(f32[4,640,128]{2,1,0:T(8,128)} %all_to_all.33.near_ref), channel_id=1, source_target_pairs={{0,4},{4,0},{1,5},{5,1},{2,6},{6,2},{3,7},{7,3},{8,12},{12,8},{9,1... | collective-permute-start | bytes 3932168 | tf_op jit(solution)/shard_map/ppermute | solution.py:270
  215.3 1.0 copy.6
  216.3 1.9 copy.7
  218.1 1.8 copy.8.seed_ref
  220.0 1.5 seeds.1.seed_ref
  222.4 13.9 %clean.1 = bf16[64,16,1536]{2,1,0:T(8,128)(2,1)} custom-call(s32[1]{0:T(128)} %bitcast.core_ref, f32[4,640,128]{2,1,0:T(8,128)} %all_to_all.33.near_ref, f32[4,640,128]{2,1,0:T(8,128)} %collective-permute-done.5.far_ref, bf16[48,1024]{1,0:T(8,128)(2,1)S(1)} %copy-done.3, bf16[512,1536]{1,0:T(8,128)(2,1)S(1)} %bitcast.12, bf16[512,1536]{1,0:T(8,128)(2,1)S(1)} %bitcast.10), custom_call_target="tpu_custom_call" | custom-call | flops 3000000000 | bytes 12000000 | tf_op jit(solution)/shard_map/clean/pallas_call | solution.py:412
  (26 shorter events, 4.3 us)
Async XLA Ops:
  0.0 11.5 %copy-start.8 = (s32[16]{0:T(128)S(1)}, s32[16]{0:T(128)}, u32[]{:S(2)}) copy-start(s32[16]{0:T(128)} %index_ref.1) | copy-start | bytes 196
  1.7 26.1 %copy-start.1 = (bf16[8,16,4096]{2,1,0:T(8,128)(2,1)}, bf16[8,16,4096]{2,1,0:T(8,128)(2,1)S(1)}, u32[]{:S(2)}) copy-start(bf16[8,16,4096]{2,1,0:T(8,128)(2,1)S(1)} %get-tuple-element.16.bottom) | copy-start | bytes 3145732
  1.7 26.0 %collective-permute-start.3 = (bf16[8,16,4096]{2,1,0:T(8,128)(2,1)S(1)}, bf16[8,16,4096]{2,1,0:T(8,128)(2,1)}, u32[]{:S(2)}, u32[]{:S(2)}) collective-permute-start(bf16[8,16,4096]{2,1,0:T(8,128)(2,1)S(1)} %get-tuple-element.15.top), channel_id=1, source_target_pairs={{1,0},{2,1},{3,2},{5,4},{6,5},{7,6},{9,8},{10,9},{11,10},{13,12},{... | collective-permute-start | bytes 3145736 | tf_op jit(solution)/shard_map/ppermute | solution.py:447
  3.0 25.5 %collective-permute-start.2 = (bf16[8,16,4096]{2,1,0:T(8,128)(2,1)S(1)}, bf16[8,16,4096]{2,1,0:T(8,128)(2,1)}, u32[]{:S(2)}, u32[]{:S(2)}) collective-permute-start(bf16[8,16,4096]{2,1,0:T(8,128)(2,1)S(1)} %get-tuple-element.16.bottom), channel_id=1, source_target_pairs={{0,1},{1,2},{2,3},{4,5},{5,6},{6,7},{8,9},{9,10},{10,11},{12,13},{... | collective-permute-start | bytes 3145736 | tf_op jit(solution)/shard_map/ppermute | solution.py:446
  11.5 17.1 %copy-start.4 = (bf16[8,256,256]{2,1,0:T(8,128)(2,1)S(1)}, bf16[8,256,256]{2,1,0:T(8,128)(2,1)}, u32[]{:S(2)}) copy-start(bf16[8,256,256]{2,1,0:T(8,128)(2,1)} %get-tuple-element.10.col_ref) | copy-start | bytes 3145732
  11.5 17.1 %copy-start.6 = (bf16[192,256]{1,0:T(8,128)(2,1)S(1)}, bf16[192,256]{1,0:T(8,128)(2,1)}, u32[]{:S(2)}) copy-start(bf16[192,256]{1,0:T(8,128)(2,1)} %get-tuple-element.12.order_ref) | copy-start | bytes 294916
  28.6 1.2 copy-start.2
  37.2 52.2 %all-to-all-start.1 = ((bf16[64,8,1536]{2,1,0:T(8,128)(2,1)}), bf16[64,8,1536]{2,1,0:T(8,128)(2,1)S(1)}, u32[]{:S(2)}, u32[]{:S(2)}) async-start(bf16[64,8,1536]{2,1,0:T(8,128)(2,1)} %smooth.3), calls=%async_computation.1 | async-start | bytes 3145728 | tf_op jit(solution)/shard_map/all_to_all | solution.py:454
  50.4 30.1 %copy-start.5 = (bf16[8,256,256]{2,1,0:T(8,128)(2,1)S(1)}, bf16[8,256,256]{2,1,0:T(8,128)(2,1)}, u32[]{:S(2)}) copy-start(bf16[8,256,256]{2,1,0:T(8,128)(2,1)} %get-tuple-element.10.col_ref) | copy-start | bytes 3145732
  52.3 27.4 %collective-permute-start.1 = (bf16[8,16,4096]{2,1,0:T(8,128)(2,1)S(1)}, bf16[8,16,4096]{2,1,0:T(8,128)(2,1)S(1)}, u32[]{:S(2)}, u32[]{:S(2)}) collective-permute-start(bf16[8,16,4096]{2,1,0:T(8,128)(2,1)S(1)} %get-tuple-element.17.top), channel_id=1, source_target_pairs={{1,0},{2,1},{3,2},{5,4},{6,5},{7,6},{9,8},{10,9},{11,10},{13,12},{... | collective-permute-start | bytes 3145736 | tf_op jit(solution)/shard_map/ppermute | solution.py:447
  53.6 27.0 %collective-permute-start = (bf16[8,16,4096]{2,1,0:T(8,128)(2,1)S(1)}, bf16[8,16,4096]{2,1,0:T(8,128)(2,1)S(1)}, u32[]{:S(2)}, u32[]{:S(2)}) collective-permute-start(bf16[8,16,4096]{2,1,0:T(8,128)(2,1)S(1)} %get-tuple-element.18.bottom), channel_id=1, source_target_pairs={{0,1},{1,2},{2,3},{4,5},{5,6},{6,7},{8,9},{9,10},{10,11},{12,13},{... | collective-permute-start | bytes 3145736 | tf_op jit(solution)/shard_map/ppermute | solution.py:446
  86.1 1.1 copy-start
  89.4 48.0 %all-to-all-start = ((bf16[64,8,1536]{2,1,0:T(8,128)(2,1)}), bf16[64,8,1536]{2,1,0:T(8,128)(2,1)S(1)}, u32[]{:S(2)}, u32[]{:S(2)}) async-start(bf16[64,8,1536]{2,1,0:T(8,128)(2,1)} %copy-done), calls=%async_computation | async-start | bytes 3145728 | tf_op jit(solution)/shard_map/all_to_all | solution.py:454
  140.4 2.4 collective-permute-start.4
  193.1 22.2 %copy-start.7 = (s32[1024,16]{0,1:T(8,128)S(1)}, s32[1024,16]{0,1:T(8,128)}, u32[]{:S(2)}) copy-start(s32[1024,16]{0,1:T(8,128)} %param.7) | copy-start | bytes 196612
  210.4 11.1 %collective-permute-start.5 = (f32[4,640,128]{2,1,0:T(8,128)}, f32[4,640,128]{2,1,0:T(8,128)}, u32[]{:S(2)}, u32[]{:S(2)}) collective-permute-start(f32[4,640,128]{2,1,0:T(8,128)} %all_to_all.33.near_ref), channel_id=1, source_target_pairs={{0,4},{4,0},{1,5},{5,1},{2,6},{6,2},{3,7},{7,3},{8,12},{12,8},{9,1... | collective-permute-start | bytes 3932168 | tf_op jit(solution)/shard_map/ppermute | solution.py:270
  221.5 0.9 copy-start.3

commit v6 on v5

--- a/solution.py
+++ b/solution.py
@@ -89,11 +89,8 @@
     )(beam_index, beam_taps)
 
 
-def smooth_kernel(
-    index_ref, before, top, bottom, after, col_ref, row_ref, order_ref, out_ref, hi_ref, mid_ref, sm_ref
-):
-    group = pl.program_id(0)
-    columns = before.shape[2]
+def smooth_group(group, index_ref, strips, col_ref, row_ref, hi_ref, mid_ref, sm_ref):
+    columns = strips[0].shape[2]
     blocks = columns // 256
     tiles = columns // 128
     lane = lax.broadcasted_iota(jnp.int32, (128, 128), 1)
@@ -108,8 +105,7 @@
     def row_step(n, tail):
         cols = pl.ds(pl.multiple_of(n * 256, 256), 256)
         data = jnp.concatenate(
-            [ref[place, :, cols] for place in range(4) for ref in (before, top, bottom, after)],
-            axis=0,
+            [ref[place, :, cols] for place in range(4) for ref in strips], axis=0
         )
         full = jnp.dot(row_ref[0], data, preferred_element_type=F32)
         value = full[0:128] + full[128:256] + full[256:384]
@@ -143,25 +139,97 @@
 
     lax.fori_loop(0, 4, col_step, 0, unroll=COL_UNROLL)
 
+
+def place_tiles(sm_refs, order_ref, out_ref):
+    channels = out_ref.shape[1]
+    lane3 = lax.broadcasted_iota(jnp.int32, (12, channels, 128), 2)
+
+    def place_step(n, carry):
+        data = jnp.concatenate(
+            [
+                jnp.concatenate([ref[2 * n + t] for ref in sm_refs], axis=0)
+                for t in range(2)
+            ],
+            axis=1,
+        )
+        moved = jnp.dot(order_ref[...], data, preferred_element_type=F32)
+        for t in range(2):
+            four = moved[:, t * 128 : t * 128 + 128].reshape(12, 2, channels, 128)
+            even, odd = four[:, 0], four[:, 1]
+            low = jnp.where(lane3 < 64, even, pltpu.roll(odd, 64, 2)).astype(BF16)
+            high = jnp.where(lane3 < 64, pltpu.roll(even, 64, 2), odd).astype(BF16)
+            for q in range(12):
+                out_ref[4 * n + 2 * t, :, q * 128 : q * 128 + 128] = low[q]
+                out_ref[4 * n + 2 * t + 1, :, q * 128 : q * 128 + 128] = high[q]
+        return carry
+
+    lax.fori_loop(0, out_ref.shape[0] // 4, place_step, 0, unroll=PLACE_UNROLL)
+
+
+def smooth_kernel(
+    index_ref, before, top, bottom, after, col_ref, row_ref, order_ref, out_ref, hi_ref, mid_ref, sm_ref
+):
+    group = pl.program_id(0)
+    strips = (before, top, bottom, after)
+    smooth_group(group, index_ref, strips, col_ref, row_ref, hi_ref, mid_ref, sm_ref)
+
     @pl.when(group == pl.num_programs(0) - 1)
     def _():
-        channels = out_ref.shape[1]
-        lane3 = lax.broadcasted_iota(jnp.int32, (12, channels, 128), 2)
-
-        def place_step(n, carry):
-            data = jnp.concatenate([sm_ref[2 * n], sm_ref[2 * n + 1]], axis=1)
-            moved = jnp.dot(order_ref[...], data, preferred_element_type=F32)
-            for t in range(2):
-                four = moved[:, t * 128 : t * 128 + 128].reshape(12, 2, channels, 128)
-                even, odd = four[:, 0], four[:, 1]
-                low = jnp.where(lane3 < 64, even, pltpu.roll(odd, 64, 2)).astype(BF16)
-                high = jnp.where(lane3 < 64, pltpu.roll(even, 64, 2), odd).astype(BF16)
-                for q in range(12):
-                    out_ref[4 * n + 2 * t, :, q * 128 : q * 128 + 128] = low[q]
-                    out_ref[4 * n + 2 * t + 1, :, q * 128 : q * 128 + 128] = high[q]
-            return carry
-
-        lax.fori_loop(0, blocks, place_step, 0, unroll=PLACE_UNROLL)
+        place_tiles((sm_ref,), order_ref, out_ref)
+
+
+def first_kernel(
+    index_ref, before, top, bottom, after, col_ref, row_ref, sm_ref, hi_ref, mid_ref
+):
+    strips = (before, top, bottom, after)
+    smooth_group(0, index_ref, strips, col_ref, row_ref, hi_ref, mid_ref, sm_ref)
+
+
+def second_kernel(
+    index_ref, before, top, bottom, after, col_ref, row_ref, first_ref, order_ref, out_ref, hi_ref, mid_ref, sm_ref
+):
+    strips = (before, top, bottom, after)
+    smooth_group(0, index_ref, strips, col_ref, row_ref, hi_ref, mid_ref, sm_ref)
+    place_tiles((first_ref, sm_ref), order_ref, out_ref)
+
+
+def smooth_cost(channels):
+    return pl.CostEstimate(
+        flops=5 * 10**8 * channels, bytes_accessed=10**6 * channels, transcendentals=0
+    )
+
+
+def half_scratch(tiles):
+    return [pltpu.VMEM((4, tiles + 1, 32, 128), BF16)] * 2
+
+
+def smooth_first(beam_index, halo, col, row):
+    tiles = halo[0].shape[2] // 128
+    return pl.pallas_call(
+        first_kernel,
+        out_shape=jax.ShapeDtypeStruct((tiles, 128, 128), BF16),
+        in_specs=[smem()] + [vmem()] * 6,
+        out_specs=vmem(),
+        scratch_shapes=half_scratch(tiles),
+        compiler_params=pltpu.CompilerParams(vmem_limit_bytes=VMEM_LIMIT),
+        cost_estimate=smooth_cost(4),
+        name="first",
+    )(beam_index, *halo, col, row)
+
+
+def smooth_second(beam_index, halo, col, row, first, order):
+    columns = halo[0].shape[2]
+    tiles = columns // 128
+    return pl.pallas_call(
+        second_kernel,
+        out_shape=jax.ShapeDtypeStruct((columns // 64, 8, 1536), BF16),
+        in_specs=[smem()] + [vmem()] * 8,
+        out_specs=vmem(),
+        scratch_shapes=half_scratch(tiles) + [pltpu.VMEM((tiles, 128, 128), BF16)],
+        compiler_params=pltpu.CompilerParams(vmem_limit_bytes=VMEM_LIMIT),
+        cost_estimate=smooth_cost(4),
+        name="second",
+    )(beam_index, *halo, col, row, first, order)
 
 
 def smooth(beam_index, before, top, bottom, after, col, row, order):
@@ -180,15 +248,9 @@
             pl.BlockSpec(order.shape, lambda g: (0, 0)),
         ],
         out_specs=pl.BlockSpec((columns // 64, channels, 1536), lambda g: (0, 0, 0)),
-        scratch_shapes=[
-            pltpu.VMEM((4, tiles + 1, 32, 128), BF16),
-            pltpu.VMEM((4, tiles + 1, 32, 128), BF16),
-            pltpu.VMEM((tiles, channels * 32, 128), BF16),
-        ],
+        scratch_shapes=half_scratch(tiles) + [pltpu.VMEM((tiles, channels * 32, 128), BF16)],
         compiler_params=pltpu.CompilerParams(vmem_limit_bytes=VMEM_LIMIT),
-        cost_estimate=pl.CostEstimate(
-            flops=5 * 10**8 * channels, bytes_accessed=10**6 * channels, transcendentals=0
-        ),
+        cost_estimate=smooth_cost(channels),
         name="smooth",
     )(beam_index, before, top, bottom, after, col, row, order)
 
@@ -206,9 +268,13 @@
     return copies
 
 
-def cov_kernel(core_ref, part0, part1, keep_ref, send_ref, data_ref, sems):
+def cov_kernel(core_ref, part0, part1, keep_ref, send_ref, tiles_ref, data_ref, sems, tiles_sem):
     for copy in load_parts((part0, part1, part0), data_ref, sems):
         copy.wait()
+    tiles_copy = pltpu.make_async_copy(
+        data_ref.at[0 : tiles_ref.shape[0]], tiles_ref, tiles_sem
+    )
+    tiles_copy.start()
     core = core_ref[0]
 
     def fill(out_ref, first):
@@ -225,6 +291,7 @@
 
     fill(keep_ref, core * 4)
     fill(send_ref, (1 - core) * 4)
+    tiles_copy.wait()
 
 
 def anywhere():
@@ -238,12 +305,14 @@
         out_shape=(
             jax.ShapeDtypeStruct((4, 640, 128), F32),
             jax.ShapeDtypeStruct((4, 640, 128), BF16),
+            jax.ShapeDtypeStruct((rows, parts[0].shape[1]), BF16),
         ),
         in_specs=[smem(), anywhere(), anywhere()],
-        out_specs=(vmem(), vmem()),
+        out_specs=(vmem(), vmem(), pl.BlockSpec(memory_space=pltpu.HBM)),
         scratch_shapes=[
             pltpu.VMEM((rows + parts[0].shape[0], parts[0].shape[1]), BF16),
             pltpu.SemaphoreType.DMA((3,)),
+            pltpu.SemaphoreType.DMA,
         ],
         compiler_params=pltpu.CompilerParams(vmem_limit_bytes=VMEM_LIMIT),
         cost_estimate=pl.CostEstimate(
@@ -261,8 +330,13 @@
 def reduce_all(keep, send):
     swap = [(0, 1), (1, 0)]
     half = (keep + lax.ppermute(send, "core", swap).astype(F32)).astype(BF16)
-    got = lax.all_to_all(half.reshape(4, 640, 128), "sky", 0, 0, tiled=True)
-    quarter = jnp.sum(got.astype(F32), axis=0).astype(BF16)
+    half = half.reshape(4, 640, 128)
+    sky = lax.axis_index("sky")
+    total = lax.dynamic_index_in_dim(half, sky, 0, False).astype(F32)
+    for d in (2, 1, 3):
+        block = lax.dynamic_index_in_dim(half, lax.rem(sky + d, 4), 0, False)
+        total += lax.ppermute(block, "sky", [(i, (i + d) % 4) for i in range(4)]).astype(F32)
+    quarter = total.astype(BF16)
     got = lax.all_to_all(quarter.reshape(32, 20, 128), ("y", "z"), 0, 0, tiled=True)
     mine = jnp.sum(got.astype(F32), axis=0)
     quarter = everywhere(mine, ("y", "z"), 32).reshape(640, 128)
@@ -302,10 +376,11 @@
 
 
 def clean_kernel(
-    core_ref, near_ref, far_ref, seed_ref, part0, part1, out_ref, data_ref, cov_ref, basis_ref, coef_ref, done_ref, sems, out_sems
+    core_ref, near_ref, far_ref, seed_ref, tiles_ref, out_ref, data_ref, cov_ref, basis_ref, coef_ref, done_ref, sem, out_sems
 ):
     core = core_ref[0]
-    copies = load_parts((part0, part1), data_ref, sems)
+    tiles_copy = pltpu.make_async_copy(tiles_ref, data_ref, sem)
+    tiles_copy.start()
     modes = seed_ref.shape[0] // 3
     count = seed_ref.shape[1]
     pixels = data_ref.shape[1]
@@ -362,8 +437,7 @@
     basis = exact_dot(end_factor(work), images)
     hi, mid, low = split3(basis)
     basis_ref[...] = jnp.concatenate([hi, hi, mid, mid, hi, low], axis=0)
-    for copy in copies:
-        copy.wait()
+    tiles_copy.wait()
     data = data_ref[...]
     coef = fold(
         jnp.dot(jnp.concatenate([hi, mid, low], axis=0), data, preferred_element_type=F32)
@@ -405,14 +479,14 @@
     )(seed)
 
 
-def clean(core, near, far, seed, parts):
+def clean(core, near, far, seed, tiles):
     modes, count = seed.shape
     modes = modes // 3
-    pixels = parts[0].shape[1]
+    pixels = tiles.shape[1]
     return pl.pallas_call(
         clean_kernel,
         out_shape=jax.ShapeDtypeStruct((count // 16, 16, pixels), BF16),
-        in_specs=[smem()] + [vmem()] * 3 + [anywhere(), anywhere()],
+        in_specs=[smem()] + [vmem()] * 3 + [pl.BlockSpec(memory_space=pltpu.HBM)],
         out_specs=anywhere(),
         scratch_shapes=[
             pltpu.VMEM((count, pixels), BF16),
@@ -420,7 +494,7 @@
             pltpu.VMEM((6 * modes, count), BF16),
             pltpu.VMEM((6 * modes, pixels), BF16),
             pltpu.VMEM((count // 128, 16, 8, pixels), BF16),
-            pltpu.SemaphoreType.DMA((2,)),
+            pltpu.SemaphoreType.DMA,
             pltpu.SemaphoreType.DMA((count // 128,)),
         ],
         compiler_params=pltpu.CompilerParams(vmem_limit_bytes=VMEM_LIMIT),
@@ -428,7 +502,7 @@
             flops=3 * 10**9, bytes_accessed=12 * 10**6, transcendentals=0
         ),
         name="clean",
-    )(core, near, far, seed, *parts)
+    )(core, near, far, seed, tiles)
 
 
 def body(sky_maps, beam_index, beam_taps, start_seed):
@@ -437,28 +511,27 @@
     core = lax.axis_index("core").astype(jnp.int32).reshape(1)
     col, row, order = prepare(beam_index, beam_taps, CHUNK)
     halos = []
-    for first in range(0, channels, CHUNK):
+    for first, last in ((0, 4), (4, 8), (8, 16)):
         strip = sky_maps if first == 0 else lax.optimization_barrier(sky_maps)
-        strip = strip[first : first + CHUNK]
+        strip = strip[first:last]
         top = strip[:, 0:16, :]
         bottom = strip[:, strip_rows - 16 : strip_rows, :]
-        k = first // CHUNK
         before = lax.ppermute(bottom, "sky", [(i, i + 1) for i in range(3)])
         after = lax.ppermute(top, "sky", [(i + 1, i) for i in range(3)])
         halos.append((before, top, bottom, after))
+    first = smooth_first(beam_index[0:4], halos[0], col, row[0:1])
+    pieces0 = smooth_second(beam_index[4:8], halos[1], col, row[1:2], first, order)
+    pieces1 = smooth(beam_index[8:16], *halos[2], col, row[2:4], order)
     parts = []
-    for k, halo in enumerate(halos):
-        mine = slice(k * CHUNK, (k + 1) * CHUNK)
-        rows = row[k * CHUNK // 4 : (k + 1) * CHUNK // 4]
-        pieces = smooth(beam_index[mine], *halo, col, rows, order)
+    for pieces in (pieces0, pieces1):
         data = lax.all_to_all(pieces, ("y", "z", "core"), 0, 0, tiled=True)
         parts.append(data.reshape(64 * CHUNK, 1536))
     seed = start_seed.T.reshape(modes, 64, channels // CHUNK, CHUNK)
     seed = seed.transpose(0, 2, 1, 3).reshape(modes, 64 * channels)
     seed = split_seed(seed)
-    keep, send = local_covariance(core, parts)
+    keep, send, tiles = local_covariance(core, parts)
     near, far = reduce_all(keep, send)
-    cleaned = clean(core, near, far, seed, parts)
+    cleaned = clean(core, near, far, seed, tiles)
     return cleaned.reshape(64 * channels, 1, 1536)
 
 

time: 237 us -> 234 us (0.987)
  blocking collectives: 64.3 us -> 52.9 us
  starting transfers between devices: 40.2 us -> 49.8 us
  waiting for transfers between devices: 80.6 us -> 73.5 us
  local copies, waits for them, and re-layouts: 14.8 us -> 19.1 us
    all_to_all x1 -> x0, blocking collectives: 15.4 us -> none  [reduce_all(): got = lax.all_to_all(half.reshape(4, 640, 128), 'sky', 0, 0, tiled=True)]
    ppermute x2 -> x3, waiting for transfers between devices: 36.1 us -> 22.1 us  [body(): after = lax.ppermute(top, 'sky', [(i + 1, i) for i in range(3)])]
    pallas_call x0 -> x2, Pallas kernels: none -> 7.71 us  [the longest x1 5.01 us: smooth_second(): pl.pallas_call(second_kernel, out_shape=jax.ShapeDtypeStruct((columns //...]
    unnamed x18 -> x30, local copies, waits for them, and re-layouts: 3.28 us -> 10.4 us
    ppermute x0 -> x3, waiting for transfers between devices: none -> 6.68 us  [reduce_all(): lax.ppermute(block, 'sky', [(i, (i + d) % 4) for i in range(4)]).astype(F32)]
    pallas_call x2 -> x1, Pallas kernels: 13 us -> 6.74 us  [smooth(): pl.pallas_call(smooth_kernel, grid=(channels // 4,), out_shape=jax.ShapeD...]
    ppermute x0 -> x3, starting transfers between devices: none -> 5.53 us  [reduce_all(): lax.ppermute(block, 'sky', [(i, (i + d) % 4) for i in range(4)]).astype(F32)]
    all_to_all x2, blocking collectives: 33.3 us -> 37.3 us  [everywhere(): return lax.all_to_all(copies, axes, 0, 0, tiled=True)]
  transfers between devices with their start and end apart: 8 -> 13, of which waited for: 7 -> 9; matrix products, arithmetic and copies ran while one was open for 3% -> 3% of each run, Pallas kernels for 4% -> 6%
where the time goes in v6:
time: 234 us; the launch traced here: 233 us
  waiting for transfers between devices  73.5 us (31%)
  blocking collectives  52.9 us (23%)
  starting transfers between devices  49.8 us (21%)
  Pallas kernels  35.6 us (15%)
  local copies, waits for them, and re-layouts  19.1 us (8%)
    all_to_all x2, waiting for transfers between devices, body(): data = lax.all_to_all(pieces, ('y', 'z', 'core'), 0, 0, tiled=True)  41.1 us
    all_to_all x2, blocking collectives, everywhere(): return lax.all_to_all(copies, axes, 0, 0, tiled=True)  37.3 us
    all_to_all x2, starting transfers between devices, body(): data = lax.all_to_all(pieces, ('y', 'z', 'core'), 0, 0, tiled=True)  22.2 us
    ppermute x3, waiting for transfers between devices, body(): after = lax.ppermute(top, 'sky', [(i + 1, i) for i in range(3)])  22.1 us
    all_to_all x1, blocking collectives, reduce_all(): lax.all_to_all(quarter.reshape(32, 20, 128), ('y', 'z'), 0, 0, tiled=True)  15.6 us
    ppermute x3, starting transfers between devices, body(): before = lax.ppermute(bottom, 'sky', [(i, i + 1) for i in range(3)])  13.7 us
    pallas_call x1, Pallas kernels, clean(): pl.pallas_call(clean_kernel, out_shape=jax.ShapeDtypeStruct((count // 16,...  12.2 us
    unnamed x30, local copies, waits for them, and re-layouts  10.4 us
  transfers between devices with their start and end apart: 13, of which 9 were waited for; matrix products, arithmetic and copies ran while one was open for 3% of the time, Pallas kernels for 6%

profile of v6, /device:TPU:33, one launch (start us, length us, event | category | flops | bytes accessed | tf_op | source)
XLA Modules:
  0.0 232.9 jit_solution(13335685210965774951)
XLA Ops:
  0.0 1.3 fusion.4
  1.3 1.3 collective-permute-start.3
  2.6 4.0 %collective-permute-start.2 = (bf16[4,16,4096]{2,1,0:T(8,128)(2,1)S(1)}, bf16[4,16,4096]{2,1,0:T(8,128)(2,1)S(1)}, u32[]{:S(2)}, u32[]{:S(2)}) collective-permute-start(bf16[4,16,4096]{2,1,0:T(8,128)(2,1)S(1)} %get-tuple-element.20.bottom), channel_id=1, source_target_pairs={{0,1},{1,2},{2,3},{4,5},{5,6},{6,7},{8,9},{9,10},{10,11},{12,13},{... | collective-permute-start | bytes 1572872 | tf_op jit(solution)/shard_map/ppermute | solution.py:519
  6.6 1.3 fusion.5
  7.9 1.3 collective-permute-start.1
  9.2 4.8 %collective-permute-start = (bf16[4,16,4096]{2,1,0:T(8,128)(2,1)S(1)}, bf16[4,16,4096]{2,1,0:T(8,128)(2,1)}, u32[]{:S(2)}, u32[]{:S(2)}) collective-permute-start(bf16[4,16,4096]{2,1,0:T(8,128)(2,1)S(1)} %get-tuple-element.22.bottom), channel_id=1, source_target_pairs={{0,1},{1,2},{2,3},{4,5},{5,6},{6,7},{8,9},{9,10},{10,11},{12,13},{... | collective-permute-start | bytes 1572872 | tf_op jit(solution)/shard_map/ppermute | solution.py:519
  14.1 3.5 %prep.1 = (bf16[8,256,256]{2,1,0:T(8,128)(2,1)}, bf16[4,384,256]{2,1,0:T(8,128)(2,1)}, bf16[192,256]{1,0:T(8,128)(2,1)}) custom-call(s32[16]{0:T(128)} %index_ref.1, f32[8,31]{1,0:T(8,128)} %taps_ref.1), custom_call_target="tpu_custom_call" | custom-call | flops 1000000 | bytes 2000000 | tf_op jit(solution)/shard_map/prep/pallas_call | solution.py:77
  23.5 2.7 %first.1.first_ref = bf16[32,128,128]{2,1,0:T(8,128)(2,1)S(1)} custom-call(s32[4]{0:T(128)S(1)} %get-tuple-element.28.index_ref, bf16[4,16,4096]{2,1,0:T(8,128)(2,1)S(1)} %copy-done.7, bf16[4,16,4096]{2,1,0:T(8,128)(2,1)S(1)} %get-tuple-element.19.top, bf16[4,16,4096]{2,1,0:T(8,128)(2,1)S(1)} %get-tuple-element.20.bottom, ...), custom_call_target="tpu_custom_call" | custom-call | flops 2000000000 | bytes 4000000 | tf_op jit(solution)/shard_map/first/pallas_call | solution.py:208
  28.1 5.0 %second.1 = bf16[64,8,1536]{2,1,0:T(8,128)(2,1)} custom-call(s32[4]{0:T(128)S(1)} %get-tuple-element.29.index_ref, bf16[4,16,4096]{2,1,0:T(8,128)(2,1)} %collective-permute-done.before, bf16[4,16,4096]{2,1,0:T(8,128)(2,1)S(1)} %get-tuple-element.21.top, bf16[4,16,4096]{2,1,0:T(8,128)(2,1)S(1)} %get-tuple-element.22.bottom, ...), custom_call_target="tpu_custom_call" | custom-call | flops 2000000000 | bytes 4000000 | tf_op jit(solution)/shard_map/second/pallas_call | solution.py:223
  33.1 13.2 %all-to-all-start = ((bf16[64,8,1536]{2,1,0:T(8,128)(2,1)}), bf16[64,8,1536]{2,1,0:T(8,128)(2,1)S(1)}, u32[]{:S(2)}, u32[]{:S(2)}) async-start(bf16[64,8,1536]{2,1,0:T(8,128)(2,1)} %second.1), calls=%async_computation | async-start | bytes 3145728 | tf_op jit(solution)/shard_map/all_to_all | solution.py:527
  46.3 1.8 fusion.3
  48.2 1.3 collective-permute-start.5
  49.5 4.9 %collective-permute-start.4 = (bf16[8,16,4096]{2,1,0:T(8,128)(2,1)S(1)}, bf16[8,16,4096]{2,1,0:T(8,128)(2,1)S(1)}, u32[]{:S(2)}, u32[]{:S(2)}) collective-permute-start(bf16[8,16,4096]{2,1,0:T(8,128)(2,1)S(1)} %get-tuple-element.18.bottom), channel_id=1, source_target_pairs={{0,1},{1,2},{2,3},{4,5},{5,6},{6,7},{8,9},{9,10},{10,11},{12,13},{... | collective-permute-start | bytes 3145736 | tf_op jit(solution)/shard_map/ppermute | solution.py:519
  54.5 21.0 %collective-permute-done.5.after = bf16[8,16,4096]{2,1,0:T(8,128)(2,1)S(1)} collective-permute-done((bf16[8,16,4096]{2,1,0:T(8,128)(2,1)S(1)}, bf16[8,16,4096]{2,1,0:T(8,128)(2,1)S(1)}, u32[]{:S(2)}, u32[]{:S(2)}) %collective-permute-start.5) | collective-permute-done | bytes 1048608 | tf_op jit(solution)/shard_map/ppermute | solution.py:520
  76.4 6.7 %smooth.1 = bf16[64,8,1536]{2,1,0:T(8,128)(2,1)} custom-call(s32[8]{0:T(128)S(1)} %slice.53.index_ref, bf16[8,16,4096]{2,1,0:T(8,128)(2,1)S(1)} %collective-permute-done.4.before, bf16[8,16,4096]{2,1,0:T(8,128)(2,1)S(1)} %get-tuple-element.17.top, bf16[8,16,4096]{2,1,0:T(8,128)(2,1)S(1)} %get-tuple-element.18.bottom, ...), custom_call_target="tpu_custom_call" | custom-call | flops 4000000000 | bytes 8000000 | tf_op jit(solution)/shard_map/smooth/pallas_call | solution.py:239
  83.2 2.1 all-to-all-done
  85.3 9.1 %all-to-all-start.1 = ((bf16[64,8,1536]{2,1,0:T(8,128)(2,1)}), bf16[64,8,1536]{2,1,0:T(8,128)(2,1)S(1)}, u32[]{:S(2)}, u32[]{:S(2)}) async-start(bf16[64,8,1536]{2,1,0:T(8,128)(2,1)} %smooth.1), calls=%async_computation.1 | async-start | bytes 3145728 | tf_op jit(solution)/shard_map/all_to_all | solution.py:527
  94.4 39.0 %all-to-all-done.1 = bf16[64,8,1536]{2,1,0:T(8,128)(2,1)S(1)} async-done(((bf16[64,8,1536]{2,1,0:T(8,128)(2,1)}), bf16[64,8,1536]{2,1,0:T(8,128)(2,1)S(1)}, u32[]{:S(2)}, u32[]{:S(2)}) %all-to-all-start.1) | async-done | bytes 1572896 | tf_op jit(solution)/shard_map/all_to_all | solution.py:527
  133.4 4.0 %cov.1 = (f32[4,640,128]{2,1,0:T(8,128)S(1)}, bf16[4,640,128]{2,1,0:T(8,128)(2,1)}, bf16[1024,1536]{1,0:T(8,128)(2,1)S(1)}) custom-call(s32[1]{0:T(128)} %bitcast.core_ref, bf16[512,1536]{1,0:T(8,128)(2,1)S(1)} %bitcast.18, bf16[512,1536]{1,0:T(8,128)(2,1)S(1)} %bitcast.19), custom_call_target="tpu_custom_call" | custom-call | flops 2000000000 | bytes 6000000 | tf_op jit(solution)/shard_map/cov/pallas_call | solution.py:303
  138.5 1.7 copy-done.9
  140.7 1.9 collective-permute-done.6
  142.6 1.4 add_convert_fusion
  144.1 4.1 %collective-permute-start.7 = (bf16[640,128]{1,0:T(8,128)(2,1)S(1)}, bf16[640,128]{1,0:T(8,128)(2,1)S(1)}, u32[]{:S(2)}, u32[]{:S(2)}) collective-permute-start(bf16[640,128]{1,0:T(8,128)(2,1)S(1)} %get-tuple-element.25), channel_id=1, source_target_pairs={{0,2},{1,3},{2,0},{3,1},{4,6},{5,7},{6,4},{7,5},{8,10},{9,11},{10,... | collective-permute-start | bytes 491528 | tf_op jit(solution)/shard_map/ppermute | solution.py:338
  149.6 2.7 %collective-permute-done.7 = bf16[640,128]{1,0:T(8,128)(2,1)S(1)} collective-permute-done((bf16[640,128]{1,0:T(8,128)(2,1)S(1)}, bf16[640,128]{1,0:T(8,128)(2,1)S(1)}, u32[]{:S(2)}, u32[]{:S(2)}) %collective-permute-start.7) | collective-permute-done | bytes 163872 | tf_op jit(solution)/shard_map/ppermute | solution.py:338
  152.4 3.9 %collective-permute-done.9 = bf16[640,128]{1,0:T(8,128)(2,1)S(1)} collective-permute-done((bf16[640,128]{1,0:T(8,128)(2,1)S(1)}, bf16[640,128]{1,0:T(8,128)(2,1)S(1)}, u32[]{:S(2)}, u32[]{:S(2)}) %collective-permute-start.9) | collective-permute-done | bytes 163872 | tf_op jit(solution)/shard_map/ppermute | solution.py:338
  156.4 15.6 %all_to_all.25 = bf16[32,20,128]{2,1,0:T(8,128)(2,1)S(1)} all-to-all(bf16[32,20,128]{2,1,0:T(8,128)(2,1)S(1)} %reshape.28), channel_id=1, replica_groups=mesh['y'=4,'z'=8,'core'=2,'sky'=4] {'y','z'}, dimensions={0} | all-to-all | bytes 327680 | tf_op jit(solution)/shard_map/all_to_all | solution.py:340
  172.1 17.3 %all_to_all.26 = f32[32,20,128]{2,1,0:T(8,128)S(1)} all-to-all(f32[32,20,128]{2,1,0:T(8,128)S(1)} %broadcast_in_dim.6), channel_id=1, replica_groups=mesh['y'=4,'z'=8,'core'=2,'sky'=4] {'y','z'}, dimensions={0} | all-to-all | bytes 655360 | tf_op jit(solution)/shard_map/all_to_all | solution.py:327
  189.5 20.0 %all_to_all.27.near_ref = f32[4,640,128]{2,1,0:T(8,128)S(1)} all-to-all(f32[4,640,128]{2,1,0:T(8,128)S(1)} %broadcast_in_dim.15), channel_id=1, replica_groups=mesh['y'=4,'z'=8,'core'=2,'sky'=4] {'sky'}, dimensions={0} | all-to-all | bytes 2621440 | tf_op jit(solution)/shard_map/all_to_all | solution.py:327
  209.6 3.9 %collective-permute-start.10 = (f32[4,640,128]{2,1,0:T(8,128)S(1)}, f32[4,640,128]{2,1,0:T(8,128)S(1)}, u32[]{:S(2)}, u32[]{:S(2)}) collective-permute-start(f32[4,640,128]{2,1,0:T(8,128)S(1)} %all_to_all.27.near_ref), channel_id=1, source_target_pairs={{0,4},{4,0},{1,5},{5,1},{2,6},{6,2},{3,7},{7,3},{8,12},{12,8},{9,1... | collective-permute-start | bytes 3932168 | tf_op jit(solution)/shard_map/ppermute | solution.py:344
  216.3 1.5 seeds.1.seed_ref
  218.7 1.9 copy-done.10
  220.6 12.2 %clean.1 = bf16[64,16,1536]{2,1,0:T(8,128)(2,1)} custom-call(s32[1]{0:T(128)} %bitcast.core_ref, f32[4,640,128]{2,1,0:T(8,128)S(1)} %all_to_all.27.near_ref, f32[4,640,128]{2,1,0:T(8,128)S(1)} %collective-permute-done.10.far_ref, bf16[48,1024]{1,0:T(8,128)(2,1)S(1)} %copy-done.1, bf16[1024,1536]{1,0:T(8,128)(2,1)S(1)} %copy-done.10), custom_call_target="tpu_custom_call" | custom-call | flops 3000000000 | bytes 12000000 | tf_op jit(solution)/shard_map/clean/pallas_call | solution.py:486
  (52 shorter events, 16.1 us)
Async XLA Ops:
  1.3 12.7 %copy-start.13 = (s32[16]{0:T(128)S(1)}, s32[16]{0:T(128)}, u32[]{:S(2)}) copy-start(s32[16]{0:T(128)} %index_ref.1) | copy-start | bytes 196
  1.3 17.3 %collective-permute-start.3 = (bf16[4,16,4096]{2,1,0:T(8,128)(2,1)S(1)}, bf16[4,16,4096]{2,1,0:T(8,128)(2,1)S(1)}, u32[]{:S(2)}, u32[]{:S(2)}) collective-permute-start(bf16[4,16,4096]{2,1,0:T(8,128)(2,1)S(1)} %get-tuple-element.19.top), channel_id=1, source_target_pairs={{1,0},{2,1},{3,2},{5,4},{6,5},{7,6},{9,8},{10,9},{11,10},{13,12},{... | collective-permute-start | bytes 1572872 | tf_op jit(solution)/shard_map/ppermute | solution.py:520
  2.6 16.8 %collective-permute-start.2 = (bf16[4,16,4096]{2,1,0:T(8,128)(2,1)S(1)}, bf16[4,16,4096]{2,1,0:T(8,128)(2,1)S(1)}, u32[]{:S(2)}, u32[]{:S(2)}) collective-permute-start(bf16[4,16,4096]{2,1,0:T(8,128)(2,1)S(1)} %get-tuple-element.20.bottom), channel_id=1, source_target_pairs={{0,1},{1,2},{2,3},{4,5},{5,6},{6,7},{8,9},{9,10},{10,11},{12,13},{... | collective-permute-start | bytes 1572872 | tf_op jit(solution)/shard_map/ppermute | solution.py:519
  7.9 19.4 %collective-permute-start.1 = (bf16[4,16,4096]{2,1,0:T(8,128)(2,1)S(1)}, bf16[4,16,4096]{2,1,0:T(8,128)(2,1)}, u32[]{:S(2)}, u32[]{:S(2)}) collective-permute-start(bf16[4,16,4096]{2,1,0:T(8,128)(2,1)S(1)} %get-tuple-element.21.top), channel_id=1, source_target_pairs={{1,0},{2,1},{3,2},{5,4},{6,5},{7,6},{9,8},{10,9},{11,10},{13,12},{... | collective-permute-start | bytes 1572872 | tf_op jit(solution)/shard_map/ppermute | solution.py:520
  9.2 18.9 %collective-permute-start = (bf16[4,16,4096]{2,1,0:T(8,128)(2,1)S(1)}, bf16[4,16,4096]{2,1,0:T(8,128)(2,1)}, u32[]{:S(2)}, u32[]{:S(2)}) collective-permute-start(bf16[4,16,4096]{2,1,0:T(8,128)(2,1)S(1)} %get-tuple-element.22.bottom), channel_id=1, source_target_pairs={{0,1},{1,2},{2,3},{4,5},{5,6},{6,7},{8,9},{9,10},{10,11},{12,13},{... | collective-permute-start | bytes 1572872 | tf_op jit(solution)/shard_map/ppermute | solution.py:519
  18.6 0.8 copy-start.4
  19.4 0.8 copy-start.6
  20.2 1.2 copy-start.2
  21.4 1.0 copy-start.5
  22.5 1.0 copy-start.7
  23.5 4.6 %copy-start.3 = (bf16[8,256,256]{2,1,0:T(8,128)(2,1)S(1)}, bf16[8,256,256]{2,1,0:T(8,128)(2,1)}, u32[]{:S(2)}) copy-start(bf16[8,256,256]{2,1,0:T(8,128)(2,1)} %get-tuple-element.11.col_ref) | copy-start | bytes 3145732
  23.5 4.6 %copy-start.8 = (bf16[192,256]{1,0:T(8,128)(2,1)S(1)}, bf16[192,256]{1,0:T(8,128)(2,1)}, u32[]{:S(2)}) copy-start(bf16[192,256]{1,0:T(8,128)(2,1)} %get-tuple-element.13.order_ref) | copy-start | bytes 294916
  33.1 52.2 %all-to-all-start = ((bf16[64,8,1536]{2,1,0:T(8,128)(2,1)}), bf16[64,8,1536]{2,1,0:T(8,128)(2,1)S(1)}, u32[]{:S(2)}, u32[]{:S(2)}) async-start(bf16[64,8,1536]{2,1,0:T(8,128)(2,1)} %second.1), calls=%async_computation | async-start | bytes 3145728 | tf_op jit(solution)/shard_map/all_to_all | solution.py:527
  46.3 8.1 %copy-start.14 = (s32[16]{0:T(128)S(1)}, s32[16]{0:T(128)}, u32[]{:S(2)}) copy-start(s32[16]{0:T(128)} %index_ref.1) | copy-start | bytes 196
  46.3 8.1 %copy-start.11 = (bf16[4,384,256]{2,1,0:T(8,128)(2,1)S(1)}, bf16[4,384,256]{2,1,0:T(8,128)(2,1)}, u32[]{:S(2)}) copy-start(bf16[4,384,256]{2,1,0:T(8,128)(2,1)} %get-tuple-element.12) | copy-start | bytes 2359300
  48.2 27.4 %collective-permute-start.5 = (bf16[8,16,4096]{2,1,0:T(8,128)(2,1)S(1)}, bf16[8,16,4096]{2,1,0:T(8,128)(2,1)S(1)}, u32[]{:S(2)}, u32[]{:S(2)}) collective-permute-start(bf16[8,16,4096]{2,1,0:T(8,128)(2,1)S(1)} %get-tuple-element.17.top), channel_id=1, source_target_pairs={{1,0},{2,1},{3,2},{5,4},{6,5},{7,6},{9,8},{10,9},{11,10},{13,12},{... | collective-permute-start | bytes 3145736 | tf_op jit(solution)/shard_map/ppermute | solution.py:520
  49.5 27.0 %collective-permute-start.4 = (bf16[8,16,4096]{2,1,0:T(8,128)(2,1)S(1)}, bf16[8,16,4096]{2,1,0:T(8,128)(2,1)S(1)}, u32[]{:S(2)}, u32[]{:S(2)}) collective-permute-start(bf16[8,16,4096]{2,1,0:T(8,128)(2,1)S(1)} %get-tuple-element.18.bottom), channel_id=1, source_target_pairs={{0,1},{1,2},{2,3},{4,5},{5,6},{6,7},{8,9},{9,10},{10,11},{12,13},{... | collective-permute-start | bytes 3145736 | tf_op jit(solution)/shard_map/ppermute | solution.py:519
  85.3 48.0 %all-to-all-start.1 = ((bf16[64,8,1536]{2,1,0:T(8,128)(2,1)}), bf16[64,8,1536]{2,1,0:T(8,128)(2,1)S(1)}, u32[]{:S(2)}, u32[]{:S(2)}) async-start(bf16[64,8,1536]{2,1,0:T(8,128)(2,1)} %smooth.1), calls=%async_computation.1 | async-start | bytes 3145728 | tf_op jit(solution)/shard_map/all_to_all | solution.py:527
  137.4 1.1 copy-start
  138.5 1.7 copy-start.9
  140.1 2.5 %collective-permute-start.6 = (bf16[4,640,128]{2,1,0:T(8,128)(2,1)}, bf16[4,640,128]{2,1,0:T(8,128)(2,1)S(1)}, u32[]{:S(2)}, u32[]{:S(2)}) collective-permute-start(bf16[4,640,128]{2,1,0:T(8,128)(2,1)} %get-tuple-element.15), channel_id=1, source_target_pairs={{0,4},{4,0},{1,5},{5,1},{2,6},{6,2},{3,7},{7,3},{8,12},{12,8},{9,1... | collective-permute-start | bytes 1966088 | tf_op jit(solution)/shard_map/ppermute | solution.py:332
  144.1 8.3 %collective-permute-start.7 = (bf16[640,128]{1,0:T(8,128)(2,1)S(1)}, bf16[640,128]{1,0:T(8,128)(2,1)S(1)}, u32[]{:S(2)}, u32[]{:S(2)}) collective-permute-start(bf16[640,128]{1,0:T(8,128)(2,1)S(1)} %get-tuple-element.25), channel_id=1, source_target_pairs={{0,2},{1,3},{2,0},{3,1},{4,6},{5,7},{6,4},{7,5},{8,10},{9,11},{10,... | collective-permute-start | bytes 491528 | tf_op jit(solution)/shard_map/ppermute | solution.py:338
  148.2 8.1 %collective-permute-start.9 = (bf16[640,128]{1,0:T(8,128)(2,1)S(1)}, bf16[640,128]{1,0:T(8,128)(2,1)S(1)}, u32[]{:S(2)}, u32[]{:S(2)}) collective-permute-start(bf16[640,128]{1,0:T(8,128)(2,1)S(1)} %get-tuple-element.26), channel_id=1, source_target_pairs={{0,3},{1,0},{2,1},{3,2},{4,7},{5,4},{6,5},{7,6},{8,11},{9,8},{10,9... | collective-permute-start | bytes 491528 | tf_op jit(solution)/shard_map/ppermute | solution.py:338
  148.8 7.5 %collective-permute-start.8 = (bf16[640,128]{1,0:T(8,128)(2,1)S(1)}, bf16[640,128]{1,0:T(8,128)(2,1)S(1)}, u32[]{:S(2)}, u32[]{:S(2)}) collective-permute-start(bf16[640,128]{1,0:T(8,128)(2,1)S(1)} %get-tuple-element.27), channel_id=1, source_target_pairs={{0,1},{1,2},{2,3},{3,0},{4,5},{5,6},{6,7},{7,4},{8,9},{9,10},{10,1... | collective-permute-start | bytes 491528 | tf_op jit(solution)/shard_map/ppermute | solution.py:338
  189.5 23.9 %copy-start.12 = (s32[1024,16]{0,1:T(8,128)S(1)}, s32[1024,16]{0,1:T(8,128)}, u32[]{:S(2)}) copy-start(s32[1024,16]{0,1:T(8,128)} %param.7) | copy-start | bytes 196612
  209.6 8.3 %collective-permute-start.10 = (f32[4,640,128]{2,1,0:T(8,128)S(1)}, f32[4,640,128]{2,1,0:T(8,128)S(1)}, u32[]{:S(2)}, u32[]{:S(2)}) collective-permute-start(f32[4,640,128]{2,1,0:T(8,128)S(1)} %all_to_all.27.near_ref), channel_id=1, source_target_pairs={{0,4},{4,0},{1,5},{5,1},{2,6},{6,2},{3,7},{7,3},{8,12},{12,8},{9,1... | collective-permute-start | bytes 3932168 | tf_op jit(solution)/shard_map/ppermute | solution.py:344
  217.8 0.9 copy-start.1
  218.7 1.9 copy-start.10

commit v7 on v6

--- a/solution.py
+++ b/solution.py
@@ -271,8 +271,9 @@
 def cov_kernel(core_ref, part0, part1, keep_ref, send_ref, tiles_ref, data_ref, sems, tiles_sem):
     for copy in load_parts((part0, part1, part0), data_ref, sems):
         copy.wait()
+    rows = part0.shape[0] + part1.shape[0]
     tiles_copy = pltpu.make_async_copy(
-        data_ref.at[0 : tiles_ref.shape[0]], tiles_ref, tiles_sem
+        data_ref.at[0:rows], tiles_ref.at[0:rows], tiles_sem
     )
     tiles_copy.start()
     core = core_ref[0]
@@ -305,7 +306,7 @@
         out_shape=(
             jax.ShapeDtypeStruct((4, 640, 128), F32),
             jax.ShapeDtypeStruct((4, 640, 128), BF16),
-            jax.ShapeDtypeStruct((rows, parts[0].shape[1]), BF16),
+            jax.ShapeDtypeStruct((8 * rows, parts[0].shape[1]), BF16),
         ),
         in_specs=[smem(), anywhere(), anywhere()],
         out_specs=(vmem(), vmem(), pl.BlockSpec(memory_space=pltpu.HBM)),
@@ -314,7 +315,7 @@
             pltpu.SemaphoreType.DMA((3,)),
             pltpu.SemaphoreType.DMA,
         ],
-        compiler_params=pltpu.CompilerParams(vmem_limit_bytes=VMEM_LIMIT),
+        compiler_params=pltpu.CompilerParams(vmem_limit_bytes=48 * 1024 * 1024),
         cost_estimate=pl.CostEstimate(
             flops=2 * 10**9, bytes_accessed=6 * 10**6, transcendentals=0
         ),
@@ -330,13 +331,8 @@
 def reduce_all(keep, send):
     swap = [(0, 1), (1, 0)]
     half = (keep + lax.ppermute(send, "core", swap).astype(F32)).astype(BF16)
-    half = half.reshape(4, 640, 128)
-    sky = lax.axis_index("sky")
-    total = lax.dynamic_index_in_dim(half, sky, 0, False).astype(F32)
-    for d in (2, 1, 3):
-        block = lax.dynamic_index_in_dim(half, lax.rem(sky + d, 4), 0, False)
-        total += lax.ppermute(block, "sky", [(i, (i + d) % 4) for i in range(4)]).astype(F32)
-    quarter = total.astype(BF16)
+    got = lax.all_to_all(half.reshape(4, 640, 128), "sky", 0, 0, tiled=True)
+    quarter = jnp.sum(got.astype(F32), axis=0).astype(BF16)
     got = lax.all_to_all(quarter.reshape(32, 20, 128), ("y", "z"), 0, 0, tiled=True)
     mine = jnp.sum(got.astype(F32), axis=0)
     quarter = everywhere(mine, ("y", "z"), 32).reshape(640, 128)
@@ -379,10 +375,10 @@
     core_ref, near_ref, far_ref, seed_ref, tiles_ref, out_ref, data_ref, cov_ref, basis_ref, coef_ref, done_ref, sem, out_sems
 ):
     core = core_ref[0]
-    tiles_copy = pltpu.make_async_copy(tiles_ref, data_ref, sem)
-    tiles_copy.start()
     modes = seed_ref.shape[0] // 3
     count = seed_ref.shape[1]
+    tiles_copy = pltpu.make_async_copy(tiles_ref.at[0:count], data_ref, sem)
+    tiles_copy.start()
     pixels = data_ref.shape[1]
     scale = 1.0 / (256 * pixels)
     for i in range(8):

time: 234 us -> 236 us (level)
  blocking collectives: 52.9 us -> 63.4 us
  waiting for transfers between devices: 73.5 us -> 66.6 us
  starting transfers between devices: 49.8 us -> 45.3 us
  local copies, waits for them, and re-layouts: 19.1 us -> 22.6 us
    all_to_all x0 -> x1, blocking collectives: none -> 15.2 us  [reduce_all(): got = lax.all_to_all(half.reshape(4, 640, 128), 'sky', 0, 0, tiled=True)]
    ppermute x3 -> x0, waiting for transfers between devices: 6.68 us -> none  [reduce_all(): lax.ppermute(block, 'sky', [(i, (i + d) % 4) for i in range(4)]).astype(F32)]
    ppermute x3 -> x0, starting transfers between devices: 5.53 us -> none  [reduce_all(): lax.ppermute(block, 'sky', [(i, (i + d) % 4) for i in range(4)]).astype(F32)]
    all_to_all x2, blocking collectives: 37.3 us -> 32.6 us  [everywhere(): return lax.all_to_all(copies, axes, 0, 0, tiled=True)]
    unnamed x30 -> x26, local copies, waits for them, and re-layouts: 10.4 us -> 14 us
  transfers between devices with their start and end apart: 13 -> 10, of which waited for: 9 -> 7; matrix products, arithmetic and copies ran while one was open for 3% -> 3% of each run, Pallas kernels for 6% -> 6%
where the time goes in v7:
time: 236 us; the launch traced here: 235 us
  waiting for transfers between devices  66.6 us (28%)
  blocking collectives  63.4 us (27%)
  starting transfers between devices  45.3 us (19%)
  Pallas kernels  36.1 us (15%)
  local copies, waits for them, and re-layouts  22.6 us (10%)
    all_to_all x2, waiting for transfers between devices, body(): data = lax.all_to_all(pieces, ('y', 'z', 'core'), 0, 0, tiled=True)  41.1 us
    all_to_all x2, blocking collectives, everywhere(): return lax.all_to_all(copies, axes, 0, 0, tiled=True)  32.6 us
    all_to_all x2, starting transfers between devices, body(): data = lax.all_to_all(pieces, ('y', 'z', 'core'), 0, 0, tiled=True)  22.2 us
    ppermute x3, waiting for transfers between devices, body(): after = lax.ppermute(top, 'sky', [(i + 1, i) for i in range(3)])  22.1 us
    all_to_all x1, blocking collectives, reduce_all(): lax.all_to_all(quarter.reshape(32, 20, 128), ('y', 'z'), 0, 0, tiled=True)  15.6 us
    all_to_all x1, blocking collectives, reduce_all(): got = lax.all_to_all(half.reshape(4, 640, 128), 'sky', 0, 0, tiled=True)  15.2 us
    unnamed x26, local copies, waits for them, and re-layouts  14 us
    ppermute x3, starting transfers between devices, body(): before = lax.ppermute(bottom, 'sky', [(i, i + 1) for i in range(3)])  13.8 us
  transfers between devices with their start and end apart: 10, of which 7 were waited for; matrix products, arithmetic and copies ran while one was open for 3% of the time, Pallas kernels for 6%

profile of v7, /device:TPU:33, one launch (start us, length us, event | category | flops | bytes accessed | tf_op | source)
XLA Modules:
  0.0 234.7 jit_solution(15736563904535234390)
XLA Ops:
  0.0 1.3 fusion.1
  1.3 1.3 collective-permute-start.3
  2.6 4.0 %collective-permute-start.2 = (bf16[4,16,4096]{2,1,0:T(8,128)(2,1)S(1)}, bf16[4,16,4096]{2,1,0:T(8,128)(2,1)S(1)}, u32[]{:S(2)}, u32[]{:S(2)}) collective-permute-start(bf16[4,16,4096]{2,1,0:T(8,128)(2,1)S(1)} %get-tuple-element.20.bottom), channel_id=1, source_target_pairs={{0,1},{1,2},{2,3},{4,5},{5,6},{6,7},{8,9},{9,10},{10,11},{12,13},{... | collective-permute-start | bytes 1572872 | tf_op jit(solution)/shard_map/ppermute | solution.py:515
  6.6 1.3 fusion.2
  7.9 1.3 collective-permute-start.1
  9.2 4.8 %collective-permute-start = (bf16[4,16,4096]{2,1,0:T(8,128)(2,1)S(1)}, bf16[4,16,4096]{2,1,0:T(8,128)(2,1)}, u32[]{:S(2)}, u32[]{:S(2)}) collective-permute-start(bf16[4,16,4096]{2,1,0:T(8,128)(2,1)S(1)} %get-tuple-element.22.bottom), channel_id=1, source_target_pairs={{0,1},{1,2},{2,3},{4,5},{5,6},{6,7},{8,9},{9,10},{10,11},{12,13},{... | collective-permute-start | bytes 1572872 | tf_op jit(solution)/shard_map/ppermute | solution.py:515
  14.1 3.5 %prep.1 = (bf16[8,256,256]{2,1,0:T(8,128)(2,1)}, bf16[4,384,256]{2,1,0:T(8,128)(2,1)}, bf16[192,256]{1,0:T(8,128)(2,1)}) custom-call(s32[16]{0:T(128)} %index_ref.1, f32[8,31]{1,0:T(8,128)} %taps_ref.1), custom_call_target="tpu_custom_call" | custom-call | flops 1000000 | bytes 2000000 | tf_op jit(solution)/shard_map/prep/pallas_call | solution.py:77
  17.6 1.0 fusion.3
  20.3 1.2 copy-done.2
  23.6 2.7 %first.1.first_ref = bf16[32,128,128]{2,1,0:T(8,128)(2,1)S(1)} custom-call(s32[4]{0:T(128)S(1)} %get-tuple-element.25.index_ref, bf16[4,16,4096]{2,1,0:T(8,128)(2,1)S(1)} %copy-done.7, bf16[4,16,4096]{2,1,0:T(8,128)(2,1)S(1)} %get-tuple-element.19.top, bf16[4,16,4096]{2,1,0:T(8,128)(2,1)S(1)} %get-tuple-element.20.bottom, ...), custom_call_target="tpu_custom_call" | custom-call | flops 2000000000 | bytes 4000000 | tf_op jit(solution)/shard_map/first/pallas_call | solution.py:208
  26.3 1.1 collective-permute-done.1.after
  28.1 5.0 %second.1 = bf16[64,8,1536]{2,1,0:T(8,128)(2,1)} custom-call(s32[4]{0:T(128)S(1)} %get-tuple-element.26.index_ref, bf16[4,16,4096]{2,1,0:T(8,128)(2,1)} %collective-permute-done.before, bf16[4,16,4096]{2,1,0:T(8,128)(2,1)S(1)} %get-tuple-element.21.top, bf16[4,16,4096]{2,1,0:T(8,128)(2,1)S(1)} %get-tuple-element.22.bottom, ...), custom_call_target="tpu_custom_call" | custom-call | flops 2000000000 | bytes 4000000 | tf_op jit(solution)/shard_map/second/pallas_call | solution.py:223
  33.1 13.2 %all-to-all-start = ((bf16[64,8,1536]{2,1,0:T(8,128)(2,1)}), bf16[64,8,1536]{2,1,0:T(8,128)(2,1)S(1)}, u32[]{:S(2)}, u32[]{:S(2)}) async-start(bf16[64,8,1536]{2,1,0:T(8,128)(2,1)} %second.1), calls=%async_computation | async-start | bytes 3145728 | tf_op jit(solution)/shard_map/all_to_all | solution.py:523
  46.3 1.8 fusion
  48.2 1.3 collective-permute-start.5
  49.5 4.9 %collective-permute-start.4 = (bf16[8,16,4096]{2,1,0:T(8,128)(2,1)S(1)}, bf16[8,16,4096]{2,1,0:T(8,128)(2,1)S(1)}, u32[]{:S(2)}, u32[]{:S(2)}) collective-permute-start(bf16[8,16,4096]{2,1,0:T(8,128)(2,1)S(1)} %get-tuple-element.18.bottom), channel_id=1, source_target_pairs={{0,1},{1,2},{2,3},{4,5},{5,6},{6,7},{8,9},{9,10},{10,11},{12,13},{... | collective-permute-start | bytes 3145736 | tf_op jit(solution)/shard_map/ppermute | solution.py:515
  54.5 21.0 %collective-permute-done.5.after = bf16[8,16,4096]{2,1,0:T(8,128)(2,1)S(1)} collective-permute-done((bf16[8,16,4096]{2,1,0:T(8,128)(2,1)S(1)}, bf16[8,16,4096]{2,1,0:T(8,128)(2,1)S(1)}, u32[]{:S(2)}, u32[]{:S(2)}) %collective-permute-start.5) | collective-permute-done | bytes 1048608 | tf_op jit(solution)/shard_map/ppermute | solution.py:516
  76.4 6.7 %smooth.1 = bf16[64,8,1536]{2,1,0:T(8,128)(2,1)} custom-call(s32[8]{0:T(128)S(1)} %slice.53.index_ref, bf16[8,16,4096]{2,1,0:T(8,128)(2,1)S(1)} %collective-permute-done.4.before, bf16[8,16,4096]{2,1,0:T(8,128)(2,1)S(1)} %get-tuple-element.17.top, bf16[8,16,4096]{2,1,0:T(8,128)(2,1)S(1)} %get-tuple-element.18.bottom, ...), custom_call_target="tpu_custom_call" | custom-call | flops 4000000000 | bytes 8000000 | tf_op jit(solution)/shard_map/smooth/pallas_call | solution.py:239
  83.2 2.1 all-to-all-done
  85.3 9.1 %all-to-all-start.1 = ((bf16[64,8,1536]{2,1,0:T(8,128)(2,1)}), bf16[64,8,1536]{2,1,0:T(8,128)(2,1)S(1)}, u32[]{:S(2)}, u32[]{:S(2)}) async-start(bf16[64,8,1536]{2,1,0:T(8,128)(2,1)} %smooth.1), calls=%async_computation.1 | async-start | bytes 3145728 | tf_op jit(solution)/shard_map/all_to_all | solution.py:523
  94.4 39.0 %all-to-all-done.1 = bf16[64,8,1536]{2,1,0:T(8,128)(2,1)S(1)} async-done(((bf16[64,8,1536]{2,1,0:T(8,128)(2,1)}), bf16[64,8,1536]{2,1,0:T(8,128)(2,1)S(1)}, u32[]{:S(2)}, u32[]{:S(2)}) %all-to-all-start.1) | async-done | bytes 1572896 | tf_op jit(solution)/shard_map/all_to_all | solution.py:523
  133.4 4.5 %cov.1 = (f32[4,640,128]{2,1,0:T(8,128)S(1)}, bf16[4,640,128]{2,1,0:T(8,128)(2,1)S(1)}, bf16[8192,1536]{1,0:T(8,128)(2,1)}) custom-call(s32[1]{0:T(128)} %bitcast.core_ref, bf16[512,1536]{1,0:T(8,128)(2,1)S(1)} %bitcast.9, bf16[512,1536]{1,0:T(8,128)(2,1)S(1)} %bitcast.10), custom_call_target="tpu_custom_call" | custom-call | flops 2000000000 | bytes 6000000 | tf_op jit(solution)/shard_map/cov/pallas_call | solution.py:304
  138.5 1.7 collective-permute-done.6
  140.4 15.2 %all_to_all.30 = bf16[4,640,128]{2,1,0:T(8,128)(2,1)S(1)} all-to-all(bf16[4,640,128]{2,1,0:T(8,128)(2,1)S(1)} %add_convert_fusion), channel_id=1, replica_groups=mesh['y'=4,'z'=8,'core'=2,'sky'=4] {'sky'}, dimensions={0} | all-to-all | bytes 1310720 | tf_op jit(solution)/shard_map/all_to_all | solution.py:334
  155.7 15.6 %all_to_all.31 = bf16[32,20,128]{2,1,0:T(8,128)(2,1)S(1)} all-to-all(bf16[32,20,128]{2,1,0:T(8,128)(2,1)S(1)} %reshape.26), channel_id=1, replica_groups=mesh['y'=4,'z'=8,'core'=2,'sky'=4] {'y','z'}, dimensions={0} | all-to-all | bytes 327680 | tf_op jit(solution)/shard_map/all_to_all | solution.py:336
  171.4 16.0 %all_to_all.32 = f32[32,20,128]{2,1,0:T(8,128)S(1)} all-to-all(f32[32,20,128]{2,1,0:T(8,128)S(1)} %broadcast_in_dim.6), channel_id=1, replica_groups=mesh['y'=4,'z'=8,'core'=2,'sky'=4] {'y','z'}, dimensions={0} | all-to-all | bytes 655360 | tf_op jit(solution)/shard_map/all_to_all | solution.py:328
  187.6 16.6 %all_to_all.33.near_ref = f32[4,640,128]{2,1,0:T(8,128)S(1)} all-to-all(f32[4,640,128]{2,1,0:T(8,128)S(1)} %broadcast_in_dim.15), channel_id=1, replica_groups=mesh['y'=4,'z'=8,'core'=2,'sky'=4] {'sky'}, dimensions={0} | all-to-all | bytes 2621440 | tf_op jit(solution)/shard_map/all_to_all | solution.py:328
  204.1 4.8 %collective-permute-start.7 = (f32[4,640,128]{2,1,0:T(8,128)S(1)}, f32[4,640,128]{2,1,0:T(8,128)S(1)}, u32[]{:S(2)}, u32[]{:S(2)}) collective-permute-start(f32[4,640,128]{2,1,0:T(8,128)S(1)} %all_to_all.33.near_ref), channel_id=1, source_target_pairs={{0,4},{4,0},{1,5},{5,1},{2,6},{6,2},{3,7},{7,3},{8,12},{12,8},{9,1... | collective-permute-start | bytes 3932168 | tf_op jit(solution)/shard_map/ppermute | solution.py:340
  210.0 1.1 copy.7
  211.9 1.5 seeds.1.seed_ref
  213.4 8.2 %copy-done = bf16[8192,1536]{1,0:T(8,128)(2,1)S(1)} copy-done((bf16[8192,1536]{1,0:T(8,128)(2,1)S(1)}, bf16[8192,1536]{1,0:T(8,128)(2,1)}, u32[]{:S(2)}) %copy-start) | copy-done | bytes 25165848
  222.4 12.2 %clean.1 = bf16[64,16,1536]{2,1,0:T(8,128)(2,1)} custom-call(s32[1]{0:T(128)} %bitcast.core_ref, f32[4,640,128]{2,1,0:T(8,128)S(1)} %all_to_all.33.near_ref, f32[4,640,128]{2,1,0:T(8,128)S(1)} %collective-permute-done.7.far_ref, bf16[48,1024]{1,0:T(8,128)(2,1)S(1)} %copy-done.1, bf16[8192,1536]{1,0:T(8,128)(2,1)S(1)} %copy-done), custom_call_target="tpu_custom_call" | custom-call | flops 3000000000 | bytes 12000000 | tf_op jit(solution)/shard_map/clean/pallas_call | solution.py:482
  (42 shorter events, 9.4 us)
Async XLA Ops:
  1.3 12.8 %copy-start.11 = (s32[16]{0:T(128)S(1)}, s32[16]{0:T(128)}, u32[]{:S(2)}) copy-start(s32[16]{0:T(128)} %index_ref.1) | copy-start | bytes 196
  1.3 17.4 %collective-permute-start.3 = (bf16[4,16,4096]{2,1,0:T(8,128)(2,1)S(1)}, bf16[4,16,4096]{2,1,0:T(8,128)(2,1)S(1)}, u32[]{:S(2)}, u32[]{:S(2)}) collective-permute-start(bf16[4,16,4096]{2,1,0:T(8,128)(2,1)S(1)} %get-tuple-element.19.top), channel_id=1, source_target_pairs={{1,0},{2,1},{3,2},{5,4},{6,5},{7,6},{9,8},{10,9},{11,10},{13,12},{... | collective-permute-start | bytes 1572872 | tf_op jit(solution)/shard_map/ppermute | solution.py:516
  2.6 16.9 %collective-permute-start.2 = (bf16[4,16,4096]{2,1,0:T(8,128)(2,1)S(1)}, bf16[4,16,4096]{2,1,0:T(8,128)(2,1)S(1)}, u32[]{:S(2)}, u32[]{:S(2)}) collective-permute-start(bf16[4,16,4096]{2,1,0:T(8,128)(2,1)S(1)} %get-tuple-element.20.bottom), channel_id=1, source_target_pairs={{0,1},{1,2},{2,3},{4,5},{5,6},{6,7},{8,9},{9,10},{10,11},{12,13},{... | collective-permute-start | bytes 1572872 | tf_op jit(solution)/shard_map/ppermute | solution.py:515
  7.9 19.4 %collective-permute-start.1 = (bf16[4,16,4096]{2,1,0:T(8,128)(2,1)S(1)}, bf16[4,16,4096]{2,1,0:T(8,128)(2,1)}, u32[]{:S(2)}, u32[]{:S(2)}) collective-permute-start(bf16[4,16,4096]{2,1,0:T(8,128)(2,1)S(1)} %get-tuple-element.21.top), channel_id=1, source_target_pairs={{1,0},{2,1},{3,2},{5,4},{6,5},{7,6},{9,8},{10,9},{11,10},{13,12},{... | collective-permute-start | bytes 1572872 | tf_op jit(solution)/shard_map/ppermute | solution.py:516
  9.2 18.9 %collective-permute-start = (bf16[4,16,4096]{2,1,0:T(8,128)(2,1)S(1)}, bf16[4,16,4096]{2,1,0:T(8,128)(2,1)}, u32[]{:S(2)}, u32[]{:S(2)}) collective-permute-start(bf16[4,16,4096]{2,1,0:T(8,128)(2,1)S(1)} %get-tuple-element.22.bottom), channel_id=1, source_target_pairs={{0,1},{1,2},{2,3},{4,5},{5,6},{6,7},{8,9},{9,10},{10,11},{12,13},{... | collective-permute-start | bytes 1572872 | tf_op jit(solution)/shard_map/ppermute | solution.py:515
  18.6 0.8 copy-start.4
  19.5 0.8 copy-start.6
  20.3 1.2 copy-start.2
  21.5 1.0 copy-start.5
  22.5 1.0 copy-start.7
  23.6 4.6 %copy-start.3 = (bf16[8,256,256]{2,1,0:T(8,128)(2,1)S(1)}, bf16[8,256,256]{2,1,0:T(8,128)(2,1)}, u32[]{:S(2)}) copy-start(bf16[8,256,256]{2,1,0:T(8,128)(2,1)} %get-tuple-element.11.col_ref) | copy-start | bytes 3145732
  23.6 4.6 %copy-start.8 = (bf16[192,256]{1,0:T(8,128)(2,1)S(1)}, bf16[192,256]{1,0:T(8,128)(2,1)}, u32[]{:S(2)}) copy-start(bf16[192,256]{1,0:T(8,128)(2,1)} %get-tuple-element.13.order_ref) | copy-start | bytes 294916
  33.1 52.2 %all-to-all-start = ((bf16[64,8,1536]{2,1,0:T(8,128)(2,1)}), bf16[64,8,1536]{2,1,0:T(8,128)(2,1)S(1)}, u32[]{:S(2)}, u32[]{:S(2)}) async-start(bf16[64,8,1536]{2,1,0:T(8,128)(2,1)} %second.1), calls=%async_computation | async-start | bytes 3145728 | tf_op jit(solution)/shard_map/all_to_all | solution.py:523
  46.3 8.1 %copy-start.12 = (s32[16]{0:T(128)S(1)}, s32[16]{0:T(128)}, u32[]{:S(2)}) copy-start(s32[16]{0:T(128)} %index_ref.1) | copy-start | bytes 196
  46.3 8.1 %copy-start.9 = (bf16[4,384,256]{2,1,0:T(8,128)(2,1)S(1)}, bf16[4,384,256]{2,1,0:T(8,128)(2,1)}, u32[]{:S(2)}) copy-start(bf16[4,384,256]{2,1,0:T(8,128)(2,1)} %get-tuple-element.12) | copy-start | bytes 2359300
  48.2 27.4 %collective-permute-start.5 = (bf16[8,16,4096]{2,1,0:T(8,128)(2,1)S(1)}, bf16[8,16,4096]{2,1,0:T(8,128)(2,1)S(1)}, u32[]{:S(2)}, u32[]{:S(2)}) collective-permute-start(bf16[8,16,4096]{2,1,0:T(8,128)(2,1)S(1)} %get-tuple-element.17.top), channel_id=1, source_target_pairs={{1,0},{2,1},{3,2},{5,4},{6,5},{7,6},{9,8},{10,9},{11,10},{13,12},{... | collective-permute-start | bytes 3145736 | tf_op jit(solution)/shard_map/ppermute | solution.py:516
  49.5 27.0 %collective-permute-start.4 = (bf16[8,16,4096]{2,1,0:T(8,128)(2,1)S(1)}, bf16[8,16,4096]{2,1,0:T(8,128)(2,1)S(1)}, u32[]{:S(2)}, u32[]{:S(2)}) collective-permute-start(bf16[8,16,4096]{2,1,0:T(8,128)(2,1)S(1)} %get-tuple-element.18.bottom), channel_id=1, source_target_pairs={{0,1},{1,2},{2,3},{4,5},{5,6},{6,7},{8,9},{9,10},{10,11},{12,13},{... | collective-permute-start | bytes 3145736 | tf_op jit(solution)/shard_map/ppermute | solution.py:515
  85.3 48.1 %all-to-all-start.1 = ((bf16[64,8,1536]{2,1,0:T(8,128)(2,1)}), bf16[64,8,1536]{2,1,0:T(8,128)(2,1)S(1)}, u32[]{:S(2)}, u32[]{:S(2)}) async-start(bf16[64,8,1536]{2,1,0:T(8,128)(2,1)} %smooth.1), calls=%async_computation.1 | async-start | bytes 3145728 | tf_op jit(solution)/shard_map/all_to_all | solution.py:523
  137.9 2.3 collective-permute-start.6
  187.5 21.4 %copy-start.10 = (s32[1024,16]{0,1:T(8,128)S(1)}, s32[1024,16]{0,1:T(8,128)}, u32[]{:S(2)}) copy-start(s32[1024,16]{0,1:T(8,128)} %param.7) | copy-start | bytes 196612
  204.1 9.2 %collective-permute-start.7 = (f32[4,640,128]{2,1,0:T(8,128)S(1)}, f32[4,640,128]{2,1,0:T(8,128)S(1)}, u32[]{:S(2)}, u32[]{:S(2)}) collective-permute-start(f32[4,640,128]{2,1,0:T(8,128)S(1)} %all_to_all.33.near_ref), channel_id=1, source_target_pairs={{0,4},{4,0},{1,5},{5,1},{2,6},{6,2},{3,7},{7,3},{8,12},{12,8},{9,1... | collective-permute-start | bytes 3932168 | tf_op jit(solution)/shard_map/ppermute | solution.py:340
  213.4 8.2 %copy-start = (bf16[8192,1536]{1,0:T(8,128)(2,1)S(1)}, bf16[8192,1536]{1,0:T(8,128)(2,1)}, u32[]{:S(2)}) copy-start(bf16[8192,1536]{1,0:T(8,128)(2,1)} %get-tuple-element.16.tiles_ref) | copy-start | bytes 75497472
  221.5 0.9 copy-start.1

commit v8 on v6

--- a/solution.py
+++ b/solution.py
@@ -330,13 +330,8 @@
 def reduce_all(keep, send):
     swap = [(0, 1), (1, 0)]
     half = (keep + lax.ppermute(send, "core", swap).astype(F32)).astype(BF16)
-    half = half.reshape(4, 640, 128)
-    sky = lax.axis_index("sky")
-    total = lax.dynamic_index_in_dim(half, sky, 0, False).astype(F32)
-    for d in (2, 1, 3):
-        block = lax.dynamic_index_in_dim(half, lax.rem(sky + d, 4), 0, False)
-        total += lax.ppermute(block, "sky", [(i, (i + d) % 4) for i in range(4)]).astype(F32)
-    quarter = total.astype(BF16)
+    got = lax.all_to_all(half.reshape(4, 640, 128), "sky", 0, 0, tiled=True)
+    quarter = jnp.sum(got.astype(F32), axis=0).astype(BF16)
     got = lax.all_to_all(quarter.reshape(32, 20, 128), ("y", "z"), 0, 0, tiled=True)
     mine = jnp.sum(got.astype(F32), axis=0)
     quarter = everywhere(mine, ("y", "z"), 32).reshape(640, 128)

time: 234 us -> 230 us (0.983)
  blocking collectives: 52.9 us -> 63.4 us
  waiting for transfers between devices: 73.5 us -> 66.6 us
  starting transfers between devices: 49.8 us -> 45.2 us
    all_to_all x0 -> x1, blocking collectives: none -> 15.2 us  [reduce_all(): got = lax.all_to_all(half.reshape(4, 640, 128), 'sky', 0, 0, tiled=True)]
    ppermute x3 -> x0, waiting for transfers between devices: 6.68 us -> none  [reduce_all(): lax.ppermute(block, 'sky', [(i, (i + d) % 4) for i in range(4)]).astype(F32)]
    ppermute x3 -> x0, starting transfers between devices: 5.53 us -> none  [reduce_all(): lax.ppermute(block, 'sky', [(i, (i + d) % 4) for i in range(4)]).astype(F32)]
    all_to_all x2, blocking collectives: 37.3 us -> 32.6 us  [everywhere(): return lax.all_to_all(copies, axes, 0, 0, tiled=True)]
    unnamed x30 -> x28, local copies, waits for them, and re-layouts: 10.4 us -> 9.37 us
  transfers between devices with their start and end apart: 13 -> 10, of which waited for: 9 -> 7; matrix products, arithmetic and copies ran while one was open for 3% -> 3% of each run, Pallas kernels for 6% -> 6%
where the time goes in v8:
time: 230 us; the launch traced here: 229 us
  waiting for transfers between devices  66.6 us (29%)
  blocking collectives  63.4 us (28%)
  starting transfers between devices  45.2 us (20%)
  Pallas kernels  34.8 us (15%)
  local copies, waits for them, and re-layouts  18 us (8%)
    all_to_all x2, waiting for transfers between devices, body(): data = lax.all_to_all(pieces, ('y', 'z', 'core'), 0, 0, tiled=True)  41.1 us
    all_to_all x2, blocking collectives, everywhere(): return lax.all_to_all(copies, axes, 0, 0, tiled=True)  32.6 us
    all_to_all x2, starting transfers between devices, body(): data = lax.all_to_all(pieces, ('y', 'z', 'core'), 0, 0, tiled=True)  22.2 us
    ppermute x3, waiting for transfers between devices, body(): after = lax.ppermute(top, 'sky', [(i + 1, i) for i in range(3)])  22.1 us
    all_to_all x1, blocking collectives, reduce_all(): lax.all_to_all(quarter.reshape(32, 20, 128), ('y', 'z'), 0, 0, tiled=True)  15.6 us
    all_to_all x1, blocking collectives, reduce_all(): got = lax.all_to_all(half.reshape(4, 640, 128), 'sky', 0, 0, tiled=True)  15.2 us
    ppermute x3, starting transfers between devices, body(): before = lax.ppermute(bottom, 'sky', [(i, i + 1) for i in range(3)])  13.7 us
    pallas_call x1, Pallas kernels, clean(): pl.pallas_call(clean_kernel, out_shape=jax.ShapeDtypeStruct((count // 16,...  12.2 us
  transfers between devices with their start and end apart: 10, of which 7 were waited for; matrix products, arithmetic and copies ran while one was open for 3% of the time, Pallas kernels for 6%

profile of v8, /device:TPU:33, one launch (start us, length us, event | category | flops | bytes accessed | tf_op | source)
XLA Modules:
  0.0 228.8 jit_solution(3814601110146580221)
XLA Ops:
  0.0 1.3 fusion.1
  1.3 1.3 collective-permute-start.3
  2.6 4.0 %collective-permute-start.2 = (bf16[4,16,4096]{2,1,0:T(8,128)(2,1)S(1)}, bf16[4,16,4096]{2,1,0:T(8,128)(2,1)S(1)}, u32[]{:S(2)}, u32[]{:S(2)}) collective-permute-start(bf16[4,16,4096]{2,1,0:T(8,128)(2,1)S(1)} %get-tuple-element.20.bottom), channel_id=1, source_target_pairs={{0,1},{1,2},{2,3},{4,5},{5,6},{6,7},{8,9},{9,10},{10,11},{12,13},{... | collective-permute-start | bytes 1572872 | tf_op jit(solution)/shard_map/ppermute | solution.py:514
  6.6 1.3 fusion.2
  7.9 1.3 collective-permute-start.1
  9.2 4.8 %collective-permute-start = (bf16[4,16,4096]{2,1,0:T(8,128)(2,1)S(1)}, bf16[4,16,4096]{2,1,0:T(8,128)(2,1)}, u32[]{:S(2)}, u32[]{:S(2)}) collective-permute-start(bf16[4,16,4096]{2,1,0:T(8,128)(2,1)S(1)} %get-tuple-element.22.bottom), channel_id=1, source_target_pairs={{0,1},{1,2},{2,3},{4,5},{5,6},{6,7},{8,9},{9,10},{10,11},{12,13},{... | collective-permute-start | bytes 1572872 | tf_op jit(solution)/shard_map/ppermute | solution.py:514
  14.1 3.5 %prep.1 = (bf16[8,256,256]{2,1,0:T(8,128)(2,1)}, bf16[4,384,256]{2,1,0:T(8,128)(2,1)}, bf16[192,256]{1,0:T(8,128)(2,1)}) custom-call(s32[16]{0:T(128)} %index_ref.1, f32[8,31]{1,0:T(8,128)} %taps_ref.1), custom_call_target="tpu_custom_call" | custom-call | flops 1000000 | bytes 2000000 | tf_op jit(solution)/shard_map/prep/pallas_call | solution.py:77
  20.3 1.2 copy-done.1
  23.6 2.7 %first.1.first_ref = bf16[32,128,128]{2,1,0:T(8,128)(2,1)S(1)} custom-call(s32[4]{0:T(128)S(1)} %get-tuple-element.25.index_ref, bf16[4,16,4096]{2,1,0:T(8,128)(2,1)S(1)} %copy-done.6, bf16[4,16,4096]{2,1,0:T(8,128)(2,1)S(1)} %get-tuple-element.19.top, bf16[4,16,4096]{2,1,0:T(8,128)(2,1)S(1)} %get-tuple-element.20.bottom, ...), custom_call_target="tpu_custom_call" | custom-call | flops 2000000000 | bytes 4000000 | tf_op jit(solution)/shard_map/first/pallas_call | solution.py:208
  26.3 1.1 collective-permute-done.1.after
  28.2 5.0 %second.1 = bf16[64,8,1536]{2,1,0:T(8,128)(2,1)} custom-call(s32[4]{0:T(128)S(1)} %get-tuple-element.26.index_ref, bf16[4,16,4096]{2,1,0:T(8,128)(2,1)} %collective-permute-done.before, bf16[4,16,4096]{2,1,0:T(8,128)(2,1)S(1)} %get-tuple-element.21.top, bf16[4,16,4096]{2,1,0:T(8,128)(2,1)S(1)} %get-tuple-element.22.bottom, ...), custom_call_target="tpu_custom_call" | custom-call | flops 2000000000 | bytes 4000000 | tf_op jit(solution)/shard_map/second/pallas_call | solution.py:223
  33.2 13.2 %all-to-all-start = ((bf16[64,8,1536]{2,1,0:T(8,128)(2,1)}), bf16[64,8,1536]{2,1,0:T(8,128)(2,1)S(1)}, u32[]{:S(2)}, u32[]{:S(2)}) async-start(bf16[64,8,1536]{2,1,0:T(8,128)(2,1)} %second.1), calls=%async_computation | async-start | bytes 3145728 | tf_op jit(solution)/shard_map/all_to_all | solution.py:522
  46.4 1.8 fusion
  48.2 1.3 collective-permute-start.5
  49.5 4.9 %collective-permute-start.4 = (bf16[8,16,4096]{2,1,0:T(8,128)(2,1)S(1)}, bf16[8,16,4096]{2,1,0:T(8,128)(2,1)S(1)}, u32[]{:S(2)}, u32[]{:S(2)}) collective-permute-start(bf16[8,16,4096]{2,1,0:T(8,128)(2,1)S(1)} %get-tuple-element.18.bottom), channel_id=1, source_target_pairs={{0,1},{1,2},{2,3},{4,5},{5,6},{6,7},{8,9},{9,10},{10,11},{12,13},{... | collective-permute-start | bytes 3145736 | tf_op jit(solution)/shard_map/ppermute | solution.py:514
  54.5 21.0 %collective-permute-done.5.after = bf16[8,16,4096]{2,1,0:T(8,128)(2,1)S(1)} collective-permute-done((bf16[8,16,4096]{2,1,0:T(8,128)(2,1)S(1)}, bf16[8,16,4096]{2,1,0:T(8,128)(2,1)S(1)}, u32[]{:S(2)}, u32[]{:S(2)}) %collective-permute-start.5) | collective-permute-done | bytes 1048608 | tf_op jit(solution)/shard_map/ppermute | solution.py:515
  76.5 6.7 %smooth.1 = bf16[64,8,1536]{2,1,0:T(8,128)(2,1)} custom-call(s32[8]{0:T(128)S(1)} %slice.53.index_ref, bf16[8,16,4096]{2,1,0:T(8,128)(2,1)S(1)} %collective-permute-done.4.before, bf16[8,16,4096]{2,1,0:T(8,128)(2,1)S(1)} %get-tuple-element.17.top, bf16[8,16,4096]{2,1,0:T(8,128)(2,1)S(1)} %get-tuple-element.18.bottom, ...), custom_call_target="tpu_custom_call" | custom-call | flops 4000000000 | bytes 8000000 | tf_op jit(solution)/shard_map/smooth/pallas_call | solution.py:239
  83.2 2.1 all-to-all-done
  85.3 9.1 %all-to-all-start.1 = ((bf16[64,8,1536]{2,1,0:T(8,128)(2,1)}), bf16[64,8,1536]{2,1,0:T(8,128)(2,1)S(1)}, u32[]{:S(2)}, u32[]{:S(2)}) async-start(bf16[64,8,1536]{2,1,0:T(8,128)(2,1)} %smooth.1), calls=%async_computation.1 | async-start | bytes 3145728 | tf_op jit(solution)/shard_map/all_to_all | solution.py:522
  94.4 39.0 %all-to-all-done.1 = bf16[64,8,1536]{2,1,0:T(8,128)(2,1)S(1)} async-done(((bf16[64,8,1536]{2,1,0:T(8,128)(2,1)}), bf16[64,8,1536]{2,1,0:T(8,128)(2,1)S(1)}, u32[]{:S(2)}, u32[]{:S(2)}) %all-to-all-start.1) | async-done | bytes 1572896 | tf_op jit(solution)/shard_map/all_to_all | solution.py:522
  133.4 3.2 %cov.1 = (f32[4,640,128]{2,1,0:T(8,128)S(1)}, bf16[4,640,128]{2,1,0:T(8,128)(2,1)S(1)}, bf16[1024,1536]{1,0:T(8,128)(2,1)S(1)}) custom-call(s32[1]{0:T(128)} %bitcast.core_ref, bf16[512,1536]{1,0:T(8,128)(2,1)S(1)} %bitcast.9, bf16[512,1536]{1,0:T(8,128)(2,1)S(1)} %bitcast.10), custom_call_target="tpu_custom_call" | custom-call | flops 2000000000 | bytes 6000000 | tf_op jit(solution)/shard_map/cov/pallas_call | solution.py:303
  136.6 1.7 copy-done.8
  138.8 1.7 collective-permute-done.6
  140.7 15.2 %all_to_all.30 = bf16[4,640,128]{2,1,0:T(8,128)(2,1)S(1)} all-to-all(bf16[4,640,128]{2,1,0:T(8,128)(2,1)S(1)} %add_convert_fusion), channel_id=1, replica_groups=mesh['y'=4,'z'=8,'core'=2,'sky'=4] {'sky'}, dimensions={0} | all-to-all | bytes 1310720 | tf_op jit(solution)/shard_map/all_to_all | solution.py:333
  156.0 15.6 %all_to_all.31 = bf16[32,20,128]{2,1,0:T(8,128)(2,1)S(1)} all-to-all(bf16[32,20,128]{2,1,0:T(8,128)(2,1)S(1)} %reshape.26), channel_id=1, replica_groups=mesh['y'=4,'z'=8,'core'=2,'sky'=4] {'y','z'}, dimensions={0} | all-to-all | bytes 327680 | tf_op jit(solution)/shard_map/all_to_all | solution.py:335
  171.7 16.0 %all_to_all.32 = f32[32,20,128]{2,1,0:T(8,128)S(1)} all-to-all(f32[32,20,128]{2,1,0:T(8,128)S(1)} %broadcast_in_dim.6), channel_id=1, replica_groups=mesh['y'=4,'z'=8,'core'=2,'sky'=4] {'y','z'}, dimensions={0} | all-to-all | bytes 655360 | tf_op jit(solution)/shard_map/all_to_all | solution.py:327
  187.9 16.6 %all_to_all.33.near_ref = f32[4,640,128]{2,1,0:T(8,128)S(1)} all-to-all(f32[4,640,128]{2,1,0:T(8,128)S(1)} %broadcast_in_dim.15), channel_id=1, replica_groups=mesh['y'=4,'z'=8,'core'=2,'sky'=4] {'sky'}, dimensions={0} | all-to-all | bytes 2621440 | tf_op jit(solution)/shard_map/all_to_all | solution.py:327
  204.5 4.8 %collective-permute-start.7 = (f32[4,640,128]{2,1,0:T(8,128)S(1)}, f32[4,640,128]{2,1,0:T(8,128)S(1)}, u32[]{:S(2)}, u32[]{:S(2)}) collective-permute-start(f32[4,640,128]{2,1,0:T(8,128)S(1)} %all_to_all.33.near_ref), channel_id=1, source_target_pairs={{0,4},{4,0},{1,5},{5,1},{2,6},{6,2},{3,7},{7,3},{8,12},{12,8},{9,1... | collective-permute-start | bytes 3932168 | tf_op jit(solution)/shard_map/ppermute | solution.py:339
  210.3 1.1 copy.7
  212.2 1.5 seeds.1.seed_ref
  214.6 1.9 copy-done.9
  216.5 12.2 %clean.1 = bf16[64,16,1536]{2,1,0:T(8,128)(2,1)} custom-call(s32[1]{0:T(128)} %bitcast.core_ref, f32[4,640,128]{2,1,0:T(8,128)S(1)} %all_to_all.33.near_ref, f32[4,640,128]{2,1,0:T(8,128)S(1)} %collective-permute-done.7.far_ref, bf16[48,1024]{1,0:T(8,128)(2,1)S(1)} %copy-done, bf16[1024,1536]{1,0:T(8,128)(2,1)S(1)} %copy-done.9), custom_call_target="tpu_custom_call" | custom-call | flops 3000000000 | bytes 12000000 | tf_op jit(solution)/shard_map/clean/pallas_call | solution.py:481
  (44 shorter events, 10.4 us)
Async XLA Ops:
  1.3 12.7 %copy-start.12 = (s32[16]{0:T(128)S(1)}, s32[16]{0:T(128)}, u32[]{:S(2)}) copy-start(s32[16]{0:T(128)} %index_ref.1) | copy-start | bytes 196
  1.3 17.3 %collective-permute-start.3 = (bf16[4,16,4096]{2,1,0:T(8,128)(2,1)S(1)}, bf16[4,16,4096]{2,1,0:T(8,128)(2,1)S(1)}, u32[]{:S(2)}, u32[]{:S(2)}) collective-permute-start(bf16[4,16,4096]{2,1,0:T(8,128)(2,1)S(1)} %get-tuple-element.19.top), channel_id=1, source_target_pairs={{1,0},{2,1},{3,2},{5,4},{6,5},{7,6},{9,8},{10,9},{11,10},{13,12},{... | collective-permute-start | bytes 1572872 | tf_op jit(solution)/shard_map/ppermute | solution.py:515
  2.6 16.8 %collective-permute-start.2 = (bf16[4,16,4096]{2,1,0:T(8,128)(2,1)S(1)}, bf16[4,16,4096]{2,1,0:T(8,128)(2,1)S(1)}, u32[]{:S(2)}, u32[]{:S(2)}) collective-permute-start(bf16[4,16,4096]{2,1,0:T(8,128)(2,1)S(1)} %get-tuple-element.20.bottom), channel_id=1, source_target_pairs={{0,1},{1,2},{2,3},{4,5},{5,6},{6,7},{8,9},{9,10},{10,11},{12,13},{... | collective-permute-start | bytes 1572872 | tf_op jit(solution)/shard_map/ppermute | solution.py:514
  7.9 19.4 %collective-permute-start.1 = (bf16[4,16,4096]{2,1,0:T(8,128)(2,1)S(1)}, bf16[4,16,4096]{2,1,0:T(8,128)(2,1)}, u32[]{:S(2)}, u32[]{:S(2)}) collective-permute-start(bf16[4,16,4096]{2,1,0:T(8,128)(2,1)S(1)} %get-tuple-element.21.top), channel_id=1, source_target_pairs={{1,0},{2,1},{3,2},{5,4},{6,5},{7,6},{9,8},{10,9},{11,10},{13,12},{... | collective-permute-start | bytes 1572872 | tf_op jit(solution)/shard_map/ppermute | solution.py:515
  9.2 18.9 %collective-permute-start = (bf16[4,16,4096]{2,1,0:T(8,128)(2,1)S(1)}, bf16[4,16,4096]{2,1,0:T(8,128)(2,1)}, u32[]{:S(2)}, u32[]{:S(2)}) collective-permute-start(bf16[4,16,4096]{2,1,0:T(8,128)(2,1)S(1)} %get-tuple-element.22.bottom), channel_id=1, source_target_pairs={{0,1},{1,2},{2,3},{4,5},{5,6},{6,7},{8,9},{9,10},{10,11},{12,13},{... | collective-permute-start | bytes 1572872 | tf_op jit(solution)/shard_map/ppermute | solution.py:514
  18.7 0.8 copy-start.3
  19.5 0.8 copy-start.5
  20.3 1.2 copy-start.1
  21.5 1.0 copy-start.4
  22.5 1.0 copy-start.6
  23.6 4.6 %copy-start.2 = (bf16[8,256,256]{2,1,0:T(8,128)(2,1)S(1)}, bf16[8,256,256]{2,1,0:T(8,128)(2,1)}, u32[]{:S(2)}) copy-start(bf16[8,256,256]{2,1,0:T(8,128)(2,1)} %get-tuple-element.11.col_ref) | copy-start | bytes 3145732
  23.6 4.6 %copy-start.7 = (bf16[192,256]{1,0:T(8,128)(2,1)S(1)}, bf16[192,256]{1,0:T(8,128)(2,1)}, u32[]{:S(2)}) copy-start(bf16[192,256]{1,0:T(8,128)(2,1)} %get-tuple-element.13.order_ref) | copy-start | bytes 294916
  33.2 52.2 %all-to-all-start = ((bf16[64,8,1536]{2,1,0:T(8,128)(2,1)}), bf16[64,8,1536]{2,1,0:T(8,128)(2,1)S(1)}, u32[]{:S(2)}, u32[]{:S(2)}) async-start(bf16[64,8,1536]{2,1,0:T(8,128)(2,1)} %second.1), calls=%async_computation | async-start | bytes 3145728 | tf_op jit(solution)/shard_map/all_to_all | solution.py:522
  46.4 8.1 %copy-start.13 = (s32[16]{0:T(128)S(1)}, s32[16]{0:T(128)}, u32[]{:S(2)}) copy-start(s32[16]{0:T(128)} %index_ref.1) | copy-start | bytes 196
  46.4 8.1 %copy-start.10 = (bf16[4,384,256]{2,1,0:T(8,128)(2,1)S(1)}, bf16[4,384,256]{2,1,0:T(8,128)(2,1)}, u32[]{:S(2)}) copy-start(bf16[4,384,256]{2,1,0:T(8,128)(2,1)} %get-tuple-element.12) | copy-start | bytes 2359300
  48.2 27.4 %collective-permute-start.5 = (bf16[8,16,4096]{2,1,0:T(8,128)(2,1)S(1)}, bf16[8,16,4096]{2,1,0:T(8,128)(2,1)S(1)}, u32[]{:S(2)}, u32[]{:S(2)}) collective-permute-start(bf16[8,16,4096]{2,1,0:T(8,128)(2,1)S(1)} %get-tuple-element.17.top), channel_id=1, source_target_pairs={{1,0},{2,1},{3,2},{5,4},{6,5},{7,6},{9,8},{10,9},{11,10},{13,12},{... | collective-permute-start | bytes 3145736 | tf_op jit(solution)/shard_map/ppermute | solution.py:515
  49.5 27.0 %collective-permute-start.4 = (bf16[8,16,4096]{2,1,0:T(8,128)(2,1)S(1)}, bf16[8,16,4096]{2,1,0:T(8,128)(2,1)S(1)}, u32[]{:S(2)}, u32[]{:S(2)}) collective-permute-start(bf16[8,16,4096]{2,1,0:T(8,128)(2,1)S(1)} %get-tuple-element.18.bottom), channel_id=1, source_target_pairs={{0,1},{1,2},{2,3},{4,5},{5,6},{6,7},{8,9},{9,10},{10,11},{12,13},{... | collective-permute-start | bytes 3145736 | tf_op jit(solution)/shard_map/ppermute | solution.py:514
  85.3 48.1 %all-to-all-start.1 = ((bf16[64,8,1536]{2,1,0:T(8,128)(2,1)}), bf16[64,8,1536]{2,1,0:T(8,128)(2,1)S(1)}, u32[]{:S(2)}, u32[]{:S(2)}) async-start(bf16[64,8,1536]{2,1,0:T(8,128)(2,1)} %smooth.1), calls=%async_computation.1 | async-start | bytes 3145728 | tf_op jit(solution)/shard_map/all_to_all | solution.py:522
  136.6 1.7 copy-start.8
  138.3 2.3 collective-permute-start.6
  187.9 21.4 %copy-start.11 = (s32[1024,16]{0,1:T(8,128)S(1)}, s32[1024,16]{0,1:T(8,128)}, u32[]{:S(2)}) copy-start(s32[1024,16]{0,1:T(8,128)} %param.7) | copy-start | bytes 196612
  204.5 9.2 %collective-permute-start.7 = (f32[4,640,128]{2,1,0:T(8,128)S(1)}, f32[4,640,128]{2,1,0:T(8,128)S(1)}, u32[]{:S(2)}, u32[]{:S(2)}) collective-permute-start(f32[4,640,128]{2,1,0:T(8,128)S(1)} %all_to_all.33.near_ref), channel_id=1, source_target_pairs={{0,4},{4,0},{1,5},{5,1},{2,6},{6,2},{3,7},{7,3},{8,12},{12,8},{9,1... | collective-permute-start | bytes 3932168 | tf_op jit(solution)/shard_map/ppermute | solution.py:339
  213.7 0.9 copy-start
  214.6 1.9 copy-start.9
